TPU v7x, 128 devices: a whole 4x4x4 slice. The times are simulated.
128 devices in a mesh: gx: 16 (over z, y), gy: 8 (over x, core).
Axes of the slice: x: 4, y: 4, z: 4, core: 2. Of those that a mesh axis runs over, the one named last changes fastest.
Arguments:
- tracers: float32 [8, 16, 4, 36, 64, 128], P('gy', 'gx'), may hold values from -6 to 6
- velocity: float32 [8, 16, 2, 36, 64, 128], P('gy', 'gx'), may hold values from -0.8 to 0.8
- mixing_rate: float32 [8, 16, 35, 64, 128], P('gy', 'gx'), may hold values from 0.05 to 5
- column_depth: float32 [8, 16, 64, 128], P('gy', 'gx'), may hold values from 0.25 to 2.5
- ocean_mask: int32 [8, 28], replicated, may hold values from 0 to 1, as said below
- clinic_list: int32 [8, 16], replicated, may hold values from 0 to 27, as said below
- tropic_list: int32 [8, 32], replicated, may hold values from -1 to 27, as said below
Outputs:
- new_tracers: float32 [8, 16, 4, 36, 64, 128], P('gy', 'gx')
- surface_height: float32 [8, 32, 64, 128], P('gy', 'gx')
Inputs may be any that keep to these rules, and one draw needn't show every extreme that they name: `ocean_mask`: every block row holds exactly 16 ocean blocks. `clinic_list`: row r lists every ocean block column of block row r exactly once. `tropic_list`: row r lists every ocean block column of block row r exactly once and holds -1 elsewhere; the 2 entries of one device are either all -1 or all blocks.
All inputs are finite; a program needn't handle non-finite values.
Results may differ from a plain program's by a relative error of at most 0.0003.
Values sent between devices are 32-bit elements; how exact they have to be, the bound alone decides.
No kernel may reach another device: no remote copies, remote signals or barrier semaphores. Data moves between devices by JAX's collectives and lax.ppermute only.
A program may use at most 128 MiB of HBM per device.

v0:
```python
import jax
import jax.numpy as jnp
from jax import lax
from jax.sharding import PartitionSpec as P

ITERS = 3


diffusion = 0.12
area_term = 0.1
thermal = 0.2
haline = 0.25
cabbeling = 0.05
forcing = 4.0


def passed_along(value, axis, steps):
    count = lax.axis_size(axis)
    leading, last = (max(0, -steps), min(count, count - steps))
    return lax.ppermute(value, axis, [(source, source + steps) for source in range(leading, last)])


def inverse_map(column_list, row_width):
    row_count, slot_count = column_list.shape
    target = jnp.where(column_list < 0, row_width, column_list)
    row_ids = jnp.broadcast_to(
        jnp.arange(row_count, dtype=jnp.int32)[:, None], (row_count, slot_count)
    )
    slot_ids = jnp.broadcast_to(
        jnp.arange(slot_count, dtype=jnp.int32)[None, :], (row_count, slot_count)
    )
    lookup = jnp.zeros((row_count, row_width + 1), jnp.int32).at[row_ids, target].set(slot_ids)
    return lookup[:, :row_width]


def links(columns, row_ids, ocean_mask, inverse):
    row_count, row_width = ocean_mask.shape
    in_use = (columns >= 0).astype(jnp.float32)
    column = jnp.maximum(columns, 0)
    east_col = (column + 1) % row_width
    west_col = (column + row_width - 1) % row_width
    north_row = jnp.minimum(row_ids + 1, row_count - 1)
    south_row = jnp.maximum(row_ids - 1, 0)
    has_north = (row_ids + 1 < row_count).astype(jnp.float32)
    has_south = (row_ids > 0).astype(jnp.float32)
    mask_float = ocean_mask.astype(jnp.float32)
    face_open = (
        in_use * mask_float[row_ids, east_col],
        in_use * mask_float[row_ids, west_col],
        in_use * has_north * mask_float[north_row, column],
        in_use * has_south * mask_float[south_row, column],
    )
    slot_ids = (
        inverse[row_ids, east_col],
        inverse[row_ids, west_col],
        inverse[north_row, column],
        inverse[south_row, column],
    )
    return (face_open, slot_ids)


def divergence(values, speeds, low_side, high_side, low_speed, open_low, open_high, along_axis):
    length = values.shape[along_axis]
    extended = jnp.concatenate(
        [jnp.expand_dims(low_side, along_axis), values, jnp.expand_dims(high_side, along_axis)],
        axis=along_axis,
    )
    face_speed = jnp.concatenate([jnp.expand_dims(low_speed, along_axis), speeds], axis=along_axis)
    behind = lax.slice_in_dim(extended, 0, length + 1, axis=along_axis)
    forward = lax.slice_in_dim(extended, 1, length + 2, axis=along_axis)
    fluxes = face_speed * (0.5 * (behind + forward)) - diffusion * (forward - behind)
    fluxes = jnp.concatenate(
        [
            lax.slice_in_dim(fluxes, 0, 1, axis=along_axis) * open_low,
            lax.slice_in_dim(fluxes, 1, length, axis=along_axis),
            lax.slice_in_dim(fluxes, length, length + 1, axis=along_axis) * open_high,
        ],
        axis=along_axis,
    )
    return lax.slice_in_dim(fluxes, 1, length + 1, axis=along_axis) - lax.slice_in_dim(
        fluxes, 0, length, axis=along_axis
    )


def vertical_mix(stirred, mixing_rate):
    levels = stirred.shape[3]
    coupling = mixing_rate[:, :, None]
    nothing = jnp.zeros_like(coupling[:, :, :, 0])
    interfaces = [coupling[:, :, :, level_index] for level_index in range(levels - 1)]
    above = [nothing] + interfaces
    beneath = interfaces + [nothing]
    factors = []
    partial_sol = []
    for level_index in range(levels):
        diagonal = 1.0 + above[level_index] + beneath[level_index]
        source = stirred[:, :, :, level_index]
        if level_index > 0:
            diagonal = diagonal - above[level_index] * factors[level_index - 1]
            source = source + above[level_index] * partial_sol[level_index - 1]
        factors.append(beneath[level_index] / diagonal)
        partial_sol.append(source / diagonal)
    result_levels = [partial_sol[levels - 1]]
    for level_index in range(levels - 2, -1, -1):
        result_levels.insert(0, partial_sol[level_index] + factors[level_index] * result_levels[0])
    return jnp.stack(result_levels, axis=3)


def tracer_core(tracers, velocity, mixing_rate, halo_values, face_open):
    west_tracer, west_speed, east_tracer, south_tracer, south_speed, north_tracer = halo_values
    open_east, open_west, open_north, open_south = [
        opening[:, :, None, None, None, None] for opening in face_open
    ]
    east_speed = velocity[:, :, 0:1]
    north_speed = velocity[:, :, 1:2]
    stirred = (
        tracers
        - divergence(
            tracers,
            east_speed,
            west_tracer,
            east_tracer,
            west_speed[:, :, None],
            open_west,
            open_east,
            5,
        )
        - divergence(
            tracers,
            north_speed,
            south_tracer,
            north_tracer,
            south_speed[:, :, None],
            open_south,
            open_north,
            4,
        )
    )
    mixed = vertical_mix(stirred, mixing_rate)
    levels = mixed.shape[3]
    spacing = 2.0 * (jnp.arange(levels, dtype=jnp.float32) + 1.0) / (levels * (levels + 1))
    heat = mixed[:, :, 0]
    salinity = mixed[:, :, 1]
    density = haline * salinity - thermal * heat - cabbeling * heat * heat
    column_forcing = forcing * jnp.sum(density * spacing[None, None, :, None, None], axis=2)
    return (mixed, column_forcing)


def face_weights(column_depth, depth_halos, face_open):
    west_depth, east_depth, south_depth, north_depth = depth_halos
    open_east, open_west, open_north, open_south = [
        opening[:, :, None, None] for opening in face_open
    ]
    cells_east = column_depth.shape[3]
    cells_north = column_depth.shape[2]
    edge_east = (jnp.arange(cells_east) == cells_east - 1)[None, None, None, :]
    edge_west = (jnp.arange(cells_east) == 0)[None, None, None, :]
    edge_north = (jnp.arange(cells_north) == cells_north - 1)[None, None, :, None]
    edge_south = (jnp.arange(cells_north) == 0)[None, None, :, None]
    to_east = jnp.concatenate([column_depth[..., 1:], east_depth[..., None]], axis=3)
    to_west = jnp.concatenate([west_depth[..., None], column_depth[..., :-1]], axis=3)
    to_north = jnp.concatenate([column_depth[:, :, 1:], north_depth[:, :, None]], axis=2)
    to_south = jnp.concatenate([south_depth[:, :, None], column_depth[:, :, :-1]], axis=2)
    weight_east = 0.5 * (column_depth + to_east) * jnp.where(edge_east, open_east, 1.0)
    weight_west = 0.5 * (column_depth + to_west) * jnp.where(edge_west, open_west, 1.0)
    weight_north = 0.5 * (column_depth + to_north) * jnp.where(edge_north, open_north, 1.0)
    weight_south = 0.5 * (column_depth + to_south) * jnp.where(edge_south, open_south, 1.0)
    return jnp.stack([weight_east, weight_west, weight_north, weight_south], axis=2)


def apply_operator(values, weights, halo_values):
    east_side, west_side, north_side, south_side = halo_values
    weight_east = weights[:, :, 0]
    weight_west = weights[:, :, 1]
    weight_north = weights[:, :, 2]
    weight_south = weights[:, :, 3]
    to_east = jnp.concatenate([values[..., 1:], east_side[..., None]], axis=3)
    to_west = jnp.concatenate([west_side[..., None], values[..., :-1]], axis=3)
    to_north = jnp.concatenate([values[:, :, 1:], north_side[:, :, None]], axis=2)
    to_south = jnp.concatenate([south_side[:, :, None], values[:, :, :-1]], axis=2)
    return (
        (area_term + weight_east + weight_west + weight_north + weight_south) * values
        - weight_east * to_east
        - weight_west * to_west
        - weight_north * to_north
        - weight_south * to_south
    )


def picked(band_rows, slot_ids):
    return jnp.take(band_rows[0], slot_ids[0], axis=0)[None]


def exchange_edges(values, slot_ids):
    slot_east, slot_west, slot_north, slot_south = slot_ids
    cells_north = values.shape[2]
    side_cols = jnp.concatenate([values[..., -1], values[..., 0]], axis=2)
    from_below = passed_along(values[:, :, -1, :], "gy", 1)
    from_above = passed_along(values[:, :, 0, :], "gy", -1)
    band_sides, band_below, band_above = (
        lax.all_gather(side_cols, "gx", axis=1, tiled=True),
        lax.all_gather(from_below, "gx", axis=1, tiled=True),
        lax.all_gather(from_above, "gx", axis=1, tiled=True),
    )
    return (
        picked(band_sides, slot_east)[..., cells_north:],
        picked(band_sides, slot_west)[..., :cells_north],
        picked(band_above, slot_north),
        picked(band_below, slot_south),
    )


def squares(residual):
    return lax.psum(jnp.sum(residual * residual), ("gx", "gy"))


def solve(forcing_field, weights, slot_ids):
    solution = jnp.zeros_like(forcing_field)
    residual = forcing_field
    direction = forcing_field
    norm_now = squares(residual)
    for iteration in range(ITERS):
        image_field = apply_operator(direction, weights, exchange_edges(direction, slot_ids))
        step_size = norm_now / lax.psum(jnp.sum(direction * image_field), ("gx", "gy"))
        solution = solution + step_size * direction
        if iteration + 1 < ITERS:
            residual = residual - step_size * image_field
            norm_next = squares(residual)
            direction = residual + norm_next / norm_now * direction
            norm_now = norm_next
    return solution


def body(tracers, velocity, mixing_rate, column_depth, ocean_mask, clinic_list, tropic_list):
    band_row = lax.axis_index("gy")
    band_col = lax.axis_index("gx")
    slot_count = tracers.shape[1]
    tracer_count = tracers.shape[2]
    levels = tracers.shape[3]
    cells_north = tracers.shape[4]
    cells_east = tracers.shape[5]
    row_width = ocean_mask.shape[1]
    inverse = inverse_map(clinic_list, row_width)
    clinic_row = lax.dynamic_index_in_dim(clinic_list, band_row, 0, keepdims=False)
    own_columns = lax.dynamic_slice_in_dim(clinic_row, band_col * slot_count, slot_count)[None]
    row_ids = jnp.full((1, slot_count), band_row, jnp.int32)
    face_open, slot_ids = links(own_columns, row_ids, ocean_mask, inverse)
    slot_east, slot_west, slot_north, slot_south = slot_ids
    east_cols = jnp.concatenate(
        [
            tracers[..., -1].reshape(1, slot_count, -1),
            velocity[:, :, 0, :, :, -1].reshape(1, slot_count, -1),
            column_depth[..., -1],
        ],
        axis=2,
    )
    west_cols = jnp.concatenate(
        [tracers[..., 0].reshape(1, slot_count, -1), column_depth[..., 0]], axis=2
    )
    side_cols = jnp.concatenate([east_cols, west_cols], axis=2)
    north_rows = jnp.concatenate(
        [
            tracers[..., -1, :].reshape(1, slot_count, -1),
            velocity[:, :, 1, :, -1, :].reshape(1, slot_count, -1),
            column_depth[..., -1, :],
        ],
        axis=2,
    )
    south_rows = jnp.concatenate(
        [tracers[..., 0, :].reshape(1, slot_count, -1), column_depth[..., 0, :]], axis=2
    )
    band_sides, band_north, band_south = (
        lax.all_gather(side_cols, "gx", axis=1, tiled=True),
        lax.all_gather(north_rows, "gx", axis=1, tiled=True),
        lax.all_gather(south_rows, "gx", axis=1, tiled=True),
    )
    band_below = passed_along(band_north, "gy", 1)
    band_above = passed_along(band_south, "gy", -1)
    tracer_len = tracer_count * levels
    east_len = (tracer_len + levels + 1) * cells_north
    from_west = picked(band_sides, slot_west)[..., :east_len]
    from_east = picked(band_sides, slot_east)[..., east_len:]
    from_south = picked(band_below, slot_south)
    from_north = picked(band_above, slot_north)
    halo_values = (
        from_west[..., : tracer_len * cells_north].reshape(
            1, slot_count, tracer_count, levels, cells_north
        ),
        from_west[..., tracer_len * cells_north : (tracer_len + levels) * cells_north].reshape(
            1, slot_count, levels, cells_north
        ),
        from_east[..., : tracer_len * cells_north].reshape(
            1, slot_count, tracer_count, levels, cells_north
        ),
        from_south[..., : tracer_len * cells_east].reshape(
            1, slot_count, tracer_count, levels, cells_east
        ),
        from_south[..., tracer_len * cells_east : (tracer_len + levels) * cells_east].reshape(
            1, slot_count, levels, cells_east
        ),
        from_north[..., : tracer_len * cells_east].reshape(
            1, slot_count, tracer_count, levels, cells_east
        ),
    )
    depth_halos = (
        from_west[..., (tracer_len + levels) * cells_north :],
        from_east[..., tracer_len * cells_north :],
        from_south[..., (tracer_len + levels) * cells_east :],
        from_north[..., tracer_len * cells_east :],
    )
    new_tracers, column_forcing = tracer_core(
        tracers, velocity, mixing_rate, halo_values, face_open
    )
    weights = face_weights(column_depth, depth_halos, face_open)
    tropic_row = lax.dynamic_index_in_dim(tropic_list, band_row, 0, keepdims=False)
    tropic_count = tropic_list.shape[1] // lax.axis_size("gx")
    own_tropic = lax.dynamic_slice_in_dim(tropic_row, band_col * tropic_count, tropic_count)[None]
    in_use = (own_tropic >= 0)[:, :, None, None]
    inverse_row = lax.dynamic_index_in_dim(inverse, band_row, 0, keepdims=False)
    source_slot = jnp.take(inverse_row, jnp.maximum(own_tropic, 0), axis=0)
    packed = jnp.concatenate([column_forcing[:, :, None], weights], axis=2)
    band_fields = lax.all_gather(packed, "gx", axis=1, tiled=True)
    moved = jnp.where(in_use[..., None], picked(band_fields, source_slot), 0.0)
    tropic_inverse = inverse_map(tropic_list, row_width)
    tropic_ids = jnp.full((1, tropic_count), band_row, jnp.int32)
    tropic_slots = links(own_tropic, tropic_ids, ocean_mask, tropic_inverse)[1]
    surface_height = solve(moved[:, :, 0], moved[:, :, 1:], tropic_slots)
    return (new_tracers, surface_height)


def solution(mesh):
    return jax.shard_map(
        body,
        mesh=mesh,
        in_specs=(
            P("gy", "gx", None, None, None, None),
            P("gy", "gx", None, None, None, None),
            P("gy", "gx", None, None, None),
            P("gy", "gx", None, None),
            P(),
            P(),
            P(),
        ),
        out_specs=(P("gy", "gx", None, None, None, None), P("gy", "gx", None, None)),
        check_vma=False,
    )
```

profile of v0, /device:TPU:0, one launch (start us, length us, event | category | flops | bytes accessed | tf_op | source)
XLA Modules:
  0.0 795.8 jit_solution(15573469216887903358)
XLA Ops:
  10.1 7.6 slice_reduce_fusion
  20.7 5.4 constant_dynamic-update-slice_fusion.1
  30.4 6.4 scatter_fusion
  36.8 5.6 fusion.188
  56.3 5.6 fusion.187
  66.1 35.4 %all-gather.5.cloned.1.call-done = f32[1,16,20864]{2,0,1:T(1,128)} async-done(((f32[1,1,20864]{2,0,1:T(1,128)}), f32[1,16,20864]{2,0,1:T(1,128)}) %all-gather.5.cloned.1.call-update) | async-done | bytes 1335312 | tf_op jit(solution)/shard_map/all_gather | solution.py:272
  103.3 6.8 concatenate.612
  110.2 6.9 concatenate.611
  120.5 3.1 constant_dynamic-update-slice_fusion
  125.2 5.6 multiply_subtract_fusion
  130.9 3.8 slice.756
  136.2 9.9 %slice_multiply_fusion = (f32[1,1,4,36,64,1]{5,4,3,2,1,0:T(8,128)}, f32[1,1,4,36,64,1]{5,4,3,2,1,0:T(8,128)}) fusion(f32[1,1,4,36,64,129]{5,4,3,2,1,0:T(8,128)} %copy-done, f32[]{:T(128)} %bitcast.22, f32[]{:T(128)} %bitcast.21), kind=kLoop, calls=%fused_computation.25 | loop fusion | flops 18432 | bytes 147464 | tf_op jit(solution)/shard_map/mul | solution.py:74
  151.8 4.6 multiply_subtract_fusion.1
  159.8 9.6 %fusion.1 = f32[1,1,4,36,64,128]{5,4,3,2,1,0:T(8,128)S(1)} fusion(f32[1,1,4,36,64,128]{5,4,3,2,1,0:T(8,128)S(1)} %bitcast.678, f32[1,1,4,36,64,1]{5,4,3,2,1,0:T(8,128)} %get-tuple-element.253, f32[1,1,4,36,64,127]{5,4,3,2,1,0:T(8,128)S(1)} %bitcast.680, f32[1,1,4,36,64,1]{5,4,3,2,1,0:T(8,128)} %get-tuple-element.252, ...), kind=kLoop, calls=%fused_computation.29 | loop fusion | flops 9437184 | bytes 18984960 | tf_op jit(solution)/shard_map/sub | solution.py:116
  169.7 3.0 add_dynamic-update-slice_fusion
  177.2 11.2 %scatter_fusion.1 = s32[8,29]{1,0:T(8,128)S(1)} fusion(s32[8,29]{1,0:T(8,128)S(1)} %broadcast.10948.clone.1, s32[256]{0:T(256)S(1)} %reshape.20049, s32[256]{0:T(256)S(1)} %reshape.20051), kind=kCustom, calls=%fused_computation.19 | custom fusion | bytes 5120 | tf_op jit(solution)/shard_map/scatter | solution.py:32
  192.0 47.6 %all-gather.11.cloned.1.call-done = f32[1,16,5,64,128]{4,3,2,0,1:T(8,128)} async-done(((f32[1,1,5,64,128]{4,3,2,0,1:T(8,128)}), f32[1,16,5,64,128]{4,3,2,0,1:T(8,128)}) %all-gather.11.cloned.1.call-update) | async-done | bytes 2621456 | tf_op jit(solution)/shard_map/all_gather | solution.py:321
  245.2 22.5 %all_gather.43 = f32[1,32,128]{2,0,1:T(1,128)S(1)} all-gather(f32[1,2,128]{2,0,1:T(1,128)S(1)} %bitcast.718), channel_id=1, replica_groups=mesh['gx'=16,'gy'=8] {'gx'}, dimensions={1}, use_global_device_ids=true | all-gather | bytes 17408 | tf_op jit(solution)/shard_map/all_gather | solution.py:200
  269.2 21.2 %all_gather.45 = f32[1,32,128]{2,0,1:T(1,128)S(1)} all-gather(f32[1,2,128]{2,0,1:T(1,128)S(1)} %bitcast.724), channel_id=1, replica_groups=mesh['gx'=16,'gy'=8] {'gx'}, dimensions={1}, use_global_device_ids=true | all-gather | bytes 17408 | tf_op jit(solution)/shard_map/all_gather | solution.py:201
  290.4 22.5 %all_gather.44 = f32[1,32,128]{2,0,1:T(1,128)S(1)} all-gather(f32[1,2,128]{2,0,1:T(1,128)S(1)} %bitcast.723), channel_id=1, replica_groups=mesh['gx'=16,'gy'=8] {'gx'}, dimensions={1}, use_global_device_ids=true | all-gather | bytes 17408 | tf_op jit(solution)/shard_map/all_gather | solution.py:202
  314.9 65.6 %all-reduce.4 = (f32[]{:T(128)}, f32[]{:T(128)}) all-reduce(f32[]{:T(128)} %get-tuple-element.130, f32[]{:T(128)} %get-tuple-element.129), channel_id=1, replica_groups=mesh['gx'=16,'gy'=8] {'gx','gy'}, use_global_device_ids=true, to_apply=%region_3.5 | all-reduce | flops 2 | bytes 16 | tf_op jit(solution)/shard_map/psum | solution.py:213
  382.5 64.3 %psum.44 = f32[]{:T(128)} all-reduce(f32[]{:T(128)} %get-tuple-element.143), channel_id=1, replica_groups=mesh['gx'=16,'gy'=8] {'gx','gy'}, use_global_device_ids=true, to_apply=%region_8.11 | all-reduce | flops 1 | bytes 8 | tf_op jit(solution)/shard_map/psum | solution.py:213
  448.4 20.8 %all_gather.46 = f32[1,32,128]{2,0,1:T(1,128)S(1)} all-gather(f32[1,2,128]{2,0,1:T(1,128)S(1)} %bitcast.719), channel_id=1, replica_groups=mesh['gx'=16,'gy'=8] {'gx'}, dimensions={1}, use_global_device_ids=true | all-gather | bytes 17408 | tf_op jit(solution)/shard_map/all_gather | solution.py:200
  473.4 22.9 %all_gather.48 = f32[1,32,128]{2,0,1:T(1,128)S(1)} all-gather(f32[1,2,128]{2,0,1:T(1,128)S(1)} %bitcast.726), channel_id=1, replica_groups=mesh['gx'=16,'gy'=8] {'gx'}, dimensions={1}, use_global_device_ids=true | all-gather | bytes 17408 | tf_op jit(solution)/shard_map/all_gather | solution.py:201
  496.9 20.8 %all_gather.47 = f32[1,32,128]{2,0,1:T(1,128)S(1)} all-gather(f32[1,2,128]{2,0,1:T(1,128)S(1)} %bitcast.725), channel_id=1, replica_groups=mesh['gx'=16,'gy'=8] {'gx'}, dimensions={1}, use_global_device_ids=true | all-gather | bytes 17408 | tf_op jit(solution)/shard_map/all_gather | solution.py:202
  519.1 65.1 %psum.45 = f32[]{:T(128)} all-reduce(f32[]{:T(128)} %get-tuple-element.141), channel_id=1, replica_groups=mesh['gx'=16,'gy'=8] {'gx','gy'}, use_global_device_ids=true, to_apply=%region_10.13 | all-reduce | flops 1 | bytes 8 | tf_op jit(solution)/shard_map/psum | solution.py:223
  586.1 65.1 %psum.46 = f32[]{:T(128)} all-reduce(f32[]{:T(128)} %multiply_reduce_fusion), channel_id=1, replica_groups=mesh['gx'=16,'gy'=8] {'gx','gy'}, use_global_device_ids=true, to_apply=%region_12.15 | all-reduce | flops 1 | bytes 8 | tf_op jit(solution)/shard_map/psum | solution.py:213
  652.9 20.4 %all_gather.49 = f32[1,32,128]{2,0,1:T(1,128)S(1)} all-gather(f32[1,2,128]{2,0,1:T(1,128)S(1)} %bitcast.720), channel_id=1, replica_groups=mesh['gx'=16,'gy'=8] {'gx'}, dimensions={1}, use_global_device_ids=true | all-gather | bytes 17408 | tf_op jit(solution)/shard_map/all_gather | solution.py:200
  676.2 3.0 collective-permute-start.7
  679.2 23.3 %all_gather.50 = f32[1,32,128]{2,0,1:T(1,128)S(1)} all-gather(f32[1,2,128]{2,0,1:T(1,128)S(1)} %bitcast.728), channel_id=1, replica_groups=mesh['gx'=16,'gy'=8] {'gx'}, dimensions={1}, use_global_device_ids=true | all-gather | bytes 17408 | tf_op jit(solution)/shard_map/all_gather | solution.py:202
  703.2 20.4 %all_gather.51 = f32[1,32,128]{2,0,1:T(1,128)S(1)} all-gather(f32[1,2,128]{2,0,1:T(1,128)S(1)} %bitcast.727), channel_id=1, replica_groups=mesh['gx'=16,'gy'=8] {'gx'}, dimensions={1}, use_global_device_ids=true | all-gather | bytes 17408 | tf_op jit(solution)/shard_map/all_gather | solution.py:201
  724.9 62.4 %psum.47 = f32[]{:T(128)} all-reduce(f32[]{:T(128)} %fusion.60), channel_id=1, replica_groups=mesh['gx'=16,'gy'=8] {'gx','gy'}, use_global_device_ids=true, to_apply=%region_14.17 | all-reduce | flops 1 | bytes 8 | tf_op jit(solution)/shard_map/psum | solution.py:223
  (328 shorter events, 63.7 us)
Async XLA Ops:
  7.2 57.5 %all-gather.9.cloned.1.call-start = ((), (), s32[]{:S(2)}) async-start(), calls=%async_computation.2 | async-start | bytes 1262080 | tf_op jit(solution)/shard_map/all_gather | solution.py:274
  10.0 91.5 %all-gather.5.cloned.1.call-start = ((), (), s32[]{:S(2)}) async-start(), calls=%async_computation | async-start | bytes 1418752 | tf_op jit(solution)/shard_map/all_gather | solution.py:272
  19.9 127.3 %all-gather.7.cloned.1.call-start = ((), (), s32[]{:S(2)}) async-start(), calls=%async_computation.1 | async-start | bytes 1575424 | tf_op jit(solution)/shard_map/all_gather | solution.py:273
  20.7 218.9 %all-gather.11.cloned.1.call-start = ((), (), s32[]{:S(2)}) async-start(), calls=%async_computation.3 | async-start | bytes 2785280 | tf_op jit(solution)/shard_map/all_gather | solution.py:321
  30.4 21.9 %copy-start.4 = (f32[1,1,35,64,128]{4,3,2,1,0:T(8,128)S(1)}, f32[1,1,35,64,128]{4,3,2,1,0:T(8,128)}, u32[]{:S(2)}) copy-start(f32[1,1,35,64,128]{4,3,2,1,0:T(8,128)} %param.13) | copy-start | bytes 3440644
  46.2 10.1 %copy-start.46 = (s32[8,28]{1,0:T(8,128)S(1)}, s32[8,28]{1,0:T(8,128)}, u32[]{:S(2)}) copy-start(s32[8,28]{1,0:T(8,128)} %param.15) | copy-start | bytes 2692
  64.7 84.0 %collective-permute-start.1 = (f32[1,16,18560]{2,0,1:T(1,128)}, f32[1,16,18560]{2,0,1:T(1,128)}, u32[]{:S(2)}, u32[]{:S(2)}) collective-permute-start(f32[1,16,18560]{2,0,1:T(1,128)} %all-gather.9.cloned.1.call-done), channel_id=1, source_target_pairs={{1,0},{2,1},{3,2},{4,3},{5,4},{6,5},{7,6},{9,8},{10,9},{11,10},{12... | collective-permute-start | bytes 3563528 | tf_op jit(solution)/shard_map/ppermute | solution.py:20
  103.3 14.9 %copy-start.6 = (f32[1,1,1,36,64,128]{5,4,3,2,1,0:T(8,128)S(1)}, f32[1,1,1,36,64,128]{5,4,3,2,1,0:T(8,128)}, u32[]{:S(2)}) copy-start(f32[1,1,1,36,64,128]{5,4,3,2,1,0:T(8,128)} %get-tuple-element.259) | copy-start | bytes 3538948
  136.2 15.4 %copy-start.5 = (f32[1,1,1,36,64,128]{5,4,3,2,1,0:T(8,128)S(1)}, f32[1,1,1,36,64,128]{5,4,3,2,1,0:T(8,128)}, u32[]{:S(2)}) copy-start(f32[1,1,1,36,64,128]{5,4,3,2,1,0:T(8,128)} %get-tuple-element.258) | copy-start | bytes 3538948
  147.1 4.4 collective-permute-start
  159.4 9.9 %copy-start.9 = (f32[64,128]{1,0:T(8,128)S(1)}, f32[64,128]{1,0:T(8,128)}, u32[]{:S(2)}) copy-start(f32[64,128]{1,0:T(8,128)} %get-tuple-element.263) | copy-start | bytes 98308
  159.4 9.9 %copy-start.10 = (f32[64,128]{1,0:T(8,128)S(1)}, f32[64,128]{1,0:T(8,128)}, u32[]{:S(2)}) copy-start(f32[64,128]{1,0:T(8,128)} %get-tuple-element.183) | copy-start | bytes 98308
  159.4 9.9 %copy-start.11 = (f32[64,128]{1,0:T(8,128)S(1)}, f32[64,128]{1,0:T(8,128)}, u32[]{:S(2)}) copy-start(f32[64,128]{1,0:T(8,128)} %get-tuple-element.188) | copy-start | bytes 98308
  159.5 9.9 %copy-start.12 = (f32[64,128]{1,0:T(8,128)S(1)}, f32[64,128]{1,0:T(8,128)}, u32[]{:S(2)}) copy-start(f32[64,128]{1,0:T(8,128)} %get-tuple-element.192) | copy-start | bytes 98308
  159.5 9.9 %copy-start.13 = (f32[64,128]{1,0:T(8,128)S(1)}, f32[64,128]{1,0:T(8,128)}, u32[]{:S(2)}) copy-start(f32[64,128]{1,0:T(8,128)} %get-tuple-element.196) | copy-start | bytes 98308
  159.5 9.9 %copy-start.14 = (f32[64,128]{1,0:T(8,128)S(1)}, f32[64,128]{1,0:T(8,128)}, u32[]{:S(2)}) copy-start(f32[64,128]{1,0:T(8,128)} %get-tuple-element.200) | copy-start | bytes 98308
  159.5 9.9 %copy-start.15 = (f32[64,128]{1,0:T(8,128)S(1)}, f32[64,128]{1,0:T(8,128)}, u32[]{:S(2)}) copy-start(f32[64,128]{1,0:T(8,128)} %get-tuple-element.204) | copy-start | bytes 98308
  159.5 9.9 %copy-start.16 = (f32[64,128]{1,0:T(8,128)S(1)}, f32[64,128]{1,0:T(8,128)}, u32[]{:S(2)}) copy-start(f32[64,128]{1,0:T(8,128)} %get-tuple-element.208) | copy-start | bytes 98308
  159.5 9.9 %copy-start.17 = (f32[64,128]{1,0:T(8,128)S(1)}, f32[64,128]{1,0:T(8,128)}, u32[]{:S(2)}) copy-start(f32[64,128]{1,0:T(8,128)} %get-tuple-element.212) | copy-start | bytes 98308
  159.5 9.9 %copy-start.18 = (f32[64,128]{1,0:T(8,128)S(1)}, f32[64,128]{1,0:T(8,128)}, u32[]{:S(2)}) copy-start(f32[64,128]{1,0:T(8,128)} %get-tuple-element.216) | copy-start | bytes 98308
  159.5 9.9 %copy-start.19 = (f32[64,128]{1,0:T(8,128)S(1)}, f32[64,128]{1,0:T(8,128)}, u32[]{:S(2)}) copy-start(f32[64,128]{1,0:T(8,128)} %get-tuple-element.220) | copy-start | bytes 98308
  159.5 9.9 %copy-start.20 = (f32[64,128]{1,0:T(8,128)S(1)}, f32[64,128]{1,0:T(8,128)}, u32[]{:S(2)}) copy-start(f32[64,128]{1,0:T(8,128)} %get-tuple-element.224) | copy-start | bytes 98308
  159.5 9.9 %copy-start.21 = (f32[64,128]{1,0:T(8,128)S(1)}, f32[64,128]{1,0:T(8,128)}, u32[]{:S(2)}) copy-start(f32[64,128]{1,0:T(8,128)} %get-tuple-element.228) | copy-start | bytes 98308
  159.6 9.9 %copy-start.22 = (f32[64,128]{1,0:T(8,128)S(1)}, f32[64,128]{1,0:T(8,128)}, u32[]{:S(2)}) copy-start(f32[64,128]{1,0:T(8,128)} %get-tuple-element.232) | copy-start | bytes 98308
  159.6 9.9 %copy-start.23 = (f32[64,128]{1,0:T(8,128)S(1)}, f32[64,128]{1,0:T(8,128)}, u32[]{:S(2)}) copy-start(f32[64,128]{1,0:T(8,128)} %get-tuple-element.236) | copy-start | bytes 98308
  159.6 9.9 %copy-start.24 = (f32[64,128]{1,0:T(8,128)S(1)}, f32[64,128]{1,0:T(8,128)}, u32[]{:S(2)}) copy-start(f32[64,128]{1,0:T(8,128)} %get-tuple-element.240) | copy-start | bytes 98308
  242.4 26.9 %collective-permute-start.3 = (f32[1,2,128]{2,1,0:T(2,128)S(1)}, f32[1,2,128]{2,1,0:T(2,128)S(1)}, u32[]{:S(2)}, u32[]{:S(2)}) collective-permute-start(f32[1,2,128]{2,1,0:T(2,128)S(1)} %bitcast.731), channel_id=1, source_target_pairs={{0,1},{1,2},{2,3},{3,4},{4,5},{5,6},{6,7},{8,9},{9,10},{10,11},{11... | collective-permute-start | bytes 3080 | tf_op jit(solution)/shard_map/ppermute | solution.py:20
  243.8 46.6 %collective-permute-start.2 = (f32[1,2,128]{2,1,0:T(2,128)S(1)}, f32[1,2,128]{2,1,0:T(2,128)S(1)}, u32[]{:S(2)}, u32[]{:S(2)}) collective-permute-start(f32[1,2,128]{2,1,0:T(2,128)S(1)} %bitcast.730), channel_id=1, source_target_pairs={{1,0},{2,1},{3,2},{4,3},{5,4},{6,5},{7,6},{9,8},{10,9},{11,10},{12... | collective-permute-start | bytes 3080 | tf_op jit(solution)/shard_map/ppermute | solution.py:20
  470.4 3.0 collective-permute-start.5
  471.7 25.3 %collective-permute-start.4 = (f32[1,2,128]{2,1,0:T(2,128)S(1)}, f32[1,2,128]{2,1,0:T(2,128)S(1)}, u32[]{:S(2)}, u32[]{:S(2)}) collective-permute-start(f32[1,2,128]{2,1,0:T(2,128)S(1)} %bitcast.729), channel_id=1, source_target_pairs={{1,0},{2,1},{3,2},{4,3},{5,4},{6,5},{7,6},{9,8},{10,9},{11,10},{12... | collective-permute-start | bytes 3080 | tf_op jit(solution)/shard_map/ppermute | solution.py:20
  674.7 4.6 collective-permute-start.6
  676.2 27.0 %collective-permute-start.7 = (f32[1,2,128]{2,1,0:T(2,128)S(1)}, f32[1,2,128]{2,1,0:T(2,128)S(1)}, u32[]{:S(2)}, u32[]{:S(2)}) collective-permute-start(f32[1,2,128]{2,1,0:T(2,128)S(1)} %bitcast.732), channel_id=1, source_target_pairs={{0,1},{1,2},{2,3},{3,4},{4,5},{5,6},{6,7},{8,9},{9,10},{10,11},{11... | collective-permute-start | bytes 3080 | tf_op jit(solution)/shard_map/ppermute | solution.py:20
  (33 other events, 258.6 us)
Sparse Core Ops, SparseCore 0:
  10.1 45.7 all-gather.8
  58.7 42.7 all-gather.4
  103.8 43.3 all-gather.6
  177.2 62.4 all-gather.10
where the time goes:
time: 798 us; the launch traced here: 796 us
  blocking collectives  517 us (65%)
  local copies, waits for them, and re-layouts  101 us (13%)
  waiting for transfers between devices  85.9 us (11%)
  other arithmetic  45.2 us (6%)
  between operations  33.6 us (4%)
  starting transfers between devices  12.9 us (2%)
    psum x3, blocking collectives, squares(): return lax.psum(jnp.sum(residual * residual), ('gx', 'gy'))  195 us
    psum x2, blocking collectives, solve(): lax.psum(jnp.sum(direction * image_field), ('gx', 'gy'))  127 us
    all_gather x3, blocking collectives, exchange_edges(): lax.all_gather(from_above, 'gx', axis=1, tiled=True)  66.6 us
    all_gather x3, blocking collectives, exchange_edges(): lax.all_gather(from_below, 'gx', axis=1, tiled=True)  64.5 us
    all_gather x3, blocking collectives, exchange_edges(): lax.all_gather(side_cols, 'gx', axis=1, tiled=True)  63.7 us
    all_gather x1, waiting for transfers between devices, body(): band_fields = lax.all_gather(packed, 'gx', axis=1, tiled=True)  47.6 us
    all_gather x1, waiting for transfers between devices, body(): lax.all_gather(side_cols, 'gx', axis=1, tiled=True)  35.4 us
    scatter x2, local copies, waits for them, and re-layouts, inverse_map(): jnp.zeros((row_count, row_width + 1), jnp.int32).at[row_ids, target]  17.6 us
  transfers between devices with their start and end apart: 12, of which 4 were waited for; matrix products, arithmetic and copies ran while one was open for 13% of the time, Pallas kernels for 0%

commit v1 on v0

v1 whole, which is shorter than its diff:
```python
import functools
import jax
import jax.numpy as jnp
from jax import lax
from jax.experimental import pallas as pl
from jax.experimental.pallas import tpu as pltpu
from jax.sharding import PartitionSpec as P

F32 = jnp.float32
LEV, BN, BE = 36, 64, 128
NBX = 28
PIECE = 40

DEPTH_ROW = 36

diffusion = 0.12
area_term = 0.1
thermal = 0.2
haline = 0.25
cabbeling = 0.05
forcing = 4.0

NBR = 0
FROM = 8
SEND = 12
TFROM = 28
TSEND = 30
PLAN = 40

DIRS = ((0, 1), (0, -1), (1, 0), (-1, 0), (1, 1), (1, -1), (-1, 1), (-1, -1))


def north_rows(group):
    return 3 * PIECE if group == 0 else 2 * PIECE


def item_rows(group):
    return north_rows(group) + 2 * PIECE + 2 * BN


def params(**more):
    return pltpu.CompilerParams(vmem_limit_bytes=48 * 1024 * 1024, **more)


VM = pl.BlockSpec(memory_space=pltpu.VMEM)
SM = pl.BlockSpec(memory_space=pltpu.SMEM)
ANY = pl.BlockSpec(memory_space=pl.ANY)


def plan_kernel(side, n_gy, slots, clinic, tropic, out):
    gx = lax.axis_index("gx")
    gy = lax.axis_index("gy")
    z = gx // side
    y = lax.rem(gx, side)

    def find(row, column, ok):
        row = jnp.clip(row, 0, n_gy - 1)
        slot = jnp.int32(-1)
        for s in range(slots):
            slot = jnp.where(clinic[row, s] == column, jnp.int32(s), slot)
        return jnp.where(ok, slot, jnp.int32(-1))

    def neighbour(column, dr, dc):
        row = gy + dr
        ok = jnp.logical_and(row >= 0, row < n_gy)
        target = column + dc
        target = jnp.where(target < 0, target + NBX, target)
        target = jnp.where(target >= NBX, target - NBX, target)
        return find(row, target, ok)

    column = clinic[gy, gx]
    for d, (dr, dc) in enumerate(DIRS):
        slot = neighbour(column, dr, dc)
        out[NBR + d] = jnp.where(slot < 0, jnp.int32(-1), slot * n_gy + gy + dr)
        if d < 4:
            shift = lax.rem(z - slot // side + side, side)
            out[FROM + d] = jnp.where(slot < 0, jnp.int32(-1), shift)
    for k in range(side):
        there = lax.rem(z + k, side) * side + y
        column = clinic[gy, there]
        for d, (dr, dc) in enumerate(DIRS[:4]):
            slot = neighbour(column, dr, dc)
            shift = lax.rem(y - lax.rem(slot, side) + side, side)
            out[SEND + 4 * k + d] = jnp.where(slot < 0, jnp.int32(0), shift)
        for b in range(2):
            column_b = tropic[gy, 2 * there + b]
            slot = find(gy, column_b, column_b >= 0)
            shift = lax.rem(y - lax.rem(slot, side) + side, side)
            out[TSEND + 2 * k + b] = jnp.where(slot < 0, jnp.int32(0), shift)
    for b in range(2):
        column_b = tropic[gy, 2 * gx + b]
        slot = find(gy, column_b, column_b >= 0)
        shift = lax.rem(z - slot // side + side, side)
        out[TFROM + b] = jnp.where(slot < 0, jnp.int32(-1), shift)
    for i in range(TSEND + 8, PLAN):
        out[i] = jnp.int32(0)


def pack_kernel(group, tracers, velocity, depth, north, south, east, west, q, vel, sems):
    first = 2 * group * LEV
    copies = [
        pltpu.make_async_copy(tracers.at[pl.ds(first + f * LEV, LEV)], q.at[f], sems.at[f])
        for f in range(2)
    ]
    if group == 0:
        copies += [
            pltpu.make_async_copy(velocity.at[pl.ds(f * LEV, LEV)], vel.at[f], sems.at[2 + f])
            for f in range(2)
        ]
    for copy in copies:
        copy.start()
    lane = lax.broadcasted_iota(jnp.int32, (BN, BE), 1)
    east[...] = jnp.zeros((BN, BE), F32)
    west[...] = jnp.zeros((BN, BE), F32)
    fields = 3 if group == 0 else 2
    for f in range(fields):
        north[pl.ds(f * PIECE + 32, 8), :] = jnp.zeros((8, BE), F32)
        if f < 2:
            south[pl.ds(f * PIECE + 32, 8), :] = jnp.zeros((8, BE), F32)
    for f in range(fields):
        copies[f].wait()
        source = q.at[f] if f < 2 else vel.at[0]

        def level(k, carry, f=f, source=source):
            tile = source[k]
            spot = f * LEV + k
            carry_e = jnp.where(lane == spot, pltpu.roll(tile, spot + 1, 1), carry[0])
            if f < 2:
                carry_w = jnp.where(lane == spot, pltpu.roll(tile, spot, 1), carry[1])
                return carry_e, carry_w
            return carry_e, carry[1]

        e, w = lax.fori_loop(0, LEV, level, (east[...], west[...]), unroll=2)
        east[...] = e
        west[...] = w
        if f == 2:
            copies[3].wait()
        rows = q.at[f] if f < 2 else vel.at[1]
        for k in range(LEV):
            north[pl.ds(f * PIECE + k, 1), :] = rows[k, pl.ds(BN - 1, 1), :]
            if f < 2:
                south[pl.ds(f * PIECE + k, 1), :] = rows[k, pl.ds(0, 1), :]
    if group == 0:
        north[pl.ds(DEPTH_ROW, 3), :] = depth[pl.ds(BN - 3, 3), :]
        south[pl.ds(DEPTH_ROW, 3), :] = depth[pl.ds(0, 3), :]


def pack(group, tracers, velocity, depth):
    shape = lambda *s: jax.ShapeDtypeStruct(s, F32)
    return pl.pallas_call(
        functools.partial(pack_kernel, group),
        out_shape=(
            shape(north_rows(group), BE),
            shape(2 * PIECE, BE),
            shape(BN, BE),
            shape(BN, BE),
        ),
        in_specs=[ANY, ANY, VM],
        out_specs=(VM, VM, VM, VM),
        scratch_shapes=[
            pltpu.VMEM((2, LEV, BN, BE), F32),
            pltpu.VMEM((2, LEV if group == 0 else 1, BN, BE), F32),
            pltpu.SemaphoreType.DMA((4,)),
        ],
        compiler_params=params(),
        name=f"pack{group}",
    )(tracers, velocity, depth)


def chosen(shift, arrays, start, rows):
    value = arrays[-1][pl.ds(start, rows), :]
    for k in range(len(arrays) - 1):
        value = jnp.where(shift == k, arrays[k][pl.ds(start, rows), :], value)
    return value


def select_kernel(group, plan, x0, x1, x2, x3, o0, o1, o2, o3):
    n = north_rows(group)
    spans = {3: (0, n), 2: (n, 2 * PIECE), 1: (n + 2 * PIECE, BN), 0: (n + 2 * PIECE + BN, BN)}
    for k, out in enumerate((o0, o1, o2, o3)):
        for d, (start, rows) in spans.items():
            out[pl.ds(start, rows), :] = chosen(
                plan[SEND + 4 * k + d], (x0, x1, x2, x3), start, rows
            )


def select(group, plan, arrays):
    rows = item_rows(group)
    return pl.pallas_call(
        functools.partial(select_kernel, group),
        out_shape=(jax.ShapeDtypeStruct((rows, BE), F32),) * 4,
        in_specs=[SM] + [VM] * 4,
        out_specs=(VM,) * 4,
        compiler_params=params(),
        name=f"select{group}",
    )(plan, *arrays)


def main_kernel(group, chunk, *refs):
    if group == 0:
        (plan, tracers, velocity, mixing, north, south, east, west, h0, h1, h2, h3, depth,
         new, force, items, q, vel, mix, fac, fe_s, fw_s, fn_s, fs_s, sems, out_sems) = refs
        vel_north, vel_east, vel_halo = north, east, (h0, h1, h2, h3)
    else:
        (plan, tracers, velocity, mixing, north, south, east, west, h0, h1, h2, h3,
         vel_north, vel_east, g0, g1, g2, g3, _aliased,
         new, q, vel, mix, fac, fe_s, fw_s, fn_s, fs_s, sems, out_sems) = refs
        vel_halo = (g0, g1, g2, g3)
    first = 2 * group * LEV
    parts = LEV // chunk
    copies = []
    for c in range(parts):
        levels = pl.ds(c * chunk, chunk)
        row = []
        for f in range(2):
            row.append(pltpu.make_async_copy(
                tracers.at[pl.ds(first + f * LEV + c * chunk, chunk)], q.at[f, levels], sems.at[c, f]))
            row.append(pltpu.make_async_copy(
                velocity.at[pl.ds(f * LEV + c * chunk, chunk)], vel.at[f, levels], sems.at[c, 2 + f]))
        size = chunk if c + 1 < parts else chunk - 1
        row.append(pltpu.make_async_copy(
            mixing.at[pl.ds(c * chunk, size)], mix.at[pl.ds(c * chunk, size)], sems.at[c, 4]))
        copies.append(row)
        for copy in row:
            copy.start()
    mix[LEV - 1] = jnp.zeros((BN, BE), F32)

    halo = (h0, h1, h2, h3)
    lane = lax.broadcasted_iota(jnp.int32, (BN, BE), 1)
    row_id = lax.broadcasted_iota(jnp.int32, (BN, BE), 0)
    n0, n = north_rows(0), north_rows(group)
    from_e, from_w, from_n, from_s = (plan[FROM + d] for d in range(4))

    def flux(speed, low, high):
        return speed * (0.5 * (low + high)) - diffusion * (high - low)

    def aligned(column_item):
        return jnp.where(lane < LEV, pltpu.roll(column_item, BE - 2 * LEV, 1),
                         pltpu.roll(column_item, BE - LEV, 1))

    col = n + 2 * PIECE
    col0 = n0 + 2 * PIECE
    from_east = chosen(from_e, halo, col + BN, BN)
    from_west = chosen(from_w, halo, col, BN)
    u_west = chosen(from_w, vel_halo, col0, BN)
    fe_s[...] = jnp.where(from_e >= 0, flux(aligned(vel_east[...]), east[...], from_east), 0.0)
    fw_s[...] = jnp.where(from_w >= 0, flux(aligned(u_west), from_west, west[...]), 0.0)
    v_own = vel_north[pl.ds(2 * PIECE, PIECE), :]
    v_south = chosen(from_s, vel_halo, 2 * PIECE, PIECE)
    for f in range(2):
        span = pl.ds(f * PIECE, PIECE)
        there = chosen(from_n, halo, n + f * PIECE, PIECE)
        fn_s[span, :] = jnp.where(from_n >= 0, flux(v_own, north[span, :], there), 0.0)
        there = chosen(from_s, halo, f * PIECE, PIECE)
        fs_s[span, :] = jnp.where(from_s >= 0, flux(v_south, there, south[span, :]), 0.0)

    def forward(k, carry):
        m_up, fac_up, sol_up = carry
        m = mix[k]
        half_u = 0.5 * vel[0, k]
        half_v = 0.5 * vel[1, k]
        ua, ub = half_u + diffusion, half_u - diffusion
        va, vb = half_v + diffusion, half_v - diffusion
        inverse = 1.0 / (1.0 + m_up + m - m_up * fac_up)
        fac_k = m * inverse
        fac[k] = fac_k
        sols = []
        for f in range(2):
            tile = q[f, k]
            spot = f * LEV + k
            fe = ua * tile + ub * pltpu.roll(tile, BE - 1, 1)
            fe = jnp.where(lane == BE - 1, pltpu.roll(fe_s[...], BE - 1 - spot, 1), fe)
            fw = jnp.where(lane == 0, pltpu.roll(fw_s[...], BE - spot, 1), pltpu.roll(fe, 1, 1))
            fn = va * tile + vb * pltpu.roll(tile, BN - 1, 0)
            fn = jnp.where(row_id == BN - 1, fn_s[pl.ds(f * PIECE + k, 1), :], fn)
            fs = jnp.where(row_id == 0, fs_s[pl.ds(f * PIECE + k, 1), :], pltpu.roll(fn, 1, 0))
            stirred = tile - (fe - fw) - (fn - fs)
            sol = (stirred + m_up * sol_up[f]) * inverse
            q[f, k] = sol
            sols.append(sol)
        return m, fac_k, tuple(sols)

    zero = jnp.zeros((BN, BE), F32)
    carry = (zero, zero, (zero, zero))
    for c in range(parts):
        for copy in copies[c]:
            copy.wait()
        carry = lax.fori_loop(c * chunk, (c + 1) * chunk, forward, carry)

    def backward(i, carry, top):
        k = top - i
        factor = fac[k]
        heat = q[0, k] + factor * carry[0]
        salt = q[1, k] + factor * carry[1]
        q[0, k] = heat
        q[1, k] = salt
        if group == 0:
            weight = (forcing * 2.0 / (LEV * (LEV + 1))) * (k + 1).astype(F32)
            density = haline * salt - thermal * heat - cabbeling * heat * heat
            return heat, salt, carry[2] + density * weight
        return heat, salt

    carry = (zero, zero, zero) if group == 0 else (zero, zero)
    outs = []
    for c in range(parts - 1, -1, -1):
        carry = lax.fori_loop(
            0, chunk, functools.partial(backward, top=(c + 1) * chunk - 1), carry)
        for f in range(2):
            copy = pltpu.make_async_copy(
                q.at[f, pl.ds(c * chunk, chunk)],
                new.at[pl.ds(first + f * LEV + c * chunk, chunk)], out_sems.at[c, f])
            copy.start()
            outs.append(copy)
    if group == 0:
        field = carry[2]
        force[...] = field
        turned = jnp.concatenate([field, depth[...]], axis=0).T
        east_item, west_item = turned[BE - 3:, :], turned[:3, :]
        sends = (east_item, west_item, field[BN - 3:, :], field[:3, :],
                 east_item, west_item, east_item, west_item)
        for d, item in enumerate(sends):
            to = plan[NBR + d]

            @pl.when(to >= 0)
            def _(to=to, item=item):
                items[to, pl.ds(0, 3), :] = item
    for copy in outs:
        copy.wait()


def main(group, args, chunk=6):
    shape = lambda *s: jax.ShapeDtypeStruct(s, F32)
    outs = [shape(4 * LEV, BN, BE)]
    out_specs = [ANY]
    in_specs = [SM, ANY, ANY, ANY] + [VM] * (len(args) - 4)
    aliases = {}
    if group == 0:
        outs += [shape(BN, BE), shape(128, 4, BE)]
        out_specs += [VM, VM]
    else:
        in_specs[-1] = ANY
        aliases = {len(args) - 1: 0}
    parts = LEV // chunk
    return pl.pallas_call(
        functools.partial(main_kernel, group, chunk),
        out_shape=tuple(outs),
        in_specs=in_specs,
        out_specs=tuple(out_specs),
        input_output_aliases=aliases,
        scratch_shapes=[
            pltpu.VMEM((2, LEV, BN, BE), F32),
            pltpu.VMEM((2, LEV, BN, BE), F32),
            pltpu.VMEM((LEV, BN, BE), F32),
            pltpu.VMEM((LEV, BN, BE), F32),
            pltpu.VMEM((BN, BE), F32),
            pltpu.VMEM((BN, BE), F32),
            pltpu.VMEM((2 * PIECE, BE), F32),
            pltpu.VMEM((2 * PIECE, BE), F32),
            pltpu.SemaphoreType.DMA((parts, 5)),
            pltpu.SemaphoreType.DMA((parts, 2)),
        ],
        compiler_params=params(),
        name=f"mix{group}",
    )(*args)


TALL, WIDE = BN + 8, 2 * BE


def krylov_kernel(plan, field, depth, h0, h1, h2, h3, got, vectors, sums, b_s, d_s):
    halo = (h0, h1, h2, h3)
    n = north_rows(0)
    lane = lax.broadcasted_iota(jnp.int32, (BE, BE), 1)
    nothing = jnp.zeros((3, BE), F32)

    def item(d):
        to = plan[NBR + d]
        return jnp.where(to >= 0, got[jnp.maximum(to, 0), pl.ds(0, 3), :], nothing)

    b_s[...] = jnp.zeros((TALL, WIDE), F32)
    d_s[...] = jnp.zeros((TALL, WIDE), F32)
    b_s[pl.ds(0, BN), pl.ds(0, BE)] = field[...]
    d_s[pl.ds(0, BN), pl.ds(0, BE)] = depth[...]
    b_s[pl.ds(BN, 3), pl.ds(0, BE)] = item(2)
    b_s[pl.ds(TALL - 3, 3), pl.ds(0, BE)] = item(3)
    from_n, from_s = plan[FROM + 2], plan[FROM + 3]
    d_s[pl.ds(BN, 3), pl.ds(0, BE)] = jnp.where(
        from_n >= 0, chosen(from_n, halo, n + DEPTH_ROW, 3), 0.0)
    d_s[pl.ds(TALL - 3, 3), pl.ds(0, BE)] = jnp.where(
        from_s >= 0, chosen(from_s, halo, DEPTH_ROW, 3), 0.0)
    middle = jnp.zeros((BE - 6, BE), F32)
    sides = jnp.concatenate([item(0), middle, item(1)], axis=0).T
    b_s[pl.ds(0, BN), pl.ds(BE, BE)] = sides[:BN]
    d_s[pl.ds(0, BN), pl.ds(BE, BE)] = sides[BN:]
    place = lax.broadcasted_iota(jnp.int32, (3, BE), 1)
    place = jnp.where(place >= BN, place - BN, place)

    def corner(north, south):
        return jnp.where(place < 3, north, jnp.where(
            jnp.logical_and(place >= 5, place < 8), pltpu.roll(south, BE - BN + 8, 1), 0.0))

    corners = jnp.concatenate([corner(item(4), item(6)), middle, corner(item(5), item(7))], axis=0).T
    b_s[pl.ds(BN, 8), pl.ds(BE, BE)] = corners[:8]
    d_s[pl.ds(BN, 8), pl.ds(BE, BE)] = corners[BN:BN + 8]

    d = d_s[...]
    east = lambda a: pltpu.roll(a, WIDE - 1, 1)
    west = lambda a: pltpu.roll(a, 1, 1)
    north = lambda a: pltpu.roll(a, TALL - 1, 0)
    south = lambda a: pltpu.roll(a, 1, 0)
    d_e, d_n = east(d), north(d)
    w_e = jnp.where(jnp.logical_and(d > 0, d_e > 0), 0.5 * (d + d_e), 0.0)
    w_n = jnp.where(jnp.logical_and(d > 0, d_n > 0), 0.5 * (d + d_n), 0.0)
    w_w, w_s = west(w_e), south(w_n)
    diagonal = area_term + w_e + w_w + w_n + w_s

    def operate(h):
        return diagonal * h - w_e * east(h) - w_w * west(h) - w_n * north(h) - w_s * south(h)

    v0 = b_s[...]
    v1 = operate(v0)
    v2 = operate(v1)
    v3 = operate(v2)
    v = [a[:BN, :BE] for a in (v0, v1, v2, v3)]
    for i in range(3):
        vectors[pl.ds(i * BN, BN), :] = v[i]
    pairs = ((0, 0), (0, 1), (1, 1), (1, 2), (2, 2), (2, 3))
    at = lax.broadcasted_iota(jnp.int32, (1, BE), 1)
    total = jnp.zeros((1, BE), F32)
    for i, (a, b) in enumerate(pairs):
        value = jnp.sum(jnp.sum(v[a] * v[b], axis=0, keepdims=True), axis=1, keepdims=True)
        total = jnp.where(at == i, value, total)
    for i in range(128):
        sums[i] = total


def krylov(plan, field, depth, halo, got):
    return pl.pallas_call(
        krylov_kernel,
        out_shape=(
            jax.ShapeDtypeStruct((3 * BN, BE), F32),
            jax.ShapeDtypeStruct((128, 1, BE), F32),
        ),
        in_specs=[SM] + [VM] * 7,
        out_specs=(VM, VM),
        scratch_shapes=[pltpu.VMEM((TALL, WIDE), F32)] * 2,
        compiler_params=params(),
        name="krylov",
    )(plan, field, depth, *halo, got)


def combine_kernel(plan, sums, a0, a1, a2, a3, o0, o1, o2, o3):
    total = jnp.sum(sums[...], axis=0, keepdims=True)
    moment = [total[:, i:i + 1] for i in range(6)]

    def inner(a, b, lift):
        value = None
        for i in range(len(a)):
            for j in range(len(b)):
                term = a[i] * b[j] * moment[i + j + lift]
                value = term if value is None else value + term
        return value

    one = jnp.ones((1, 1), F32)
    zero = jnp.zeros((1, 1), F32)
    residual, direction = [one], [one]
    solution = [zero, zero, zero]
    rr = moment[0]
    for step in range(3):
        alpha = rr / inner(direction, direction, 1)
        for i, c in enumerate(direction):
            solution[i] = solution[i] + alpha * c
        if step < 2:
            image = [zero] + direction
            padded = residual + [zero]
            residual = [r - alpha * c for r, c in zip(padded, image)]
            following = inner(residual, residual, 0)
            beta = following / rr
            direction = [r + beta * c for r, c in zip(residual, direction + [zero])]
            rr = following
    solved = []
    for a in (a0, a1, a2, a3):
        v = [a[pl.ds(i * BN, BN), :] for i in range(3)]
        solved.append(solution[0] * v[0] + solution[1] * v[1] + solution[2] * v[2])
    for k, out in enumerate((o0, o1, o2, o3)):
        for b in range(2):
            shift = plan[TSEND + 2 * k + b]
            value = solved[3]
            for j in range(3):
                value = jnp.where(shift == j, solved[j], value)
            out[pl.ds(b * BN, BN), :] = value


def combine(plan, sums, arrays):
    return pl.pallas_call(
        combine_kernel,
        out_shape=(jax.ShapeDtypeStruct((2 * BN, BE), F32),) * 4,
        in_specs=[SM] + [VM] * 5,
        out_specs=(VM,) * 4,
        compiler_params=params(),
        name="combine",
    )(plan, sums, *arrays)


def place_kernel(plan, a0, a1, a2, a3, out):
    for b in range(2):
        shift = plan[TFROM + b]
        value = chosen(shift, (a0, a1, a2, a3), b * BN, BN)
        out[b] = jnp.where(shift >= 0, value, 0.0)


def place(plan, arrays):
    return pl.pallas_call(
        place_kernel,
        out_shape=jax.ShapeDtypeStruct((2, BN, BE), F32),
        in_specs=[SM] + [VM] * 4,
        out_specs=VM,
        compiler_params=params(),
        name="place",
    )(plan, *arrays)


def body(tracers, velocity, mixing_rate, column_depth, ocean_mask, clinic_list, tropic_list):
    n_gx, n_gy = lax.axis_size("gx"), lax.axis_size("gy")
    side = 4
    tracers = tracers.reshape(4 * LEV, BN, BE)
    velocity = velocity.reshape(2 * LEV, BN, BE)
    mixing = mixing_rate.reshape(LEV - 1, BN, BE)
    depth = column_depth.reshape(BN, BE)

    def along_y(value, k):
        return lax.ppermute(value, "gx", [
            (z * side + y, z * side + (y + k) % side) for z in range(side) for y in range(side)])

    def along_z(value, k):
        return lax.ppermute(value, "gx", [
            (z * side + y, (z + k) % side * side + y) for z in range(side) for y in range(side)])

    plan = pl.pallas_call(
        functools.partial(plan_kernel, side, n_gy, n_gx),
        out_shape=jax.ShapeDtypeStruct((PLAN,), jnp.int32),
        in_specs=[SM, SM],
        out_specs=SM,
        name="plan",
    )(clinic_list, tropic_list)

    def route(group):
        north, south, east, west = pack(group, tracers, velocity, depth)
        below = lax.ppermute(north, "gy", [(i, i + 1) for i in range(n_gy - 1)])
        above = lax.ppermute(south, "gy", [(i, i - 1) for i in range(1, n_gy)])
        own = jnp.concatenate([below, above, east, west], axis=0)
        line = [own] + [along_y(own, k) for k in range(1, side)]
        sends = select(group, plan, line)
        halo = [sends[0]] + [along_z(sends[k], k) for k in range(1, side)]
        return (north, south, east, west), halo

    edges0, halo0 = route(0)
    new, field, items = main(0, (plan, tracers, velocity, mixing, *edges0, *halo0, depth))
    edges1, halo1 = route(1)
    (new,) = main(1, (plan, tracers, velocity, mixing, *edges1, *halo1,
                      edges0[0], edges0[2], *halo0, new))
    got = lax.all_to_all(items, ("gx", "gy"), 0, 0)
    vectors, sums = krylov(plan, field, depth, halo0, got)
    line = [vectors] + [along_y(vectors, k) for k in range(1, side)]
    totals = lax.all_to_all(sums, ("gx", "gy"), 0, 0)
    sends = combine(plan, totals.reshape(128, BE), line)
    arrived = [sends[0]] + [along_z(sends[k], k) for k in range(1, side)]
    height = place(plan, arrived)
    return new.reshape(1, 1, 4, LEV, BN, BE), height[None]


def solution(mesh):
    return jax.shard_map(
        body,
        mesh=mesh,
        in_specs=(
            P("gy", "gx", None, None, None, None),
            P("gy", "gx", None, None, None, None),
            P("gy", "gx", None, None, None),
            P("gy", "gx", None, None),
            P(),
            P(),
            P(),
        ),
        out_specs=(P("gy", "gx", None, None, None, None), P("gy", "gx", None, None)),
        check_vma=False,
    )
```

time: 798 us -> 151 us (0.19)
  blocking collectives: 517 us -> 16 us
  waiting for transfers between devices: 85.9 us -> 11.6 us
  local copies, waits for them, and re-layouts: 101 us -> 27.6 us
  Pallas kernels: 0 us -> 48.5 us
  other arithmetic: 45.2 us -> 0 us
  between operations: 33.6 us -> 1.01 us
  starting transfers between devices: 12.9 us -> 44.6 us
    psum x5 -> x0, blocking collectives: 322 us -> none  [the longest x3 195 us: squares(): return lax.psum(jnp.sum(residual * residual), ('gx', 'gy'))]
    all_gather x9 -> x0, blocking collectives: 195 us -> none  [the longest x3 66.6 us: exchange_edges(): lax.all_gather(from_above, 'gx', axis=1, tiled=True)]
    all_gather x4 -> x0, waiting for transfers between devices: 84 us -> none  [the longest x1 47.6 us: body(): band_fields = lax.all_gather(packed, 'gx', axis=1, tiled=True)]
    pallas_call x0 -> x10, Pallas kernels: none -> 48.5 us  [the longest x2 28.3 us: main(): pl.pallas_call(functools.partial(main_kernel, group, chunk), out_shape=tu...]
    ppermute x8 -> x22, starting transfers between devices: 12.7 us -> 37.5 us  [the longest x9 14.7 us: along_y(): lax.ppermute(value, 'gx', [(z * side + y, z * side + (y + k) % side) for...]
    sub x4 -> x0, other arithmetic: 21.3 us -> none  [the longest x2 10.2 us: divergence(): face_speed * (0.5 * (behind + forward)) - diffusion * (forward - behind)]
    slice x26 -> x0, local copies, waits for them, and re-layouts: 19.4 us -> none  [the longest x1 7.65 us: body(): tracers[..., 0].reshape(1, slot_count, -1)]
    gather x19 -> x0, local copies, waits for them, and re-layouts: 17.8 us -> none  [the longest x13 9 us: picked(): return jnp.take(band_rows[0], slot_ids[0], axis=0)[None]]
  transfers between devices with their start and end apart: 12 -> 23, of which waited for: 4 -> 4; matrix products, arithmetic and copies ran while one was open for 13% -> 3% of each run, Pallas kernels for 0% -> 18%
where the time goes in v1:
time: 151 us; the launch traced here: 149 us
  Pallas kernels  48.5 us (32%)
  starting transfers between devices  44.6 us (30%)
  local copies, waits for them, and re-layouts  27.6 us (18%)
  blocking collectives  16 us (11%)
  waiting for transfers between devices  11.6 us (8%)
    pallas_call x2, Pallas kernels, main(): pl.pallas_call(functools.partial(main_kernel, group, chunk), out_shape=tu...  28.3 us
    unnamed x82, local copies, waits for them, and re-layouts  25.6 us
    all_to_all x1, blocking collectives, body(): totals = lax.all_to_all(sums, ('gx', 'gy'), 0, 0)  16 us
    ppermute x9, starting transfers between devices, along_y(): lax.ppermute(value, 'gx', [(z * side + y, z * side + (y + k) % side) for...  14.7 us
    ppermute x9, starting transfers between devices, along_z(): lax.ppermute(value, 'gx', [(z * side + y, (z + k) % side * side + y) for...  14.3 us
    pallas_call x2, Pallas kernels, pack(): pl.pallas_call(functools.partial(pack_kernel, group), out_shape=(shape(no...  12.1 us
    all_to_all x1, starting transfers between devices, body(): got = lax.all_to_all(items, ('gx', 'gy'), 0, 0)  7.03 us
    ppermute x9, waiting for transfers between devices, along_z(): lax.ppermute(value, 'gx', [(z * side + y, (z + k) % side * side + y) for...  6.01 us
  transfers between devices with their start and end apart: 23, of which 4 were waited for; matrix products, arithmetic and copies ran while one was open for 3% of the time, Pallas kernels for 18%

profile of v1, /device:TPU:0, one launch (start us, length us, event | category | flops | bytes accessed | tf_op | source)
XLA Modules:
  0.0 149.3 jit_solution(9720811691614900758)
XLA Ops:
  0.6 1.7 %copy-done = f32[1,1,2,36,64,128]{5,4,3,2,1,0:T(8,128)S(1)} copy-done((f32[1,1,2,36,64,128]{5,4,3,2,1,0:T(8,128)S(1)}, f32[1,1,2,36,64,128]{5,4,3,2,1,0:T(8,128)}, u32[]{:S(2)}) %copy-start) | copy-done | bytes 2359320
  3.1 6.5 %pack0.1 = (f32[120,128]{1,0:T(8,128)S(1)}, f32[80,128]{1,0:T(8,128)S(1)}, f32[64,128]{1,0:T(8,128)S(1)}, f32[64,128]{1,0:T(8,128)S(1)}) custom-call(f32[144,64,128]{2,1,0:T(8,128)} %bitcast.18, f32[72,64,128]{2,1,0:T(8,128)S(1)} %bitcast.7, f32[64,128]{1,0:T(8,128)S(1)} %bitcast.13), custom_call_target="tpu_custom_call" | custom-call | tf_op jit(solution)/shard_map/pack0/pallas_call | solution.py:150
  9.6 1.6 %collective-permute-start.8 = (f32[120,128]{1,0:T(8,128)S(1)}, f32[120,128]{1,0:T(8,128)S(1)}, u32[]{:S(2)}, u32[]{:S(2)}) collective-permute-start(f32[120,128]{1,0:T(8,128)S(1)} %get-tuple-element.35.refs_4_.refs_12_), channel_id=1, source_target_pairs={{0,1},{1,2},{2,3},{3,4},{4,5},{5,6},{6,7},{8,9},{9,10},{10,11},{11... | collective-permute-start | bytes 184328 | tf_op jit(solution)/shard_map/ppermute | solution.py:549
  11.2 1.3 collective-permute-start.9
  13.1 3.0 %collective-permute-done.9 = f32[80,128]{1,0:T(8,128)S(1)} collective-permute-done((f32[80,128]{1,0:T(8,128)S(1)}, f32[80,128]{1,0:T(8,128)S(1)}, u32[]{:S(2)}, u32[]{:S(2)}) %collective-permute-start.9) | collective-permute-done | bytes 40992 | tf_op jit(solution)/shard_map/ppermute | solution.py:550
  18.0 1.6 %collective-permute-start.10 = (f32[328,128]{1,0:T(8,128)}, f32[328,128]{1,0:T(8,128)}, u32[]{:S(2)}, u32[]{:S(2)}) collective-permute-start(f32[328,128]{1,0:T(8,128)} %constant_dynamic-update-slice_fusion.4.x0), channel_id=1, source_target_pairs={{0,8},{8,16},{16,24},{24,0},{32,40},{40,48},{48,56},{56,32},{64,72... | collective-permute-start | bytes 503816 | tf_op jit(solution)/shard_map/ppermute | solution.py:532
  19.6 2.9 %collective-permute-start.11 = (f32[328,128]{1,0:T(8,128)}, f32[328,128]{1,0:T(8,128)}, u32[]{:S(2)}, u32[]{:S(2)}) collective-permute-start(f32[328,128]{1,0:T(8,128)} %constant_dynamic-update-slice_fusion.4.x0), channel_id=1, source_target_pairs={{0,16},{8,24},{16,0},{24,8},{32,48},{40,56},{48,32},{56,40},{64,80... | collective-permute-start | bytes 503816 | tf_op jit(solution)/shard_map/ppermute | solution.py:532
  22.5 1.3 collective-permute-start.12
  23.8 5.6 %pack1.1 = (f32[80,128]{1,0:T(8,128)}, f32[80,128]{1,0:T(8,128)}, f32[64,128]{1,0:T(8,128)S(1)}, f32[64,128]{1,0:T(8,128)S(1)}) custom-call(f32[144,64,128]{2,1,0:T(8,128)} %bitcast.19, f32[72,64,128]{2,1,0:T(8,128)S(1)} %bitcast.8, f32[64,128]{1,0:T(8,128)S(1)} %bitcast.14), custom_call_target="tpu_custom_call" | custom-call | tf_op jit(solution)/shard_map/pack1/pallas_call | solution.py:150
  30.6 4.4 %collective-permute-start = (f32[80,128]{1,0:T(8,128)}, f32[80,128]{1,0:T(8,128)}, u32[]{:S(2)}, u32[]{:S(2)}) collective-permute-start(f32[80,128]{1,0:T(8,128)} %get-tuple-element.27.refs_4_), channel_id=1, source_target_pairs={{0,1},{1,2},{2,3},{3,4},{4,5},{5,6},{6,7},{8,9},{9,10},{10,11},{11... | collective-permute-start | bytes 122888 | tf_op jit(solution)/shard_map/ppermute | solution.py:549
  35.0 1.3 collective-permute-start.1
  36.3 2.1 %plan.1.refs_0_ = s32[40]{0:T(128)} custom-call(s32[8,16]{1,0:T(8,128)} %clinic.1, s32[8,32]{1,0:T(8,128)} %tropic.1), custom_call_target="tpu_custom_call" | custom-call | tf_op jit(solution)/shard_map/plan/pallas_call | solution.py:539
  39.1 1.3 select0.1
  40.4 2.0 %collective-permute-start.13 = (f32[328,128]{1,0:T(8,128)S(1)}, f32[328,128]{1,0:T(8,128)S(1)}, u32[]{:S(2)}, u32[]{:S(2)}) collective-permute-start(f32[328,128]{1,0:T(8,128)S(1)} %get-tuple-element.40), channel_id=1, source_target_pairs={{0,32},{8,40},{16,48},{24,56},{32,64},{40,72},{48,80},{56,88},{64,... | collective-permute-start | bytes 503816 | tf_op jit(solution)/shard_map/ppermute | solution.py:536
  42.4 3.6 %collective-permute-start.14 = (f32[328,128]{1,0:T(8,128)S(1)}, f32[328,128]{1,0:T(8,128)S(1)}, u32[]{:S(2)}, u32[]{:S(2)}) collective-permute-start(f32[328,128]{1,0:T(8,128)S(1)} %get-tuple-element.41), channel_id=1, source_target_pairs={{0,64},{8,72},{16,80},{24,88},{32,96},{40,104},{48,112},{56,120},{... | collective-permute-start | bytes 503816 | tf_op jit(solution)/shard_map/ppermute | solution.py:536
  49.3 5.3 %collective-permute-done.14.refs_10_.refs_16_.h2 = f32[328,128]{1,0:T(8,128)S(1)} collective-permute-done((f32[328,128]{1,0:T(8,128)S(1)}, f32[328,128]{1,0:T(8,128)S(1)}, u32[]{:S(2)}, u32[]{:S(2)}) %collective-permute-start.14) | collective-permute-done | bytes 167968 | tf_op jit(solution)/shard_map/ppermute | solution.py:536
  57.7 13.6 %mix0.1 = (f32[144,64,128]{2,1,0:T(8,128)}, f32[64,128]{1,0:T(8,128)S(1)}, f32[128,4,128]{2,1,0:T(4,128)S(1)}) custom-call(s32[40]{0:T(128)S(1)} %copy-done.34, f32[144,64,128]{2,1,0:T(8,128)} %bitcast.20, f32[72,64,128]{2,1,0:T(8,128)S(1)} %bitcast.9, f32[35,64,128]{2,1,0:T(8,128)S(1)} %bitcast.11, f32[120,128]{1,0:T(8,128)S(1)} %copy-done.22, ...), custom_call_target="tpu_custom_call" | custom-call | tf_op jit(solution)/shard_map/mix0/pallas_call | solution.py:344
  72.7 7.0 %all-to-all-start = ((f32[128,4,128]{2,1,0:T(4,128)}), f32[128,4,128]{2,1,0:T(4,128)}, u32[]{:S(2)}, u32[]{:S(2)}) async-start(f32[128,4,128]{2,1,0:T(4,128)} %copy-done.20), calls=%async_computation | async-start | bytes 524288 | tf_op jit(solution)/shard_map/all_to_all | solution.py:562
  79.8 1.4 constant_dynamic-update-slice_fusion.1
  81.1 1.4 constant_dynamic-update-slice_fusion.x0
  83.4 2.7 %collective-permute-start.3 = (f32[288,128]{1,0:T(8,128)}, f32[288,128]{1,0:T(8,128)}, u32[]{:S(2)}, u32[]{:S(2)}) collective-permute-start(f32[288,128]{1,0:T(8,128)} %constant_dynamic-update-slice_fusion.x0), channel_id=1, source_target_pairs={{0,16},{8,24},{16,0},{24,8},{32,48},{40,56},{48,32},{56,40},{64,80... | collective-permute-start | bytes 442376 | tf_op jit(solution)/shard_map/ppermute | solution.py:532
  86.1 1.4 collective-permute-start.4
  87.5 2.6 %all-to-all-done.got = f32[128,4,128]{2,1,0:T(4,128)} async-done(((f32[128,4,128]{2,1,0:T(4,128)}), f32[128,4,128]{2,1,0:T(4,128)}, u32[]{:S(2)}, u32[]{:S(2)}) %all-to-all-start) | async-done | bytes 262176 | tf_op jit(solution)/shard_map/all_to_all | solution.py:562
  94.5 1.6 %krylov.1 = (f32[192,128]{1,0:T(8,128)S(1)}, f32[128,1,128]{2,1,0:T(1,128)S(1)}) custom-call(s32[40]{0:T(128)S(1)} %copy-done.35, f32[64,128]{1,0:T(8,128)S(1)} %copy-done.37, f32[64,128]{1,0:T(8,128)S(1)} %bitcast.16, f32[328,128]{1,0:T(8,128)S(1)} %copy-done.4, f32[328,128]{1,0:T(8,128)S(1)} %copy-done.7, f32[328,128]{1,0:T(8,128)S(1)} %copy-done.10, ...), custom_call_target="tpu_custom_call" | custom-call | tf_op jit(solution)/shard_map/krylov/pallas_call | solution.py:438
  99.6 1.9 %collective-permute-start.17 = (f32[192,128]{1,0:T(8,128)S(1)}, f32[192,128]{1,0:T(8,128)S(1)}, u32[]{:S(2)}, u32[]{:S(2)}) collective-permute-start(f32[192,128]{1,0:T(8,128)S(1)} %get-tuple-element.47.a0), channel_id=1, source_target_pairs={{0,16},{8,24},{16,0},{24,8},{32,48},{40,56},{48,32},{56,40},{64,80... | collective-permute-start | bytes 294920 | tf_op jit(solution)/shard_map/ppermute | solution.py:532
  101.5 1.5 collective-permute-start.18
  102.9 1.5 %collective-permute-start.6 = (f32[288,128]{1,0:T(8,128)S(1)}, f32[288,128]{1,0:T(8,128)S(1)}, u32[]{:S(2)}, u32[]{:S(2)}) collective-permute-start(f32[288,128]{1,0:T(8,128)S(1)} %get-tuple-element.33), channel_id=1, source_target_pairs={{0,64},{8,72},{16,80},{24,88},{32,96},{40,104},{48,112},{56,120},{... | collective-permute-start | bytes 442376 | tf_op jit(solution)/shard_map/ppermute | solution.py:536
  104.5 1.3 collective-permute-start.7
  105.7 16.0 %all_to_all.10 = f32[128,1,128]{2,1,0:T(1,128)S(1)} all-to-all(f32[128,1,128]{2,1,0:T(1,128)S(1)} %get-tuple-element.46), channel_id=1, replica_groups=mesh['gx'=16,'gy'=8] {'gx','gy'}, dimensions={0} | all-to-all | bytes 131072 | tf_op jit(solution)/shard_map/all_to_all | solution.py:565
  123.4 1.5 %collective-permute-start.20 = (f32[128,128]{1,0:T(8,128)S(1)}, f32[128,128]{1,0:T(8,128)S(1)}, u32[]{:S(2)}, u32[]{:S(2)}) collective-permute-start(f32[128,128]{1,0:T(8,128)S(1)} %get-tuple-element.50), channel_id=1, source_target_pairs={{0,64},{8,72},{16,80},{24,88},{32,96},{40,104},{48,112},{56,120},{... | collective-permute-start | bytes 196616 | tf_op jit(solution)/shard_map/ppermute | solution.py:536
  125.0 1.7 %collective-permute-start.21 = (f32[128,128]{1,0:T(8,128)S(1)}, f32[128,128]{1,0:T(8,128)S(1)}, u32[]{:S(2)}, u32[]{:S(2)}) collective-permute-start(f32[128,128]{1,0:T(8,128)S(1)} %get-tuple-element.51), channel_id=1, source_target_pairs={{0,96},{8,104},{16,112},{24,120},{32,0},{40,8},{48,16},{56,24},{64... | collective-permute-start | bytes 196616 | tf_op jit(solution)/shard_map/ppermute | solution.py:536
  133.4 14.7 %mix1.1 = f32[144,64,128]{2,1,0:T(8,128)} custom-call(s32[40]{0:T(128)S(1)} %copy-done.35, f32[144,64,128]{2,1,0:T(8,128)} %bitcast.21, f32[72,64,128]{2,1,0:T(8,128)S(1)} %bitcast.10, f32[35,64,128]{2,1,0:T(8,128)S(1)} %bitcast.12, f32[80,128]{1,0:T(8,128)} %get-tuple-element.27.refs_4_, ...), custom_call_target="tpu_custom_call", output_to_operand_aliasing={{}: (18, {})} | custom-call | tf_op jit(solution)/shard_map/mix1/pallas_call | solution.py:344
  (109 shorter events, 31.4 us)
Async XLA Ops:
  9.6 12.9 %copy-start.30 = (f32[64,128]{1,0:T(8,128)}, f32[64,128]{1,0:T(8,128)S(1)}, u32[]{:S(2)}) copy-start(f32[64,128]{1,0:T(8,128)S(1)} %get-tuple-element.38.refs_7_) | copy-start | bytes 98308
  9.6 45.0 %copy-start.1 = (f32[1,1,2,36,64,128]{5,4,3,2,1,0:T(8,128)S(1)}, f32[1,1,2,36,64,128]{5,4,3,2,1,0:T(8,128)}, u32[]{:S(2)}) copy-start(f32[1,1,2,36,64,128]{5,4,3,2,1,0:T(8,128)} %param.8) | copy-start | bytes 7077892
  9.6 45.0 %copy-start.2 = (f32[1,1,35,64,128]{4,3,2,1,0:T(8,128)S(1)}, f32[1,1,35,64,128]{4,3,2,1,0:T(8,128)}, u32[]{:S(2)}) copy-start(f32[1,1,35,64,128]{4,3,2,1,0:T(8,128)} %param.9) | copy-start | bytes 3440644
  9.6 44.9 %copy-start.16 = (f32[1,1,64,128]{3,2,1,0:T(8,128)S(1)}, f32[1,1,64,128]{3,2,1,0:T(8,128)}, u32[]{:S(2)}) copy-start(f32[1,1,64,128]{3,2,1,0:T(8,128)} %param.10) | copy-start | bytes 98308
  9.6 2.9 %collective-permute-start.8 = (f32[120,128]{1,0:T(8,128)S(1)}, f32[120,128]{1,0:T(8,128)S(1)}, u32[]{:S(2)}, u32[]{:S(2)}) collective-permute-start(f32[120,128]{1,0:T(8,128)S(1)} %get-tuple-element.35.refs_4_.refs_12_), channel_id=1, source_target_pairs={{0,1},{1,2},{2,3},{3,4},{4,5},{5,6},{6,7},{8,9},{9,10},{10,11},{11... | collective-permute-start | bytes 184328 | tf_op jit(solution)/shard_map/ppermute | solution.py:549
  11.2 4.9 %collective-permute-start.9 = (f32[80,128]{1,0:T(8,128)S(1)}, f32[80,128]{1,0:T(8,128)S(1)}, u32[]{:S(2)}, u32[]{:S(2)}) collective-permute-start(f32[80,128]{1,0:T(8,128)S(1)} %get-tuple-element.37.refs_5_), channel_id=1, source_target_pairs={{1,0},{2,1},{3,2},{4,3},{5,4},{6,5},{7,6},{9,8},{10,9},{11,10},{12... | collective-permute-start | bytes 122888 | tf_op jit(solution)/shard_map/ppermute | solution.py:550
  18.0 20.4 %collective-permute-start.10 = (f32[328,128]{1,0:T(8,128)}, f32[328,128]{1,0:T(8,128)}, u32[]{:S(2)}, u32[]{:S(2)}) collective-permute-start(f32[328,128]{1,0:T(8,128)} %constant_dynamic-update-slice_fusion.4.x0), channel_id=1, source_target_pairs={{0,8},{8,16},{16,24},{24,0},{32,40},{40,48},{48,56},{56,32},{64,72... | collective-permute-start | bytes 503816 | tf_op jit(solution)/shard_map/ppermute | solution.py:532
  19.6 18.9 %collective-permute-start.11 = (f32[328,128]{1,0:T(8,128)}, f32[328,128]{1,0:T(8,128)}, u32[]{:S(2)}, u32[]{:S(2)}) collective-permute-start(f32[328,128]{1,0:T(8,128)} %constant_dynamic-update-slice_fusion.4.x0), channel_id=1, source_target_pairs={{0,16},{8,24},{16,0},{24,8},{32,48},{40,56},{48,32},{56,40},{64,80... | collective-permute-start | bytes 503816 | tf_op jit(solution)/shard_map/ppermute | solution.py:532
  22.5 16.0 %collective-permute-start.12 = (f32[328,128]{1,0:T(8,128)}, f32[328,128]{1,0:T(8,128)}, u32[]{:S(2)}, u32[]{:S(2)}) collective-permute-start(f32[328,128]{1,0:T(8,128)} %constant_dynamic-update-slice_fusion.4.x0), channel_id=1, source_target_pairs={{0,24},{8,0},{16,8},{24,16},{32,56},{40,32},{48,40},{56,48},{64,88... | collective-permute-start | bytes 503816 | tf_op jit(solution)/shard_map/ppermute | solution.py:532
  30.6 16.3 %collective-permute-start = (f32[80,128]{1,0:T(8,128)}, f32[80,128]{1,0:T(8,128)}, u32[]{:S(2)}, u32[]{:S(2)}) collective-permute-start(f32[80,128]{1,0:T(8,128)} %get-tuple-element.27.refs_4_), channel_id=1, source_target_pairs={{0,1},{1,2},{2,3},{3,4},{4,5},{5,6},{6,7},{8,9},{9,10},{10,11},{11... | collective-permute-start | bytes 122888 | tf_op jit(solution)/shard_map/ppermute | solution.py:549
  35.0 12.7 %collective-permute-start.1 = (f32[80,128]{1,0:T(8,128)}, f32[80,128]{1,0:T(8,128)}, u32[]{:S(2)}, u32[]{:S(2)}) collective-permute-start(f32[80,128]{1,0:T(8,128)} %get-tuple-element.28.refs_5_), channel_id=1, source_target_pairs={{1,0},{2,1},{3,2},{4,3},{5,4},{6,5},{7,6},{9,8},{10,9},{11,10},{12... | collective-permute-start | bytes 122888 | tf_op jit(solution)/shard_map/ppermute | solution.py:550
  40.4 14.2 %copy-start.3 = (f32[328,128]{1,0:T(8,128)}, f32[328,128]{1,0:T(8,128)S(1)}, u32[]{:S(2)}) copy-start(f32[328,128]{1,0:T(8,128)S(1)} %get-tuple-element.39.refs_8_.refs_14_.h0) | copy-start | bytes 503812
  40.4 8.9 %collective-permute-start.13 = (f32[328,128]{1,0:T(8,128)S(1)}, f32[328,128]{1,0:T(8,128)S(1)}, u32[]{:S(2)}, u32[]{:S(2)}) collective-permute-start(f32[328,128]{1,0:T(8,128)S(1)} %get-tuple-element.40), channel_id=1, source_target_pairs={{0,32},{8,40},{16,48},{24,56},{32,64},{40,72},{48,80},{56,88},{64,... | collective-permute-start | bytes 503816 | tf_op jit(solution)/shard_map/ppermute | solution.py:536
  42.4 12.2 %collective-permute-start.14 = (f32[328,128]{1,0:T(8,128)S(1)}, f32[328,128]{1,0:T(8,128)S(1)}, u32[]{:S(2)}, u32[]{:S(2)}) collective-permute-start(f32[328,128]{1,0:T(8,128)S(1)} %get-tuple-element.41), channel_id=1, source_target_pairs={{0,64},{8,72},{16,80},{24,88},{32,96},{40,104},{48,112},{56,120},{... | collective-permute-start | bytes 503816 | tf_op jit(solution)/shard_map/ppermute | solution.py:536
  46.0 8.6 %collective-permute-start.15 = (f32[328,128]{1,0:T(8,128)S(1)}, f32[328,128]{1,0:T(8,128)S(1)}, u32[]{:S(2)}, u32[]{:S(2)}) collective-permute-start(f32[328,128]{1,0:T(8,128)S(1)} %get-tuple-element.42), channel_id=1, source_target_pairs={{0,96},{8,104},{16,112},{24,120},{32,0},{40,8},{48,16},{56,24},{64... | collective-permute-start | bytes 503816 | tf_op jit(solution)/shard_map/ppermute | solution.py:536
  49.3 22.1 %copy-start.6 = (f32[328,128]{1,0:T(8,128)}, f32[328,128]{1,0:T(8,128)S(1)}, u32[]{:S(2)}) copy-start(f32[328,128]{1,0:T(8,128)S(1)} %collective-permute-done.13.refs_9_.refs_15_.h1) | copy-start | bytes 503812
  54.5 16.8 %copy-start.9 = (f32[328,128]{1,0:T(8,128)}, f32[328,128]{1,0:T(8,128)S(1)}, u32[]{:S(2)}) copy-start(f32[328,128]{1,0:T(8,128)S(1)} %collective-permute-done.14.refs_10_.refs_16_.h2) | copy-start | bytes 503812
  54.5 16.9 %copy-start.12 = (f32[328,128]{1,0:T(8,128)}, f32[328,128]{1,0:T(8,128)S(1)}, u32[]{:S(2)}) copy-start(f32[328,128]{1,0:T(8,128)S(1)} %collective-permute-done.15.refs_11_.refs_17_.h3) | copy-start | bytes 503812
  57.7 32.3 %copy-start.35 = (s32[40]{0:T(128)S(1)}, s32[40]{0:T(128)}, u32[]{:S(2)}) copy-start(s32[40]{0:T(128)} %plan.1.refs_0_) | copy-start | bytes 484
  72.7 17.3 %all-to-all-start = ((f32[128,4,128]{2,1,0:T(4,128)}), f32[128,4,128]{2,1,0:T(4,128)}, u32[]{:S(2)}, u32[]{:S(2)}) async-start(f32[128,4,128]{2,1,0:T(4,128)} %copy-done.20), calls=%async_computation | async-start | bytes 524288 | tf_op jit(solution)/shard_map/all_to_all | solution.py:562
  82.5 14.1 %collective-permute-start.2 = (f32[288,128]{1,0:T(8,128)}, f32[288,128]{1,0:T(8,128)}, u32[]{:S(2)}, u32[]{:S(2)}) collective-permute-start(f32[288,128]{1,0:T(8,128)} %constant_dynamic-update-slice_fusion.x0), channel_id=1, source_target_pairs={{0,8},{8,16},{16,24},{24,0},{32,40},{40,48},{48,56},{56,32},{64,72... | collective-permute-start | bytes 442376 | tf_op jit(solution)/shard_map/ppermute | solution.py:532
  83.4 13.3 %collective-permute-start.3 = (f32[288,128]{1,0:T(8,128)}, f32[288,128]{1,0:T(8,128)}, u32[]{:S(2)}, u32[]{:S(2)}) collective-permute-start(f32[288,128]{1,0:T(8,128)} %constant_dynamic-update-slice_fusion.x0), channel_id=1, source_target_pairs={{0,16},{8,24},{16,0},{24,8},{32,48},{40,56},{48,32},{56,40},{64,80... | collective-permute-start | bytes 442376 | tf_op jit(solution)/shard_map/ppermute | solution.py:532
  86.1 10.5 %collective-permute-start.4 = (f32[288,128]{1,0:T(8,128)}, f32[288,128]{1,0:T(8,128)}, u32[]{:S(2)}, u32[]{:S(2)}) collective-permute-start(f32[288,128]{1,0:T(8,128)} %constant_dynamic-update-slice_fusion.x0), channel_id=1, source_target_pairs={{0,24},{8,0},{16,8},{24,16},{32,56},{40,32},{48,40},{56,48},{64,88... | collective-permute-start | bytes 442376 | tf_op jit(solution)/shard_map/ppermute | solution.py:532
  96.1 8.4 %collective-permute-start.16 = (f32[192,128]{1,0:T(8,128)S(1)}, f32[192,128]{1,0:T(8,128)S(1)}, u32[]{:S(2)}, u32[]{:S(2)}) collective-permute-start(f32[192,128]{1,0:T(8,128)S(1)} %get-tuple-element.47.a0), channel_id=1, source_target_pairs={{0,8},{8,16},{16,24},{24,0},{32,40},{40,48},{48,56},{56,32},{64,72... | collective-permute-start | bytes 294920 | tf_op jit(solution)/shard_map/ppermute | solution.py:532
  98.7 26.2 %collective-permute-start.5 = (f32[288,128]{1,0:T(8,128)S(1)}, f32[288,128]{1,0:T(8,128)S(1)}, u32[]{:S(2)}, u32[]{:S(2)}) collective-permute-start(f32[288,128]{1,0:T(8,128)S(1)} %get-tuple-element.32), channel_id=1, source_target_pairs={{0,32},{8,40},{16,48},{24,56},{32,64},{40,72},{48,80},{56,88},{64,... | collective-permute-start | bytes 442376 | tf_op jit(solution)/shard_map/ppermute | solution.py:536
  99.6 22.2 %collective-permute-start.17 = (f32[192,128]{1,0:T(8,128)S(1)}, f32[192,128]{1,0:T(8,128)S(1)}, u32[]{:S(2)}, u32[]{:S(2)}) collective-permute-start(f32[192,128]{1,0:T(8,128)S(1)} %get-tuple-element.47.a0), channel_id=1, source_target_pairs={{0,16},{8,24},{16,0},{24,8},{32,48},{40,56},{48,32},{56,40},{64,80... | collective-permute-start | bytes 294920 | tf_op jit(solution)/shard_map/ppermute | solution.py:532
  101.5 20.3 %collective-permute-start.18 = (f32[192,128]{1,0:T(8,128)S(1)}, f32[192,128]{1,0:T(8,128)S(1)}, u32[]{:S(2)}, u32[]{:S(2)}) collective-permute-start(f32[192,128]{1,0:T(8,128)S(1)} %get-tuple-element.47.a0), channel_id=1, source_target_pairs={{0,24},{8,0},{16,8},{24,16},{32,56},{40,32},{48,40},{56,48},{64,88... | collective-permute-start | bytes 294920 | tf_op jit(solution)/shard_map/ppermute | solution.py:532
  102.9 23.7 %collective-permute-start.6 = (f32[288,128]{1,0:T(8,128)S(1)}, f32[288,128]{1,0:T(8,128)S(1)}, u32[]{:S(2)}, u32[]{:S(2)}) collective-permute-start(f32[288,128]{1,0:T(8,128)S(1)} %get-tuple-element.33), channel_id=1, source_target_pairs={{0,64},{8,72},{16,80},{24,88},{32,96},{40,104},{48,112},{56,120},{... | collective-permute-start | bytes 442376 | tf_op jit(solution)/shard_map/ppermute | solution.py:536
  104.5 22.2 %collective-permute-start.7 = (f32[288,128]{1,0:T(8,128)S(1)}, f32[288,128]{1,0:T(8,128)S(1)}, u32[]{:S(2)}, u32[]{:S(2)}) collective-permute-start(f32[288,128]{1,0:T(8,128)S(1)} %get-tuple-element.34), channel_id=1, source_target_pairs={{0,96},{8,104},{16,112},{24,120},{32,0},{40,8},{48,16},{56,24},{64... | collective-permute-start | bytes 442376 | tf_op jit(solution)/shard_map/ppermute | solution.py:536
  122.6 25.5 %collective-permute-start.19 = (f32[128,128]{1,0:T(8,128)S(1)}, f32[128,128]{1,0:T(8,128)S(1)}, u32[]{:S(2)}, u32[]{:S(2)}) collective-permute-start(f32[128,128]{1,0:T(8,128)S(1)} %get-tuple-element.49), channel_id=1, source_target_pairs={{0,32},{8,40},{16,48},{24,56},{32,64},{40,72},{48,80},{56,88},{64,... | collective-permute-start | bytes 196616 | tf_op jit(solution)/shard_map/ppermute | solution.py:536
  123.4 24.7 %collective-permute-start.20 = (f32[128,128]{1,0:T(8,128)S(1)}, f32[128,128]{1,0:T(8,128)S(1)}, u32[]{:S(2)}, u32[]{:S(2)}) collective-permute-start(f32[128,128]{1,0:T(8,128)S(1)} %get-tuple-element.50), channel_id=1, source_target_pairs={{0,64},{8,72},{16,80},{24,88},{32,96},{40,104},{48,112},{56,120},{... | collective-permute-start | bytes 196616 | tf_op jit(solution)/shard_map/ppermute | solution.py:536
  125.0 23.1 %collective-permute-start.21 = (f32[128,128]{1,0:T(8,128)S(1)}, f32[128,128]{1,0:T(8,128)S(1)}, u32[]{:S(2)}, u32[]{:S(2)}) collective-permute-start(f32[128,128]{1,0:T(8,128)S(1)} %get-tuple-element.51), channel_id=1, source_target_pairs={{0,96},{8,104},{16,112},{24,120},{32,0},{40,8},{48,16},{56,24},{64... | collective-permute-start | bytes 196616 | tf_op jit(solution)/shard_map/ppermute | solution.py:536
  (29 other events, 54.7 us)

commit v2 on v1

v2 whole, which is shorter than its diff:
```python
import functools
import jax
import jax.numpy as jnp
from jax import lax
from jax.experimental import pallas as pl
from jax.experimental.pallas import tpu as pltpu
from jax.sharding import PartitionSpec as P

F32 = jnp.float32
LEV, BN, BE = 36, 64, 128
NBX = 28
CELLS = LEV * BN
HALF = BE // 2

NORTH = 0
NORTH_Q = (0, LEV, 3 * LEV, 4 * LEV)
NORTH_V = 2 * LEV
NORTH_D = 5 * LEV
SOUTH = 184
SOUTH_Q = tuple(SOUTH + f * LEV for f in range(4))
SOUTH_D = SOUTH + 4 * LEV
EAST = 332
WEST = 440
ITEM = 512
PART = 4

diffusion = 0.12
area_term = 0.1
thermal = 0.2
haline = 0.25
cabbeling = 0.05
forcing = 4.0

NBR = 0
TFROM = 8
TSEND = 10
RELAY = 18
PLAN = RELAY + 128
WRAP = NBX + 4

DIRS = ((0, 1), (0, -1), (1, 0), (-1, 0), (1, 1), (1, -1), (-1, 1), (-1, -1))


def params(mib, **more):
    return pltpu.CompilerParams(vmem_limit_bytes=mib * 1024 * 1024, **more)


VM = pl.BlockSpec(memory_space=pltpu.VMEM)
SM = pl.BlockSpec(memory_space=pltpu.SMEM)
ANY = pl.BlockSpec(memory_space=pl.ANY)
HBM = pl.BlockSpec(memory_space=pltpu.HBM)


def shaped(*shape):
    return jax.ShapeDtypeStruct(shape, F32)


def plan_kernel(side, n_gy, slots, clinic, tropic, out, pos):
    gx = lax.axis_index("gx")
    gy = lax.axis_index("gy")
    z = gx // side
    y = lax.rem(gx, side)

    def clear(i, carry):
        pos[i] = jnp.int32(-1)
        return carry

    lax.fori_loop(0, (n_gy + 2) * WRAP, clear, 0, unroll=16)
    for row in range(n_gy):
        for slot in range(slots):
            pos[(row + 1) * WRAP + 1 + clinic[row, slot]] = jnp.int32(slot * n_gy + row)
    for row in range(1, n_gy + 1):
        pos[row * WRAP] = pos[row * WRAP + NBX]
        pos[row * WRAP + NBX + 1] = pos[row * WRAP + 1]
    centre = (gy + 1) * WRAP + 1 + clinic[gy, gx]
    for d, (dr, dc) in enumerate(DIRS):
        out[NBR + d] = pos[centre + (dr * WRAP + dc)]
    me = gx * n_gy + gy
    kind_s, kind_n, kind_w = me < SOUTH // PART, me < EAST // PART, me < WEST // PART
    move = jnp.where(kind_s, jnp.int32(-WRAP), jnp.where(kind_n, jnp.int32(WRAP), jnp.where(
        kind_w, jnp.int32(-1), jnp.int32(1))))
    for row in range(n_gy):
        for there in range(slots):
            source = pos[(row + 1) * WRAP + 1 + clinic[row, there] + move]
            out[RELAY + there * n_gy + row] = jnp.maximum(source, 0)

    def owner(there, b):
        column_b = tropic[gy, 2 * there + b]
        device = pos[(gy + 1) * WRAP + 1 + jnp.maximum(column_b, 0)]
        return jnp.where(column_b < 0, jnp.int32(-1), device // n_gy)

    for k in range(side):
        there = lax.rem(z + k, side) * side + y
        for b in range(2):
            slot = owner(there, b)
            shift = lax.rem(y - lax.rem(slot, side) + side, side)
            out[TSEND + 2 * k + b] = jnp.where(slot < 0, jnp.int32(0), shift)
    for b in range(2):
        slot = owner(gx, b)
        shift = lax.rem(z - slot // side + side, side)
        out[TFROM + b] = jnp.where(slot < 0, jnp.int32(-1), shift)


def pack_kernel(tracers, velocity, depth_in, item, q, vel, turn, own, depth, sems):
    order = (0, 2, 4, 1, 3, 5)
    copies = {}
    fetch_depth = pltpu.make_async_copy(depth_in, depth, sems.at[6])
    fetch_depth.start()
    for f in order:
        source, at = (tracers, f) if f < 4 else (velocity, f - 4)
        target = q if f < 4 else vel
        span = pl.ds(at * CELLS, CELLS)
        copies[f] = pltpu.make_async_copy(source.at[span], target.at[span], sems.at[f])
        copies[f].start()
    fetch_depth.wait()
    lane = lax.broadcasted_iota(jnp.int32, (BN, BE), 1)
    level = lane // 2
    own[pl.ds(NORTH_D, 3), :] = depth[pl.ds(BN - 3, 3), :]
    own[pl.ds(NORTH_D + 3, 1), :] = jnp.zeros((1, BE), F32)
    own[pl.ds(SOUTH_D, 3), :] = depth[pl.ds(0, 3), :]
    own[pl.ds(SOUTH_D + 3, 1), :] = jnp.zeros((1, BE), F32)

    def columns(f):
        copies[f].wait()
        sides = jnp.zeros((BN, BE), F32)
        for k in range(LEV):
            tile = q[pl.ds(f * CELLS + k * BN, BN), :]
            sides = jnp.where(level == k, pltpu.roll(tile, 2 * k + 1, 1), sides)
        own[pl.ds(NORTH_Q[f], LEV), :] = q[pl.ds(f * CELLS + BN - 1, LEV, stride=BN), :]
        own[pl.ds(SOUTH_Q[f], LEV), :] = q[pl.ds(f * CELLS, LEV, stride=BN), :]
        return sides

    for j in range(2):
        first, second = columns(j), columns(2 + j)
        if j == 0:
            copies[4].wait()
            for k in range(LEV):
                tile = vel[pl.ds(k * BN, BN), :]
                first = jnp.where(lane == 2 * LEV + k, pltpu.roll(tile, 2 * LEV + 1 + k, 1), first)
        turn[...] = jnp.concatenate([first, second], axis=0).T
        own[pl.ds(EAST + j * LEV, LEV), :] = turn[pl.ds(0, LEV, stride=2), :]
        own[pl.ds(WEST + j * LEV, LEV), :] = turn[pl.ds(1, LEV, stride=2), :]
        if j == 0:
            own[pl.ds(EAST + 2 * LEV, LEV), :] = turn[pl.ds(2 * LEV, LEV), :]
    copies[5].wait()
    own[pl.ds(NORTH_V, LEV), :] = vel[pl.ds(CELLS + BN - 1, LEV, stride=BN), :]
    pltpu.sync_copy(own, item)


def pack(tracers, velocity, depth):
    return pl.pallas_call(
        pack_kernel,
        out_shape=pltpu.HBM((ITEM, BE), F32),
        in_specs=[HBM, HBM, HBM],
        out_specs=HBM,
        scratch_shapes=[
            pltpu.VMEM((4 * CELLS, BE), F32),
            pltpu.VMEM((2 * CELLS, BE), F32),
            pltpu.VMEM((BE, BE), F32),
            pltpu.VMEM((ITEM, BE), F32),
            pltpu.VMEM((BN, BE), F32),
            pltpu.SemaphoreType.DMA((7,)),
        ],
        compiler_params=params(12),
        name="pack",
    )(tracers, velocity, depth)


def select_kernel(plan, got, out, chosen_parts):
    def one(d, carry):
        chosen_parts[d] = got[plan[RELAY + d]]
        return carry

    lax.fori_loop(0, 128, one, 0, unroll=8)
    pltpu.sync_copy(chosen_parts, out)


def select(plan, got):
    return pl.pallas_call(
        select_kernel,
        out_shape=pltpu.HBM((128, PART, BE), F32),
        in_specs=[SM, VM],
        out_specs=HBM,
        scratch_shapes=[pltpu.VMEM((128, PART, BE), F32)],
        compiler_params=params(2),
        name="select",
    )(plan, got)


def stencil_loads(fields, chunk, tracers, velocity, mixing, q, u, v, mix, sems):
    parts = LEV // chunk
    rows = chunk * BN
    copies = []
    for c in range(parts):
        row = []
        for i, f in enumerate(fields):
            row.append(pltpu.make_async_copy(
                tracers.at[pl.ds(f * CELLS + c * rows, rows)], q[i].at[pl.ds(8 + c * rows, rows)],
                sems.at[c, i]))
        row.append(pltpu.make_async_copy(
            velocity.at[pl.ds(CELLS + c * rows, rows)], v.at[pl.ds(8 + c * rows, rows)], sems.at[c, 2]))
        row.append(pltpu.make_async_copy(
            velocity.at[pl.ds(c * rows, rows)], u.at[pl.ds(c * rows, rows)], sems.at[c, 3]))
        if mixing is not None:
            size = rows if c + 1 < parts else rows - BN
            row.append(pltpu.make_async_copy(
                mixing.at[pl.ds(c * rows, size)], mix.at[pl.ds(c * rows, size)], sems.at[c, 4]))
        copies.append(row)
    pad = jnp.zeros((8, BE), F32)
    for ref in (*q, v):
        ref[pl.ds(0, 8), :] = pad
        ref[pl.ds(8 + CELLS, 8), :] = pad
    return copies


def stencil_level(k, q, u, v, s):
    lane = lax.broadcasted_iota(jnp.int32, (BN, BE), 1)
    row_id = lax.broadcasted_iota(jnp.int32, (BN, BE), 0)
    at = pl.multiple_of(k * BN, BN)
    here, north, south = pl.ds(at + 8, BN), pl.ds(at + 9, BN), pl.ds(at + 7, BN)
    half_u = 0.5 * u[pl.ds(at, BN), :]
    half_w = pltpu.roll(half_u, 1, 1)
    ua = jnp.where(lane == BE - 1, 0.0, half_u + diffusion)
    ub = jnp.where(lane == BE - 1, 0.0, half_u - diffusion)
    uaw = jnp.where(lane == 0, 0.0, half_w + diffusion)
    ubw = jnp.where(lane == 0, 0.0, half_w - diffusion)
    half_v, half_s = 0.5 * v[here, :], 0.5 * v[south, :]
    va = jnp.where(row_id == BN - 1, 0.0, half_v + diffusion)
    vb = jnp.where(row_id == BN - 1, 0.0, half_v - diffusion)
    vas = jnp.where(row_id == 0, 0.0, half_s + diffusion)
    vbs = jnp.where(row_id == 0, 0.0, half_s - diffusion)
    centre = 1.0 - (ua - ubw) - (va - vbs)
    for f in range(2):
        tile = q[f][here, :]
        s[pl.ds(pl.multiple_of(f * CELLS + at, BN), BN), :] = (
            centre * tile - ub * pltpu.roll(tile, BE - 1, 1) + uaw * pltpu.roll(tile, 1, 1)
            - vb * q[f][north, :] + vas * q[f][south, :])


AHEAD = 6


def begin(copies, c):
    for copy in copies[c] if c < len(copies) else ():
        copy.start()


def arrived(copies, c, beyond=0):
    for d in range(1 + beyond) if c == 0 else (c + beyond,):
        for copy in copies[d] if d < len(copies) else ():
            copy.wait()
    begin(copies, c + AHEAD)


def stencil_kernel(group, chunk, *refs):
    parts = LEV // chunk
    rows = chunk * BN
    if group == 0:
        tracers, velocity, mixing, s, inv_out, q0, q1, u, v, inv, mix, sems, out_sems = refs
    else:
        tracers, velocity, stirred, q0, q1, u, v, s, sems, out_sems = refs
        mixing = mix = None
    q = (q0, q1)
    copies = stencil_loads((2 * group, 2 * group + 1), chunk, tracers, velocity, mixing, q, u, v, mix, sems)
    for c in range(AHEAD):
        begin(copies, c)
    zero = jnp.zeros((BN, BE), F32)
    if group == 0:
        mix[pl.ds(CELLS - BN, BN), :] = zero

    def level(k, carry):
        stencil_level(k, q, u, v, s)
        if group == 1:
            return carry
        m_up, fac_up = carry
        span = pl.ds(pl.multiple_of(k * BN, BN), BN)
        m = mix[span, :]
        inverse = 1.0 / (1.0 + m_up + m - m_up * fac_up)
        inv[span, :] = inverse
        return m, m * inverse

    carry = (zero, zero) if group == 0 else 0
    outs = []
    for c in range(parts):
        arrived(copies, c, 1)
        carry = lax.fori_loop(c * chunk, (c + 1) * chunk, level, carry, unroll=2)
        if group == 0:
            span = pl.ds(c * rows, rows)
            outs.append(pltpu.make_async_copy(inv.at[span], inv_out.at[span], out_sems.at[c, 0]))
            outs[-1].start()
        else:
            for f in range(2):
                span = pl.ds(f * CELLS + c * rows, rows)
                outs.append(pltpu.make_async_copy(s.at[span], stirred.at[span], out_sems.at[c, f]))
                outs[-1].start()
    for copy in outs:
        copy.wait()


def cells(extra=0, fields=1):
    return pltpu.VMEM((fields * CELLS + extra, BE), F32)


def stencil(group, args, chunk=6):
    parts = LEV // chunk
    if group == 0:
        outs, out_specs = (cells(0, 2), pltpu.HBM((CELLS, BE), F32)), (VM, HBM)
        more = [cells(), cells()]
    else:
        outs, out_specs = (pltpu.HBM((2 * CELLS, BE), F32),), (HBM,)
        more = [cells(0, 2)]
    return pl.pallas_call(
        functools.partial(stencil_kernel, group, chunk),
        out_shape=outs,
        in_specs=[HBM] * len(args),
        out_specs=out_specs,
        scratch_shapes=[
            cells(16), cells(16), cells(), cells(16), *more,
            pltpu.SemaphoreType.DMA((parts, 5)),
            pltpu.SemaphoreType.DMA((parts, 2)),
        ],
        compiler_params=params(10),
        name=f"stencil{group}",
    )(*args)


EDGE_N, EDGE_S, EDGE = BN, BN + 40, BN + 80
EDGE_D = 4 * EDGE


def flux(speed, low, high):
    return speed * (0.5 * (low + high)) - diffusion * (high - low)


def edges(plan, own, halo, out, turn):
    lane = lax.broadcasted_iota(jnp.int32, (LEV, BE), 1)
    open_e, open_w, open_n, open_s = (plan[NBR + d] >= 0 for d in range(4))
    row = lambda ref, at: ref[pl.ds(at, LEV), :]
    v_own, v_south = row(own, NORTH_V), row(halo, NORTH_V)
    for f in range(4):
        fn = flux(v_own, row(own, NORTH_Q[f]), row(halo, SOUTH_Q[f]))
        fs = flux(v_south, row(halo, NORTH_Q[f]), row(own, SOUTH_Q[f]))
        out[pl.ds(f * EDGE + EDGE_N, LEV), :] = jnp.where(open_n, -fn, 0.0)
        out[pl.ds(f * EDGE + EDGE_S, LEV), :] = jnp.where(open_s, fs, 0.0)

    def both(speed):
        return jnp.where(lane < HALF, speed, pltpu.roll(speed, HALF, 1))

    u_own, u_west = both(row(own, EAST + 2 * LEV)), both(row(halo, EAST + 2 * LEV))
    for j in range(2):
        fe = flux(u_own, row(own, EAST + j * LEV), row(halo, WEST + j * LEV))
        fw = flux(u_west, row(halo, EAST + j * LEV), row(own, WEST + j * LEV))
        turn[...] = jnp.zeros((BE, BE), F32)
        turn[pl.ds(0, LEV, stride=2), :] = jnp.where(open_e, -fe, 0.0)
        turn[pl.ds(1, LEV, stride=2), :] = jnp.where(open_w, fw, 0.0)
        turned = turn[...].T
        out[pl.ds(j * EDGE, BN), :] = turned[:BN]
        out[pl.ds((2 + j) * EDGE, BN), :] = turned[BN:]


def solve_kernel(group, chunk, out_chunk, *refs):
    parts = LEV // chunk
    rows = chunk * BN
    outs = []
    if group == 0:
        (plan, source, inv_in, mixing, own_in, halo, depth_in,
         new, edge_out, force_out, items, s, inv, mix, edge, turn, parts_out, own, depth, force,
         sems, out_sems, side_sems) = refs
        sides = [pltpu.make_async_copy(a, b, side_sems.at[i]) for i, (a, b) in enumerate(
            ((own_in, own), (depth_in, depth)))]
    else:
        (stirred, inv_in, mixing, edge_in, _aliased,
         new, s, inv, mix, edge, sems, out_sems, side_sems) = refs
        source = s
        sides = [pltpu.make_async_copy(edge_in, edge, side_sems.at[0])]
    for copy in sides:
        copy.start()
    first = 2 * group
    copies = []
    for c in range(parts):
        row = []
        if group == 1:
            for f in range(2):
                span = pl.ds(f * CELLS + c * rows, rows)
                row.append(pltpu.make_async_copy(stirred.at[span], s.at[span], sems.at[c, f]))
        span = pl.ds(c * rows, rows)
        row.append(pltpu.make_async_copy(inv_in.at[span], inv.at[span], sems.at[c, 2]))
        span = pl.ds(c * rows, rows if c + 1 < parts else rows - BN)
        row.append(pltpu.make_async_copy(mixing.at[span], mix.at[span], sems.at[c, 3]))
        copies.append(row)
        begin(copies, c)
    for copy in sides:
        copy.wait()
    if group == 0:
        edges(plan, own, halo, edge, turn)
        edge[pl.ds(EDGE_D, 8), :] = halo[pl.ds(NORTH_D - 4, 8), :]
        edge[pl.ds(EDGE_D + 8, 8), :] = halo[pl.ds(SOUTH_D, 8), :]
        outs.append(pltpu.make_async_copy(edge, edge_out, side_sems.at[3]))
        outs[-1].start()
    lane = lax.broadcasted_iota(jnp.int32, (BN, BE), 1)
    rim = jnp.logical_or(lane == 0, lane == BE - 1)
    sub = lax.broadcasted_iota(jnp.int32, (8, BE), 0)
    tile = lambda f, k: pl.ds(f * CELLS + k * BN, BN)
    m_up, sol_up = None, [None, None]
    columns = [edge[pl.ds((first + f) * EDGE, BN), :] for f in range(2)]

    for c in range(parts):
        for copy in copies[c]:
            copy.wait()
        for k in range(c * chunk, (c + 1) * chunk):
            inverse = inv[tile(0, k), :]
            for f in range(2):
                value = source[tile(f, k), :] + jnp.where(
                    rim, pltpu.roll(columns[f], BE - 1 - 2 * k, 1), 0.0)
                row = (first + f) * EDGE + k
                value = jnp.concatenate([
                    value[:8] + jnp.where(sub == 0, edge[pl.ds(row + EDGE_S, 1), :], 0.0),
                    value[8:BN - 8],
                    value[BN - 8:] + jnp.where(sub == 7, edge[pl.ds(row + EDGE_N, 1), :], 0.0),
                ], axis=0)
                if k:
                    value = value + m_up * sol_up[f]
                sol_up[f] = value * inverse
                s[tile(f, k), :] = sol_up[f]
            m_up = mix[tile(0, k), :] if k + 1 < LEV else None
    heat, salt = sol_up
    total = None
    for k in range(LEV - 1, -1, -1):
        if k + 1 < LEV:
            factor = mix[tile(0, k), :] * inv[tile(0, k), :]
            heat = s[tile(0, k), :] + factor * heat
            salt = s[tile(1, k), :] + factor * salt
            s[tile(0, k), :] = heat
            s[tile(1, k), :] = salt
        if group == 0:
            weight = forcing * 2.0 * (k + 1) / (LEV * (LEV + 1))
            density = (haline * weight) * salt - heat * (thermal * weight + (cabbeling * weight) * heat)
            total = density if total is None else total + density
        if k % out_chunk == 0:
            for f in range(2):
                outs.append(pltpu.make_async_copy(
                    s.at[pl.ds(f * CELLS + k * BN, out_chunk * BN)],
                    new.at[pl.ds((first + f) * CELLS + k * BN, out_chunk * BN)],
                    out_sems.at[k // out_chunk, f]))
                outs[-1].start()
    if group == 0:
        field = total
        force[...] = field
        outs.append(pltpu.make_async_copy(force, force_out, side_sems.at[4]))
        outs[-1].start()
        turned = jnp.concatenate([field, depth[...]], axis=0).T
        east_item, west_item = turned[BE - 3:, :], turned[:3, :]
        sends = (east_item, west_item, field[BN - 3:, :], field[:3, :],
                 east_item, west_item, east_item, west_item)
        for d, item in enumerate(sends):
            to = plan[NBR + d]

            @pl.when(to >= 0)
            def _(to=to, item=item):
                parts_out[to, pl.ds(0, 3), :] = item

        outs.append(pltpu.make_async_copy(parts_out, items, side_sems.at[5]))
        outs[-1].start()
    for copy in outs:
        copy.wait()


def solve(group, args, chunk=12, out_chunk=6):
    outs, out_specs = [pltpu.HBM((4 * CELLS, BE), F32)], [HBM]
    edge_rows = EDGE_D + 16
    block = lambda rows: pltpu.VMEM((rows, BE), F32)
    aliases = {}
    scratch = [cells(0, 2), cells(), cells(), block(edge_rows)]
    if group == 0:
        in_specs = [SM, VM, HBM, HBM, HBM, VM, HBM]
        outs += [pltpu.HBM((edge_rows, BE), F32), pltpu.HBM((BN, BE), F32),
                 pltpu.HBM((128, PART, BE), F32)]
        out_specs += [HBM] * 3
        scratch += [block(BE), pltpu.VMEM((128, PART, BE), F32), block(ITEM), block(BN), block(BN)]
    else:
        in_specs = [HBM] * 5
        aliases = {4: 0}
    scratch += [pltpu.SemaphoreType.DMA((LEV // chunk, 4)),
                pltpu.SemaphoreType.DMA((LEV // out_chunk, 2)), pltpu.SemaphoreType.DMA((6,))]
    return pl.pallas_call(
        functools.partial(solve_kernel, group, chunk, out_chunk),
        out_shape=tuple(outs),
        in_specs=in_specs,
        out_specs=tuple(out_specs),
        input_output_aliases=aliases,
        scratch_shapes=scratch,
        compiler_params=params(8),
        name=f"solve{group}",
    )(*args)


def chosen(shift, arrays, start, rows):
    value = arrays[-1][pl.ds(start, rows), :]
    for k in range(len(arrays) - 1):
        value = jnp.where(shift == k, arrays[k][pl.ds(start, rows), :], value)
    return value


TALL, WIDE = BN + 8, 2 * BE


def krylov_kernel(plan, field, depth, edge, got, vectors, sums, b_s, d_s, edge_d, sems):
    copies = [
        pltpu.make_async_copy(field, b_s.at[pl.ds(0, BN), pl.ds(0, BE)], sems.at[0]),
        pltpu.make_async_copy(depth, d_s.at[pl.ds(0, BN), pl.ds(0, BE)], sems.at[1]),
        pltpu.make_async_copy(edge.at[pl.ds(EDGE_D, 16)], edge_d, sems.at[2]),
    ]
    for copy in copies:
        copy.start()
    nothing = jnp.zeros((3, BE), F32)

    def item(d):
        to = plan[NBR + d]
        return jnp.where(to >= 0, got[jnp.maximum(to, 0), pl.ds(0, 3), :], nothing)

    for ref in (b_s, d_s):
        ref[pl.ds(BN, 8), :] = jnp.zeros((8, WIDE), F32)
    b_s[pl.ds(BN, 3), pl.ds(0, BE)] = item(2)
    b_s[pl.ds(TALL - 3, 3), pl.ds(0, BE)] = item(3)
    middle = jnp.zeros((BE - 6, BE), F32)
    sides = jnp.concatenate([item(0), middle, item(1)], axis=0).T
    b_s[pl.ds(0, BN), pl.ds(BE, BE)] = sides[:BN]
    d_s[pl.ds(0, BN), pl.ds(BE, BE)] = sides[BN:]
    place = lax.broadcasted_iota(jnp.int32, (3, BE), 1)
    place = jnp.where(place >= BN, place - BN, place)

    def corner(north, south):
        return jnp.where(place < 3, north, jnp.where(
            jnp.logical_and(place >= 5, place < 8), pltpu.roll(south, BE - BN + 8, 1), 0.0))

    corners = jnp.concatenate([corner(item(4), item(6)), middle, corner(item(5), item(7))], axis=0).T
    b_s[pl.ds(BN, 8), pl.ds(BE, BE)] = corners[:8]
    d_s[pl.ds(BN, 8), pl.ds(BE, BE)] = corners[BN:BN + 8]

    for copy in copies:
        copy.wait()
    d_s[pl.ds(BN, 3), pl.ds(0, BE)] = jnp.where(
        plan[NBR + 2] >= 0, edge_d[pl.ds(8, 3), :], 0.0)
    d_s[pl.ds(TALL - 3, 3), pl.ds(0, BE)] = jnp.where(
        plan[NBR + 3] >= 0, edge_d[pl.ds(4, 3), :], 0.0)
    d = d_s[...]
    east = lambda a: pltpu.roll(a, WIDE - 1, 1)
    west = lambda a: pltpu.roll(a, 1, 1)
    north = lambda a: pltpu.roll(a, TALL - 1, 0)
    south = lambda a: pltpu.roll(a, 1, 0)
    d_e, d_n = east(d), north(d)
    w_e = jnp.where(jnp.logical_and(d > 0, d_e > 0), 0.5 * (d + d_e), 0.0)
    w_n = jnp.where(jnp.logical_and(d > 0, d_n > 0), 0.5 * (d + d_n), 0.0)
    w_w, w_s = west(w_e), south(w_n)
    diagonal = area_term + w_e + w_w + w_n + w_s

    def operate(h):
        return diagonal * h - w_e * east(h) - w_w * west(h) - w_n * north(h) - w_s * south(h)

    v0 = b_s[...]
    v1 = operate(v0)
    v2 = operate(v1)
    v3 = operate(v2)
    v = [a[:BN, :BE] for a in (v0, v1, v2, v3)]
    for i in range(3):
        vectors[pl.ds(i * BN, BN), :] = v[i]
    pairs = ((0, 0), (0, 1), (1, 1), (1, 2), (2, 2), (2, 3))
    at = lax.broadcasted_iota(jnp.int32, (1, BE), 1)
    total = jnp.zeros((1, BE), F32)
    for i, (a, b) in enumerate(pairs):
        value = jnp.sum(jnp.sum(v[a] * v[b], axis=0, keepdims=True), axis=1, keepdims=True)
        total = jnp.where(at == i, value, total)
    for i in range(128):
        sums[i] = total


def krylov(plan, field, depth, edge, got):
    return pl.pallas_call(
        krylov_kernel,
        out_shape=(
            jax.ShapeDtypeStruct((3 * BN, BE), F32),
            jax.ShapeDtypeStruct((128, 1, BE), F32),
        ),
        in_specs=[SM] + [HBM] * 3 + [VM],
        out_specs=(VM, VM),
        scratch_shapes=[pltpu.VMEM((TALL, WIDE), F32)] * 2 + [
            pltpu.VMEM((16, BE), F32), pltpu.SemaphoreType.DMA((3,))],
        compiler_params=params(4),
        name="krylov",
    )(plan, field, depth, edge, got)


def combine_kernel(plan, sums, a0, a1, a2, a3, o0, o1, o2, o3):
    total = jnp.sum(sums[...], axis=0, keepdims=True)
    moment = [total[:, i:i + 1] for i in range(6)]

    def inner(a, b, lift):
        value = None
        for i in range(len(a)):
            for j in range(len(b)):
                term = a[i] * b[j] * moment[i + j + lift]
                value = term if value is None else value + term
        return value

    one = jnp.ones((1, 1), F32)
    zero = jnp.zeros((1, 1), F32)
    residual, direction = [one], [one]
    solution = [zero, zero, zero]
    rr = moment[0]
    for step in range(3):
        alpha = rr / inner(direction, direction, 1)
        for i, c in enumerate(direction):
            solution[i] = solution[i] + alpha * c
        if step < 2:
            image = [zero] + direction
            padded = residual + [zero]
            residual = [r - alpha * c for r, c in zip(padded, image)]
            following = inner(residual, residual, 0)
            beta = following / rr
            direction = [r + beta * c for r, c in zip(residual, direction + [zero])]
            rr = following
    solved = []
    for a in (a0, a1, a2, a3):
        v = [a[pl.ds(i * BN, BN), :] for i in range(3)]
        solved.append(solution[0] * v[0] + solution[1] * v[1] + solution[2] * v[2])
    for k, out in enumerate((o0, o1, o2, o3)):
        for b in range(2):
            shift = plan[TSEND + 2 * k + b]
            value = solved[3]
            for j in range(3):
                value = jnp.where(shift == j, solved[j], value)
            out[pl.ds(b * BN, BN), :] = value


def combine(plan, sums, arrays):
    return pl.pallas_call(
        combine_kernel,
        out_shape=(jax.ShapeDtypeStruct((2 * BN, BE), F32),) * 4,
        in_specs=[SM] + [VM] * 5,
        out_specs=(VM,) * 4,
        compiler_params=params(4),
        name="combine",
    )(plan, sums, *arrays)


def place_kernel(plan, a0, a1, a2, a3, out):
    for b in range(2):
        shift = plan[TFROM + b]
        value = chosen(shift, (a0, a1, a2, a3), b * BN, BN)
        out[b] = jnp.where(shift >= 0, value, 0.0)


def place(plan, arrays):
    return pl.pallas_call(
        place_kernel,
        out_shape=jax.ShapeDtypeStruct((2, BN, BE), F32),
        in_specs=[SM] + [VM] * 4,
        out_specs=VM,
        compiler_params=params(4),
        name="place",
    )(plan, *arrays)


def body(tracers, velocity, mixing_rate, column_depth, ocean_mask, clinic_list, tropic_list):
    n_gx, n_gy = lax.axis_size("gx"), lax.axis_size("gy")
    side = 4
    depth = column_depth.reshape(BN, BE)
    every = lambda value: lax.all_to_all(value, ("gx", "gy"), 0, 0)

    def along_y(value, k):
        return lax.ppermute(value, "gx", [
            (z * side + y, z * side + (y + k) % side) for z in range(side) for y in range(side)])

    def along_z(value, k):
        return lax.ppermute(value, "gx", [
            (z * side + y, (z + k) % side * side + y) for z in range(side) for y in range(side)])

    in_hbm = lambda value: pltpu.with_memory_space_constraint(value, pltpu.HBM)
    tracers = in_hbm(tracers.reshape(4 * CELLS, BE))
    velocity = in_hbm(velocity.reshape(2 * CELLS, BE))
    mixing = in_hbm(mixing_rate.reshape((LEV - 1) * BN, BE))
    depth = in_hbm(depth)
    own = pack(tracers, velocity, depth)
    plan = pl.pallas_call(
        functools.partial(plan_kernel, side, n_gy, n_gx),
        out_shape=jax.ShapeDtypeStruct((PLAN,), jnp.int32),
        in_specs=[SM, SM],
        out_specs=SM,
        scratch_shapes=[pltpu.SMEM(((n_gy + 2) * WRAP,), jnp.int32)],
        compiler_params=params(1),
        name="plan",
    )(clinic_list, tropic_list)
    in_vmem = lambda value: pltpu.with_memory_space_constraint(value, pltpu.VMEM)
    (last_two,) = stencil(1, (tracers, velocity))
    first_two, inv = stencil(0, (tracers, velocity, mixing))
    first_two, inv = in_vmem(first_two), in_hbm(inv)
    scattered = every(own.reshape(128, PART, BE))
    scattered, last_two = lax.optimization_barrier((scattered, last_two))
    halo = every(select(plan, scattered)).reshape(ITEM, BE)
    new, edge, field, items = solve(0, (plan, first_two, inv, mixing, in_hbm(own), halo, depth))
    got = every(items)
    edge, field = in_hbm(edge), in_hbm(field)
    (new,) = solve(1, (in_hbm(last_two), inv, mixing, edge, new))
    got, new = lax.optimization_barrier((got, new))
    vectors, sums = krylov(plan, field, depth, edge, got)
    totals = every(sums)
    line = [vectors] + [along_y(vectors, k) for k in range(1, side)]
    sends = combine(plan, totals.reshape(128, BE), line)
    arrived = [sends[0]] + [along_z(sends[k], k) for k in range(1, side)]
    height = place(plan, arrived)
    return new.reshape(1, 1, 4, LEV, BN, BE), height[None]


def solution(mesh):
    return jax.shard_map(
        body,
        mesh=mesh,
        in_specs=(
            P("gy", "gx", None, None, None, None),
            P("gy", "gx", None, None, None, None),
            P("gy", "gx", None, None, None),
            P("gy", "gx", None, None),
            P(),
            P(),
            P(),
        ),
        out_specs=(P("gy", "gx", None, None, None, None), P("gy", "gx", None, None)),
        check_vma=False,
    )
```

time: 151 us -> 96.7 us (0.64)
  local copies, waits for them, and re-layouts: 27.6 us -> 0.01 us
  Pallas kernels: 48.5 us -> 33.1 us
  starting transfers between devices: 44.6 us -> 29.6 us
  waiting for transfers between devices: 11.6 us -> 16.7 us
    unnamed x82 -> x4, local copies, waits for them, and re-layouts: 25.6 us -> 0.01 us
    all_to_all x1 -> x3, starting transfers between devices: 7.03 us -> 22.9 us  [body(): every = lambda value: lax.all_to_all(value, ('gx', 'gy'), 0, 0)]
    pallas_call x6, Pallas kernels: 42.8 us -> 27.1 us  [the longest x2 11.3 us: stencil(): pl.pallas_call(functools.partial(stencil_kernel, group, chunk), out_shape...]
    ppermute x9 -> x3, starting transfers between devices: 14.7 us -> 2.67 us  [along_y(): lax.ppermute(value, 'gx', [(z * side + y, z * side + (y + k) % side) for...]
    all_to_all x1 -> x3, waiting for transfers between devices: 2.55 us -> 13.7 us  [body(): every = lambda value: lax.all_to_all(value, ('gx', 'gy'), 0, 0)]
    ppermute x9 -> x3, starting transfers between devices: 14.3 us -> 4.06 us  [along_z(): lax.ppermute(value, 'gx', [(z * side + y, (z + k) % side * side + y) for...]
    ppermute x4 -> x0, starting transfers between devices: 8.5 us -> none  [the longest x2 5.93 us: route(): below = lax.ppermute(north, 'gy', [(i, i + 1) for i in range(n_gy - 1)])]
    ppermute x4 -> x0, waiting for transfers between devices: 2.99 us -> none  [the longest x2 2.98 us: route(): above = lax.ppermute(south, 'gy', [(i, i - 1) for i in range(1, n_gy)])]
  transfers between devices with their start and end apart: 23 -> 9, of which waited for: 4 -> 6; matrix products, arithmetic and copies ran while one was open for 3% -> 0% of each run, Pallas kernels for 18% -> 19%
where the time goes in v2:
time: 96.7 us; the launch traced here: 96.3 us
  Pallas kernels  33.1 us (34%)
  starting transfers between devices  29.6 us (31%)
  waiting for transfers between devices  16.7 us (17%)
  blocking collectives  16.1 us (17%)
    all_to_all x3, starting transfers between devices, body(): every = lambda value: lax.all_to_all(value, ('gx', 'gy'), 0, 0)  22.9 us
    all_to_all x1, blocking collectives, body(): every = lambda value: lax.all_to_all(value, ('gx', 'gy'), 0, 0)  16.1 us
    all_to_all x3, waiting for transfers between devices, body(): every = lambda value: lax.all_to_all(value, ('gx', 'gy'), 0, 0)  13.7 us
    pallas_call x2, Pallas kernels, stencil(): pl.pallas_call(functools.partial(stencil_kernel, group, chunk), out_shape...  11.3 us
    pallas_call x2, Pallas kernels, solve(): pl.pallas_call(functools.partial(solve_kernel, group, chunk, out_chunk),...  10.1 us
    pallas_call x1, Pallas kernels, pack(): pl.pallas_call(pack_kernel, out_shape=pltpu.HBM((ITEM, BE), F32), in_spec...  4.29 us
    ppermute x3, starting transfers between devices, along_z(): lax.ppermute(value, 'gx', [(z * side + y, (z + k) % side * side + y) for...  4.06 us
    ppermute x3, waiting for transfers between devices, along_z(): lax.ppermute(value, 'gx', [(z * side + y, (z + k) % side * side + y) for...  3.05 us
  transfers between devices with their start and end apart: 9, of which 6 were waited for; matrix products, arithmetic and copies ran while one was open for 0% of the time, Pallas kernels for 19%

profile of v2, /device:TPU:0, one launch (start us, length us, event | category | flops | bytes accessed | tf_op | source)
XLA Modules:
  0.0 96.3 jit_solution(5978451718523680098)
XLA Ops:
  0.6 4.3 %pack.1.refs_4_ = f32[512,128]{1,0:T(8,128)} custom-call(f32[9216,128]{1,0:T(8,128)} %bitcast.11, f32[4608,128]{1,0:T(8,128)} %bitcast.14, f32[64,128]{1,0:T(8,128)} %bitcast.22), custom_call_target="tpu_custom_call" | custom-call | tf_op jit(solution)/shard_map/pack/pallas_call | solution.py:151
  4.9 11.1 %all-to-all-start = ((f32[128,4,128]{2,1,0:T(4,128)}), f32[128,4,128]{2,1,0:T(4,128)S(1)}, u32[]{:S(2)}, u32[]{:S(2)}) async-start(f32[128,4,128]{2,1,0:T(4,128)} %bitcast.21), calls=%async_computation | async-start | bytes 524288 | tf_op jit(solution)/shard_map/all_to_all | solution.py:668
  16.1 0.0 copy-start
  16.1 0.0 copy-start.1
  16.1 5.7 %stencil1.1.refs_0_ = f32[4608,128]{1,0:T(8,128)} custom-call(f32[9216,128]{1,0:T(8,128)} %bitcast.12, f32[4608,128]{1,0:T(8,128)} %bitcast.15), custom_call_target="tpu_custom_call" | custom-call | tf_op jit(solution)/shard_map/stencil1/pallas_call | solution.py:312
  21.8 0.0 copy-done
  21.8 2.1 %plan.1.refs_0_ = s32[146]{0:T(256)S(1)} custom-call(s32[8,16]{1,0:T(8,128)S(1)} %copy-done, s32[8,32]{1,0:T(8,128)S(1)} %copy-done.1), custom_call_target="tpu_custom_call" | custom-call | tf_op jit(solution)/shard_map/plan/pallas_call | solution.py:684
  24.0 2.8 %all-to-all-done.got = f32[128,4,128]{2,1,0:T(4,128)S(1)} async-done(((f32[128,4,128]{2,1,0:T(4,128)}), f32[128,4,128]{2,1,0:T(4,128)S(1)}, u32[]{:S(2)}, u32[]{:S(2)}) %all-to-all-start) | async-done | bytes 262176 | tf_op jit(solution)/shard_map/all_to_all | solution.py:668
  26.8 1.5 %select.1 = f32[128,4,128]{2,1,0:T(4,128)} custom-call(s32[146]{0:T(256)S(1)} %plan.1.refs_0_, f32[128,4,128]{2,1,0:T(4,128)S(1)} %all-to-all-done.got), custom_call_target="tpu_custom_call" | custom-call | tf_op jit(solution)/shard_map/select/pallas_call | solution.py:179
  28.3 6.9 %all-to-all-start.1 = ((f32[128,4,128]{2,1,0:T(4,128)}), f32[128,4,128]{2,1,0:T(4,128)S(1)}, u32[]{:S(2)}, u32[]{:S(2)}) async-start(f32[128,4,128]{2,1,0:T(4,128)} %select.1), calls=%async_computation.1 | async-start | bytes 524288 | tf_op jit(solution)/shard_map/all_to_all | solution.py:668
  35.2 5.6 %stencil0.1 = (f32[4608,128]{1,0:T(8,128)S(1)}, f32[2304,128]{1,0:T(8,128)}) custom-call(f32[9216,128]{1,0:T(8,128)} %bitcast.13, f32[4608,128]{1,0:T(8,128)} %bitcast.16, f32[2240,128]{1,0:T(8,128)} %bitcast.17), custom_call_target="tpu_custom_call" | custom-call | tf_op jit(solution)/shard_map/stencil0/pallas_call | solution.py:312
  40.9 5.1 %all-to-all-done.1 = f32[128,4,128]{2,1,0:T(4,128)S(1)} async-done(((f32[128,4,128]{2,1,0:T(4,128)}), f32[128,4,128]{2,1,0:T(4,128)S(1)}, u32[]{:S(2)}, u32[]{:S(2)}) %all-to-all-start.1) | async-done | bytes 262176 | tf_op jit(solution)/shard_map/all_to_all | solution.py:668
  46.0 5.1 %solve0.1 = (f32[9216,128]{1,0:T(8,128)}, f32[592,128]{1,0:T(8,128)}, f32[64,128]{1,0:T(8,128)}, f32[128,4,128]{2,1,0:T(4,128)}) custom-call(s32[146]{0:T(256)S(1)} %plan.1.refs_0_, f32[4608,128]{1,0:T(8,128)S(1)} %get-tuple-element.18.refs_1_, f32[2304,128]{1,0:T(8,128)} %get-tuple-element.19.refs_2_.refs_1_, f32[2240,128]{1,0:T(8,128)} %bitcast.18, ...), custom_call_target="tpu_custom_call" | custom-call | tf_op jit(solution)/shard_map/solve0/pallas_call | solution.py:485
  51.1 4.8 %all-to-all-start.2 = ((f32[128,4,128]{2,1,0:T(4,128)}), f32[128,4,128]{2,1,0:T(4,128)S(1)}, u32[]{:S(2)}, u32[]{:S(2)}) async-start(f32[128,4,128]{2,1,0:T(4,128)} %get-tuple-element.21), calls=%async_computation.2 | async-start | bytes 524288 | tf_op jit(solution)/shard_map/all_to_all | solution.py:668
  55.9 4.9 %solve1.1 = f32[9216,128]{1,0:T(8,128)} custom-call(f32[4608,128]{1,0:T(8,128)} %stencil1.1.refs_0_, f32[2304,128]{1,0:T(8,128)} %get-tuple-element.19.refs_2_.refs_1_, f32[2240,128]{1,0:T(8,128)} %bitcast.19, f32[592,128]{1,0:T(8,128)} %get-tuple-element.23.refs_3_.edge, f32[9216,128]{1,0:T(8,128)} %get-tuple-element.24.refs_4_), custom_call_target="tpu_custom_call", output_to_operand_aliasing={{}: (4, {})} | custom-call | tf_op jit(solution)/shard_map/solve1/pallas_call | solution.py:485
  60.8 5.8 %all-to-all-done.2.got = f32[128,4,128]{2,1,0:T(4,128)S(1)} async-done(((f32[128,4,128]{2,1,0:T(4,128)}), f32[128,4,128]{2,1,0:T(4,128)S(1)}, u32[]{:S(2)}, u32[]{:S(2)}) %all-to-all-start.2) | async-done | bytes 262176 | tf_op jit(solution)/shard_map/all_to_all | solution.py:668
  66.6 1.8 %krylov.1 = (f32[192,128]{1,0:T(8,128)S(1)}, f32[128,1,128]{2,1,0:T(1,128)S(1)}) custom-call(s32[146]{0:T(256)S(1)} %plan.1.refs_0_, f32[64,128]{1,0:T(8,128)} %get-tuple-element.26.field, f32[64,128]{1,0:T(8,128)} %bitcast.24, f32[592,128]{1,0:T(8,128)} %get-tuple-element.23.refs_3_.edge, f32[128,4,128]{2,1,0:T(4,128)S(1)} %all-to-all-done.2.got), custom_call_target="tpu_custom_call" | custom-call | tf_op jit(solution)/shard_map/krylov/pallas_call | solution.py:578
  68.4 1.0 collective-permute-start.2
  69.4 1.5 %collective-permute-start.1 = (f32[192,128]{1,0:T(8,128)S(1)}, f32[192,128]{1,0:T(8,128)S(1)}, u32[]{:S(2)}, u32[]{:S(2)}) collective-permute-start(f32[192,128]{1,0:T(8,128)S(1)} %get-tuple-element.29.a0), channel_id=1, source_target_pairs={{0,16},{8,24},{16,0},{24,8},{32,48},{40,56},{48,32},{56,40},{64,80... | collective-permute-start | bytes 294920 | tf_op jit(solution)/shard_map/ppermute | solution.py:671
  70.9 0.2 collective-permute-start
  71.1 16.1 %all_to_all.20 = f32[128,1,128]{2,1,0:T(1,128)S(1)} all-to-all(f32[128,1,128]{2,1,0:T(1,128)S(1)} %get-tuple-element.28), channel_id=1, replica_groups=mesh['gx'=16,'gy'=8] {'gx','gy'}, dimensions={0} | all-to-all | bytes 131072 | tf_op jit(solution)/shard_map/all_to_all | solution.py:668
  87.2 0.0 collective-permute-done.2.a3
  87.2 0.0 collective-permute-done.1.a2
  87.2 0.0 collective-permute-done.a1
  87.2 0.8 combine.1
  88.0 0.9 collective-permute-start.3
  88.9 1.5 %collective-permute-start.4 = (f32[128,128]{1,0:T(8,128)S(1)}, f32[128,128]{1,0:T(8,128)S(1)}, u32[]{:S(2)}, u32[]{:S(2)}) collective-permute-start(f32[128,128]{1,0:T(8,128)S(1)} %get-tuple-element.32), channel_id=1, source_target_pairs={{0,64},{8,72},{16,80},{24,88},{32,96},{40,104},{48,112},{56,120},{... | collective-permute-start | bytes 196616 | tf_op jit(solution)/shard_map/ppermute | solution.py:675
  90.4 1.7 %collective-permute-start.5 = (f32[128,128]{1,0:T(8,128)S(1)}, f32[128,128]{1,0:T(8,128)S(1)}, u32[]{:S(2)}, u32[]{:S(2)}) collective-permute-start(f32[128,128]{1,0:T(8,128)S(1)} %get-tuple-element.33), channel_id=1, source_target_pairs={{0,96},{8,104},{16,112},{24,120},{32,0},{40,8},{48,16},{56,24},{64... | collective-permute-start | bytes 196616 | tf_op jit(solution)/shard_map/ppermute | solution.py:675
  92.1 1.8 %collective-permute-done.3.a1 = f32[128,128]{1,0:T(8,128)S(1)} collective-permute-done((f32[128,128]{1,0:T(8,128)S(1)}, f32[128,128]{1,0:T(8,128)S(1)}, u32[]{:S(2)}, u32[]{:S(2)}) %collective-permute-start.3) | collective-permute-done | bytes 65568 | tf_op jit(solution)/shard_map/ppermute | solution.py:675
  93.9 0.7 collective-permute-done.4.a2
  94.7 0.5 collective-permute-done.5.a3
  95.1 1.2 %place.1 = f32[2,64,128]{2,1,0:T(8,128)} custom-call(s32[146]{0:T(256)S(1)} %plan.1.refs_0_, f32[128,128]{1,0:T(8,128)S(1)} %get-tuple-element.30.a0, f32[128,128]{1,0:T(8,128)S(1)} %collective-permute-done.3.a1, f32[128,128]{1,0:T(8,128)S(1)} %collective-permute-done.4.a2, f32[128,128]{1,0:T(8,128)S(1)} %collective-permute-done.5.a3), custom_call_target="tpu_custom_call" | custom-call | tf_op jit(solution)/shard_map/place/pallas_call | solution.py:654
  (1 shorter events, 0.0 us)
Async XLA Ops:
  4.9 21.9 %all-to-all-start = ((f32[128,4,128]{2,1,0:T(4,128)}), f32[128,4,128]{2,1,0:T(4,128)S(1)}, u32[]{:S(2)}, u32[]{:S(2)}) async-start(f32[128,4,128]{2,1,0:T(4,128)} %bitcast.21), calls=%async_computation | async-start | bytes 524288 | tf_op jit(solution)/shard_map/all_to_all | solution.py:668
  16.1 5.7 %copy-start = (s32[8,16]{1,0:T(8,128)S(1)}, s32[8,16]{1,0:T(8,128)}, u32[]{:S(2)}) copy-start(s32[8,16]{1,0:T(8,128)} %clinic.1) | copy-start | bytes 1540
  16.1 5.7 %copy-start.1 = (s32[8,32]{1,0:T(8,128)S(1)}, s32[8,32]{1,0:T(8,128)}, u32[]{:S(2)}) copy-start(s32[8,32]{1,0:T(8,128)} %tropic.1) | copy-start | bytes 3076
  28.3 17.7 %all-to-all-start.1 = ((f32[128,4,128]{2,1,0:T(4,128)}), f32[128,4,128]{2,1,0:T(4,128)S(1)}, u32[]{:S(2)}, u32[]{:S(2)}) async-start(f32[128,4,128]{2,1,0:T(4,128)} %select.1), calls=%async_computation.1 | async-start | bytes 524288 | tf_op jit(solution)/shard_map/all_to_all | solution.py:668
  51.1 15.5 %all-to-all-start.2 = ((f32[128,4,128]{2,1,0:T(4,128)}), f32[128,4,128]{2,1,0:T(4,128)S(1)}, u32[]{:S(2)}, u32[]{:S(2)}) async-start(f32[128,4,128]{2,1,0:T(4,128)} %get-tuple-element.21), calls=%async_computation.2 | async-start | bytes 524288 | tf_op jit(solution)/shard_map/all_to_all | solution.py:668
  68.4 18.8 %collective-permute-start.2 = (f32[192,128]{1,0:T(8,128)S(1)}, f32[192,128]{1,0:T(8,128)S(1)}, u32[]{:S(2)}, u32[]{:S(2)}) collective-permute-start(f32[192,128]{1,0:T(8,128)S(1)} %get-tuple-element.29.a0), channel_id=1, source_target_pairs={{0,24},{8,0},{16,8},{24,16},{32,56},{40,32},{48,40},{56,48},{64,88... | collective-permute-start | bytes 294920 | tf_op jit(solution)/shard_map/ppermute | solution.py:671
  69.4 17.8 %collective-permute-start.1 = (f32[192,128]{1,0:T(8,128)S(1)}, f32[192,128]{1,0:T(8,128)S(1)}, u32[]{:S(2)}, u32[]{:S(2)}) collective-permute-start(f32[192,128]{1,0:T(8,128)S(1)} %get-tuple-element.29.a0), channel_id=1, source_target_pairs={{0,16},{8,24},{16,0},{24,8},{32,48},{40,56},{48,32},{56,40},{64,80... | collective-permute-start | bytes 294920 | tf_op jit(solution)/shard_map/ppermute | solution.py:671
  70.9 16.3 %collective-permute-start = (f32[192,128]{1,0:T(8,128)S(1)}, f32[192,128]{1,0:T(8,128)S(1)}, u32[]{:S(2)}, u32[]{:S(2)}) collective-permute-start(f32[192,128]{1,0:T(8,128)S(1)} %get-tuple-element.29.a0), channel_id=1, source_target_pairs={{0,8},{8,16},{16,24},{24,0},{32,40},{40,48},{48,56},{56,32},{64,72... | collective-permute-start | bytes 294920 | tf_op jit(solution)/shard_map/ppermute | solution.py:671
  88.0 5.9 %collective-permute-start.3 = (f32[128,128]{1,0:T(8,128)S(1)}, f32[128,128]{1,0:T(8,128)S(1)}, u32[]{:S(2)}, u32[]{:S(2)}) collective-permute-start(f32[128,128]{1,0:T(8,128)S(1)} %get-tuple-element.31), channel_id=1, source_target_pairs={{0,32},{8,40},{16,48},{24,56},{32,64},{40,72},{48,80},{56,88},{64,... | collective-permute-start | bytes 196616 | tf_op jit(solution)/shard_map/ppermute | solution.py:675
  88.9 5.8 %collective-permute-start.4 = (f32[128,128]{1,0:T(8,128)S(1)}, f32[128,128]{1,0:T(8,128)S(1)}, u32[]{:S(2)}, u32[]{:S(2)}) collective-permute-start(f32[128,128]{1,0:T(8,128)S(1)} %get-tuple-element.32), channel_id=1, source_target_pairs={{0,64},{8,72},{16,80},{24,88},{32,96},{40,104},{48,112},{56,120},{... | collective-permute-start | bytes 196616 | tf_op jit(solution)/shard_map/ppermute | solution.py:675
  90.4 4.7 %collective-permute-start.5 = (f32[128,128]{1,0:T(8,128)S(1)}, f32[128,128]{1,0:T(8,128)S(1)}, u32[]{:S(2)}, u32[]{:S(2)}) collective-permute-start(f32[128,128]{1,0:T(8,128)S(1)} %get-tuple-element.33), channel_id=1, source_target_pairs={{0,96},{8,104},{16,112},{24,120},{32,0},{40,8},{48,16},{56,24},{64... | collective-permute-start | bytes 196616 | tf_op jit(solution)/shard_map/ppermute | solution.py:675

commit v3 on v2

--- a/solution.py
+++ b/solution.py
@@ -9,6 +9,7 @@
 F32 = jnp.float32
 LEV, BN, BE = 36, 64, 128
 NBX = 28
+N_GX, N_GY, SIDE = 16, 8, 4
 CELLS = LEV * BN
 HALF = BE // 2
 
@@ -55,7 +56,7 @@
     return jax.ShapeDtypeStruct(shape, F32)
 
 
-def plan_kernel(side, n_gy, slots, clinic, tropic, out, pos):
+def make_plan(side, n_gy, slots, clinic, tropic, out, pos):
     gx = lax.axis_index("gx")
     gy = lax.axis_index("gy")
     z = gx // side
@@ -219,21 +220,19 @@
     at = pl.multiple_of(k * BN, BN)
     here, north, south = pl.ds(at + 8, BN), pl.ds(at + 9, BN), pl.ds(at + 7, BN)
     half_u = 0.5 * u[pl.ds(at, BN), :]
-    half_w = pltpu.roll(half_u, 1, 1)
     ua = jnp.where(lane == BE - 1, 0.0, half_u + diffusion)
     ub = jnp.where(lane == BE - 1, 0.0, half_u - diffusion)
-    uaw = jnp.where(lane == 0, 0.0, half_w + diffusion)
-    ubw = jnp.where(lane == 0, 0.0, half_w - diffusion)
     half_v, half_s = 0.5 * v[here, :], 0.5 * v[south, :]
     va = jnp.where(row_id == BN - 1, 0.0, half_v + diffusion)
     vb = jnp.where(row_id == BN - 1, 0.0, half_v - diffusion)
     vas = jnp.where(row_id == 0, 0.0, half_s + diffusion)
     vbs = jnp.where(row_id == 0, 0.0, half_s - diffusion)
-    centre = 1.0 - (ua - ubw) - (va - vbs)
+    centre = 1.0 - (va - vbs)
     for f in range(2):
         tile = q[f][here, :]
+        fe = ua * tile + ub * pltpu.roll(tile, BE - 1, 1)
         s[pl.ds(pl.multiple_of(f * CELLS + at, BN), BN), :] = (
-            centre * tile - ub * pltpu.roll(tile, BE - 1, 1) + uaw * pltpu.roll(tile, 1, 1)
+            centre * tile - (fe - pltpu.roll(fe, 1, 1))
             - vb * q[f][north, :] + vas * q[f][south, :])
 
 
@@ -258,8 +257,10 @@
     if group == 0:
         tracers, velocity, mixing, s, inv_out, q0, q1, u, v, inv, mix, sems, out_sems = refs
     else:
-        tracers, velocity, stirred, q0, q1, u, v, s, sems, out_sems = refs
+        tracers, velocity, _aliased, s, new, q0, q1, u, v, sems, out_sems = refs
         mixing = mix = None
+        leave = pltpu.make_async_copy(s, new.at[pl.ds(0, 2 * CELLS)], out_sems.at[0, 0])
+        leave.start()
     q = (q0, q1)
     copies = stencil_loads((2 * group, 2 * group + 1), chunk, tracers, velocity, mixing, q, u, v, mix, sems)
     for c in range(AHEAD):
@@ -267,6 +268,8 @@
     zero = jnp.zeros((BN, BE), F32)
     if group == 0:
         mix[pl.ds(CELLS - BN, BN), :] = zero
+    else:
+        leave.wait()
 
     def level(k, carry):
         stencil_level(k, q, u, v, s)
@@ -288,11 +291,6 @@
             span = pl.ds(c * rows, rows)
             outs.append(pltpu.make_async_copy(inv.at[span], inv_out.at[span], out_sems.at[c, 0]))
             outs[-1].start()
-        else:
-            for f in range(2):
-                span = pl.ds(f * CELLS + c * rows, rows)
-                outs.append(pltpu.make_async_copy(s.at[span], stirred.at[span], out_sems.at[c, f]))
-                outs[-1].start()
     for copy in outs:
         copy.wait()
 
@@ -307,13 +305,14 @@
         outs, out_specs = (cells(0, 2), pltpu.HBM((CELLS, BE), F32)), (VM, HBM)
         more = [cells(), cells()]
     else:
-        outs, out_specs = (pltpu.HBM((2 * CELLS, BE), F32),), (HBM,)
-        more = [cells(0, 2)]
+        outs, out_specs = (cells(0, 2), pltpu.HBM((4 * CELLS, BE), F32)), (VM, HBM)
+        more = []
     return pl.pallas_call(
         functools.partial(stencil_kernel, group, chunk),
         out_shape=outs,
-        in_specs=[HBM] * len(args),
+        in_specs=[HBM] * 3 if group == 0 else [HBM, HBM, VM],
         out_specs=out_specs,
+        input_output_aliases={} if group == 0 else {2: 0},
         scratch_shapes=[
             cells(16), cells(16), cells(), cells(16), *more,
             pltpu.SemaphoreType.DMA((parts, 5)),
@@ -363,15 +362,14 @@
     rows = chunk * BN
     outs = []
     if group == 0:
-        (plan, source, inv_in, mixing, own_in, halo, depth_in,
-         new, edge_out, force_out, items, s, inv, mix, edge, turn, parts_out, own, depth, force,
-         sems, out_sems, side_sems) = refs
+        (plan, _aliased, inv_in, mixing, own_in, halo, depth_in,
+         s, edge_out, force_out, items, inv, mix, edge, turn, parts_out, own, depth, force,
+         sems, side_sems) = refs
         sides = [pltpu.make_async_copy(a, b, side_sems.at[i]) for i, (a, b) in enumerate(
             ((own_in, own), (depth_in, depth)))]
     else:
-        (stirred, inv_in, mixing, edge_in, _aliased,
-         new, s, inv, mix, edge, sems, out_sems, side_sems) = refs
-        source = s
+        (_stirred, inv_in, mixing, edge_in, _new,
+         s, new, inv, mix, edge, sems, out_sems, side_sems) = refs
         sides = [pltpu.make_async_copy(edge_in, edge, side_sems.at[0])]
     for copy in sides:
         copy.start()
@@ -379,10 +377,6 @@
     copies = []
     for c in range(parts):
         row = []
-        if group == 1:
-            for f in range(2):
-                span = pl.ds(f * CELLS + c * rows, rows)
-                row.append(pltpu.make_async_copy(stirred.at[span], s.at[span], sems.at[c, f]))
         span = pl.ds(c * rows, rows)
         row.append(pltpu.make_async_copy(inv_in.at[span], inv.at[span], sems.at[c, 2]))
         span = pl.ds(c * rows, rows if c + 1 < parts else rows - BN)
@@ -410,7 +404,7 @@
         for k in range(c * chunk, (c + 1) * chunk):
             inverse = inv[tile(0, k), :]
             for f in range(2):
-                value = source[tile(f, k), :] + jnp.where(
+                value = s[tile(f, k), :] + jnp.where(
                     rim, pltpu.roll(columns[f], BE - 1 - 2 * k, 1), 0.0)
                 row = (first + f) * EDGE + k
                 value = jnp.concatenate([
@@ -436,7 +430,7 @@
             weight = forcing * 2.0 * (k + 1) / (LEV * (LEV + 1))
             density = (haline * weight) * salt - heat * (thermal * weight + (cabbeling * weight) * heat)
             total = density if total is None else total + density
-        if k % out_chunk == 0:
+        if group == 1 and k % out_chunk == 0:
             for f in range(2):
                 outs.append(pltpu.make_async_copy(
                     s.at[pl.ds(f * CELLS + k * BN, out_chunk * BN)],
@@ -466,29 +460,30 @@
 
 
 def solve(group, args, chunk=12, out_chunk=6):
-    outs, out_specs = [pltpu.HBM((4 * CELLS, BE), F32)], [HBM]
     edge_rows = EDGE_D + 16
     block = lambda rows: pltpu.VMEM((rows, BE), F32)
-    aliases = {}
-    scratch = [cells(0, 2), cells(), cells(), block(edge_rows)]
     if group == 0:
         in_specs = [SM, VM, HBM, HBM, HBM, VM, HBM]
-        outs += [pltpu.HBM((edge_rows, BE), F32), pltpu.HBM((BN, BE), F32),
-                 pltpu.HBM((128, PART, BE), F32)]
-        out_specs += [HBM] * 3
-        scratch += [block(BE), pltpu.VMEM((128, PART, BE), F32), block(ITEM), block(BN), block(BN)]
+        outs = [cells(0, 2), pltpu.HBM((edge_rows, BE), F32), pltpu.HBM((BN, BE), F32),
+                pltpu.HBM((128, PART, BE), F32)]
+        out_specs = [VM] + [HBM] * 3
+        scratch = [cells(), cells(), block(edge_rows), block(BE), pltpu.VMEM((128, PART, BE), F32),
+                   block(ITEM), block(BN), block(BN)]
     else:
-        in_specs = [HBM] * 5
-        aliases = {4: 0}
-    scratch += [pltpu.SemaphoreType.DMA((LEV // chunk, 4)),
-                pltpu.SemaphoreType.DMA((LEV // out_chunk, 2)), pltpu.SemaphoreType.DMA((6,))]
+        in_specs = [VM] + [HBM] * 4
+        outs, out_specs = [cells(0, 2), pltpu.HBM((4 * CELLS, BE), F32)], [VM, HBM]
+        scratch = [cells(), cells(), block(edge_rows)]
+    scratch += [pltpu.SemaphoreType.DMA((LEV // chunk, 4))]
+    if group == 1:
+        scratch += [pltpu.SemaphoreType.DMA((LEV // out_chunk, 2))]
+    scratch += [pltpu.SemaphoreType.DMA((6,))]
     return pl.pallas_call(
         functools.partial(solve_kernel, group, chunk, out_chunk),
         out_shape=tuple(outs),
         in_specs=in_specs,
         out_specs=tuple(out_specs),
-        input_output_aliases=aliases,
         scratch_shapes=scratch,
+        input_output_aliases={1: 0} if group == 0 else {0: 0, 4: 1},
         compiler_params=params(8),
         name=f"solve{group}",
     )(*args)
@@ -662,8 +657,7 @@
 
 
 def body(tracers, velocity, mixing_rate, column_depth, ocean_mask, clinic_list, tropic_list):
-    n_gx, n_gy = lax.axis_size("gx"), lax.axis_size("gy")
-    side = 4
+    side = SIDE
     depth = column_depth.reshape(BN, BE)
     every = lambda value: lax.all_to_all(value, ("gx", "gy"), 0, 0)
 
@@ -681,29 +675,29 @@
     mixing = in_hbm(mixing_rate.reshape((LEV - 1) * BN, BE))
     depth = in_hbm(depth)
     own = pack(tracers, velocity, depth)
+    in_vmem = lambda value: pltpu.with_memory_space_constraint(value, pltpu.VMEM)
     plan = pl.pallas_call(
-        functools.partial(plan_kernel, side, n_gy, n_gx),
+        functools.partial(make_plan, SIDE, N_GY, N_GX),
         out_shape=jax.ShapeDtypeStruct((PLAN,), jnp.int32),
         in_specs=[SM, SM],
         out_specs=SM,
-        scratch_shapes=[pltpu.SMEM(((n_gy + 2) * WRAP,), jnp.int32)],
+        scratch_shapes=[pltpu.SMEM(((N_GY + 2) * WRAP,), jnp.int32)],
         compiler_params=params(1),
         name="plan",
     )(clinic_list, tropic_list)
-    in_vmem = lambda value: pltpu.with_memory_space_constraint(value, pltpu.VMEM)
-    (last_two,) = stencil(1, (tracers, velocity))
     first_two, inv = stencil(0, (tracers, velocity, mixing))
     first_two, inv = in_vmem(first_two), in_hbm(inv)
     scattered = every(own.reshape(128, PART, BE))
-    scattered, last_two = lax.optimization_barrier((scattered, last_two))
     halo = every(select(plan, scattered)).reshape(ITEM, BE)
-    new, edge, field, items = solve(0, (plan, first_two, inv, mixing, in_hbm(own), halo, depth))
+    mixed, edge, field, items = solve(0, (plan, first_two, inv, mixing, in_hbm(own), halo, depth))
     got = every(items)
     edge, field = in_hbm(edge), in_hbm(field)
-    (new,) = solve(1, (in_hbm(last_two), inv, mixing, edge, new))
-    got, new = lax.optimization_barrier((got, new))
+    last_two, new = stencil(1, (tracers, velocity, in_vmem(mixed)))
+    got, last_two = lax.optimization_barrier((got, last_two))
     vectors, sums = krylov(plan, field, depth, edge, got)
     totals = every(sums)
+    _, new = solve(1, (in_vmem(last_two), inv, mixing, edge, in_hbm(new)))
+    totals, new = lax.optimization_barrier((totals, new))
     line = [vectors] + [along_y(vectors, k) for k in range(1, side)]
     sends = combine(plan, totals.reshape(128, BE), line)
     arrived = [sends[0]] + [along_z(sends[k], k) for k in range(1, side)]

time: 96.7 us -> 95.1 us (0.983)
  blocking collectives: 16.1 us -> 0 us
  waiting for transfers between devices: 16.7 us -> 25.7 us
  starting transfers between devices: 29.6 us -> 34.8 us
    all_to_all x1 -> x0, blocking collectives: 16.1 us -> none  [body(): every = lambda value: lax.all_to_all(value, ('gx', 'gy'), 0, 0)]
    all_to_all x3 -> x4, waiting for transfers between devices: 13.7 us -> 22.7 us  [body(): every = lambda value: lax.all_to_all(value, ('gx', 'gy'), 0, 0)]
    all_to_all x3 -> x4, starting transfers between devices: 22.9 us -> 28.1 us  [body(): every = lambda value: lax.all_to_all(value, ('gx', 'gy'), 0, 0)]
    pallas_call x2, Pallas kernels: 10.1 us -> 8.83 us  [solve(): pl.pallas_call(functools.partial(solve_kernel, group, chunk, out_chunk),...]
  transfers between devices with their start and end apart: 9 -> 10, of which waited for: 6 -> 7; matrix products, arithmetic and copies ran while one was open for 0% -> 0% of each run, Pallas kernels for 19% -> 20%
where the time goes in v3:
time: 95.1 us; the launch traced here: 94.7 us
  starting transfers between devices  34.8 us (37%)
  Pallas kernels  33.4 us (35%)
  waiting for transfers between devices  25.7 us (27%)
    all_to_all x4, starting transfers between devices, body(): every = lambda value: lax.all_to_all(value, ('gx', 'gy'), 0, 0)  28.1 us
    all_to_all x4, waiting for transfers between devices, body(): every = lambda value: lax.all_to_all(value, ('gx', 'gy'), 0, 0)  22.7 us
    pallas_call x2, Pallas kernels, stencil(): pl.pallas_call(functools.partial(stencil_kernel, group, chunk), out_shape...  12.2 us
    pallas_call x2, Pallas kernels, solve(): pl.pallas_call(functools.partial(solve_kernel, group, chunk, out_chunk),...  8.83 us
    pallas_call x1, Pallas kernels, pack(): pl.pallas_call(pack_kernel, out_shape=pltpu.HBM((ITEM, BE), F32), in_spec...  4.31 us
    ppermute x3, starting transfers between devices, along_z(): lax.ppermute(value, 'gx', [(z * side + y, (z + k) % side * side + y) for...  4.06 us
    ppermute x3, waiting for transfers between devices, along_z(): lax.ppermute(value, 'gx', [(z * side + y, (z + k) % side * side + y) for...  3.05 us
    ppermute x3, starting transfers between devices, along_y(): lax.ppermute(value, 'gx', [(z * side + y, z * side + (y + k) % side) for...  2.67 us
  transfers between devices with their start and end apart: 10, of which 7 were waited for; matrix products, arithmetic and copies ran while one was open for 0% of the time, Pallas kernels for 20%

profile of v3, /device:TPU:0, one launch (start us, length us, event | category | flops | bytes accessed | tf_op | source)
XLA Modules:
  0.0 94.7 jit_solution(5352189426104193092)
XLA Ops:
  0.6 0.0 copy-start
  0.6 0.0 copy-start.1
  0.6 4.3 %pack.1.refs_4_ = f32[512,128]{1,0:T(8,128)} custom-call(f32[9216,128]{1,0:T(8,128)} %bitcast.11, f32[4608,128]{1,0:T(8,128)} %bitcast.14, f32[64,128]{1,0:T(8,128)} %bitcast.22), custom_call_target="tpu_custom_call" | custom-call | tf_op jit(solution)/shard_map/pack/pallas_call | solution.py:152
  5.0 11.1 %all-to-all-start = ((f32[128,4,128]{2,1,0:T(4,128)}), f32[128,4,128]{2,1,0:T(4,128)S(1)}, u32[]{:S(2)}, u32[]{:S(2)}) async-start(f32[128,4,128]{2,1,0:T(4,128)} %bitcast.21), calls=%async_computation | async-start | bytes 524288 | tf_op jit(solution)/shard_map/all_to_all | solution.py:662
  16.1 2.1 %plan.1.refs_0_ = s32[146]{0:T(256)S(1)} custom-call(s32[8,16]{1,0:T(8,128)S(1)} %copy-done, s32[8,32]{1,0:T(8,128)S(1)} %copy-done.1), custom_call_target="tpu_custom_call" | custom-call | tf_op jit(solution)/shard_map/plan/pallas_call | solution.py:679
  18.3 8.6 %all-to-all-done.got = f32[128,4,128]{2,1,0:T(4,128)S(1)} async-done(((f32[128,4,128]{2,1,0:T(4,128)}), f32[128,4,128]{2,1,0:T(4,128)S(1)}, u32[]{:S(2)}, u32[]{:S(2)}) %all-to-all-start) | async-done | bytes 262176 | tf_op jit(solution)/shard_map/all_to_all | solution.py:662
  26.8 1.5 %select.1 = f32[128,4,128]{2,1,0:T(4,128)} custom-call(s32[146]{0:T(256)S(1)} %plan.1.refs_0_, f32[128,4,128]{2,1,0:T(4,128)S(1)} %all-to-all-done.got), custom_call_target="tpu_custom_call" | custom-call | tf_op jit(solution)/shard_map/select/pallas_call | solution.py:180
  28.3 4.8 %all-to-all-start.1 = ((f32[128,4,128]{2,1,0:T(4,128)}), f32[128,4,128]{2,1,0:T(4,128)S(1)}, u32[]{:S(2)}, u32[]{:S(2)}) async-start(f32[128,4,128]{2,1,0:T(4,128)} %select.1), calls=%async_computation.1 | async-start | bytes 524288 | tf_op jit(solution)/shard_map/all_to_all | solution.py:662
  33.1 6.1 %stencil0.1 = (f32[4608,128]{1,0:T(8,128)S(1)}, f32[2304,128]{1,0:T(8,128)}) custom-call(f32[9216,128]{1,0:T(8,128)} %bitcast.12, f32[4608,128]{1,0:T(8,128)} %bitcast.15, f32[2240,128]{1,0:T(8,128)} %bitcast.17), custom_call_target="tpu_custom_call" | custom-call | tf_op jit(solution)/shard_map/stencil0/pallas_call | solution.py:310
  39.2 4.7 %all-to-all-done.1 = f32[128,4,128]{2,1,0:T(4,128)S(1)} async-done(((f32[128,4,128]{2,1,0:T(4,128)}), f32[128,4,128]{2,1,0:T(4,128)S(1)}, u32[]{:S(2)}, u32[]{:S(2)}) %all-to-all-start.1) | async-done | bytes 262176 | tf_op jit(solution)/shard_map/all_to_all | solution.py:662
  43.9 4.5 %solve0.1 = (f32[4608,128]{1,0:T(8,128)S(1)}, f32[592,128]{1,0:T(8,128)}, f32[64,128]{1,0:T(8,128)}, f32[128,4,128]{2,1,0:T(4,128)}) custom-call(s32[146]{0:T(256)S(1)} %plan.1.refs_0_, f32[4608,128]{1,0:T(8,128)S(1)} %get-tuple-element.21.refs_1_, f32[2304,128]{1,0:T(8,128)} %get-tuple-element.22.refs_2_.refs_1_, ...), custom_call_target="tpu_custom_call", output_to_operand_aliasing={{0}: (1, {})} | custom-call | tf_op jit(solution)/shard_map/solve0/pallas_call | solution.py:480
  48.4 5.1 %all-to-all-start.2 = ((f32[128,4,128]{2,1,0:T(4,128)}), f32[128,4,128]{2,1,0:T(4,128)S(1)}, u32[]{:S(2)}, u32[]{:S(2)}) async-start(f32[128,4,128]{2,1,0:T(4,128)} %get-tuple-element.25), calls=%async_computation.2 | async-start | bytes 524288 | tf_op jit(solution)/shard_map/all_to_all | solution.py:662
  53.5 6.1 %stencil1.1 = (f32[4608,128]{1,0:T(8,128)S(1)}, f32[9216,128]{1,0:T(8,128)}) custom-call(f32[9216,128]{1,0:T(8,128)} %bitcast.13, f32[4608,128]{1,0:T(8,128)} %bitcast.16, f32[4608,128]{1,0:T(8,128)S(1)} %get-tuple-element.26.refs_2_), custom_call_target="tpu_custom_call", output_to_operand_aliasing={{0}: (2, {})} | custom-call | tf_op jit(solution)/shard_map/stencil1/pallas_call | solution.py:310
  59.6 4.6 %all-to-all-done.2.got = f32[128,4,128]{2,1,0:T(4,128)S(1)} async-done(((f32[128,4,128]{2,1,0:T(4,128)}), f32[128,4,128]{2,1,0:T(4,128)S(1)}, u32[]{:S(2)}, u32[]{:S(2)}) %all-to-all-start.2) | async-done | bytes 262176 | tf_op jit(solution)/shard_map/all_to_all | solution.py:662
  64.2 2.4 %krylov.1 = (f32[192,128]{1,0:T(8,128)S(1)}, f32[128,1,128]{2,1,0:T(1,128)}) custom-call(s32[146]{0:T(256)S(1)} %plan.1.refs_0_, f32[64,128]{1,0:T(8,128)} %get-tuple-element.23.field, f32[64,128]{1,0:T(8,128)} %bitcast.24, f32[592,128]{1,0:T(8,128)} %get-tuple-element.24.edge.refs_3_, f32[128,4,128]{2,1,0:T(4,128)S(1)} %all-to-all-done.2.got), custom_call_target="tpu_custom_call" | custom-call | tf_op jit(solution)/shard_map/krylov/pallas_call | solution.py:573
  66.7 1.0 %collective-permute-start.2 = (f32[192,128]{1,0:T(8,128)S(1)}, f32[192,128]{1,0:T(8,128)S(1)}, u32[]{:S(2)}, u32[]{:S(2)}) collective-permute-start(f32[192,128]{1,0:T(8,128)S(1)} %get-tuple-element.35.a0), channel_id=1, source_target_pairs={{0,24},{8,0},{16,8},{24,16},{32,56},{40,32},{48,40},{56,48},{64,88... | collective-permute-start | bytes 294920 | tf_op jit(solution)/shard_map/ppermute | solution.py:665
  67.6 1.5 %collective-permute-start.1 = (f32[192,128]{1,0:T(8,128)S(1)}, f32[192,128]{1,0:T(8,128)S(1)}, u32[]{:S(2)}, u32[]{:S(2)}) collective-permute-start(f32[192,128]{1,0:T(8,128)S(1)} %get-tuple-element.35.a0), channel_id=1, source_target_pairs={{0,16},{8,24},{16,0},{24,8},{32,48},{40,56},{48,32},{56,40},{64,80... | collective-permute-start | bytes 294920 | tf_op jit(solution)/shard_map/ppermute | solution.py:665
  69.1 0.2 collective-permute-start
  69.3 7.0 %all-to-all-start.3 = ((f32[128,1,128]{2,1,0:T(1,128)}), f32[128,1,128]{2,1,0:T(1,128)S(1)}, u32[]{:S(2)}, u32[]{:S(2)}) async-start(f32[128,1,128]{2,1,0:T(1,128)} %get-tuple-element.29), calls=%async_computation.3 | async-start | bytes 131072 | tf_op jit(solution)/shard_map/all_to_all | solution.py:662
  76.4 4.3 %solve1.1 = (f32[4608,128]{1,0:T(8,128)S(1)}, f32[9216,128]{1,0:T(8,128)}) custom-call(f32[4608,128]{1,0:T(8,128)S(1)} %get-tuple-element.30.refs_0_, f32[2304,128]{1,0:T(8,128)} %get-tuple-element.22.refs_2_.refs_1_, f32[2240,128]{1,0:T(8,128)} %bitcast.19, ...), custom_call_target="tpu_custom_call", output_to_operand_aliasing={{0}: (0, {}), {1}: (4, {})} | custom-call | tf_op jit(solution)/shard_map/solve1/pallas_call | solution.py:480
  80.7 4.9 %all-to-all-done.3 = f32[128,1,128]{2,1,0:T(1,128)S(1)} async-done(((f32[128,1,128]{2,1,0:T(1,128)}), f32[128,1,128]{2,1,0:T(1,128)S(1)}, u32[]{:S(2)}, u32[]{:S(2)}) %all-to-all-start.3) | async-done | bytes 65568 | tf_op jit(solution)/shard_map/all_to_all | solution.py:662
  85.6 0.0 collective-permute-done.2.a3
  85.6 0.0 collective-permute-done.1.a2
  85.6 0.0 collective-permute-done.a1
  85.6 0.8 combine.1
  86.4 0.9 collective-permute-start.3
  87.3 1.5 %collective-permute-start.4 = (f32[128,128]{1,0:T(8,128)S(1)}, f32[128,128]{1,0:T(8,128)S(1)}, u32[]{:S(2)}, u32[]{:S(2)}) collective-permute-start(f32[128,128]{1,0:T(8,128)S(1)} %get-tuple-element.38), channel_id=1, source_target_pairs={{0,64},{8,72},{16,80},{24,88},{32,96},{40,104},{48,112},{56,120},{... | collective-permute-start | bytes 196616 | tf_op jit(solution)/shard_map/ppermute | solution.py:669
  88.8 1.7 %collective-permute-start.5 = (f32[128,128]{1,0:T(8,128)S(1)}, f32[128,128]{1,0:T(8,128)S(1)}, u32[]{:S(2)}, u32[]{:S(2)}) collective-permute-start(f32[128,128]{1,0:T(8,128)S(1)} %get-tuple-element.39), channel_id=1, source_target_pairs={{0,96},{8,104},{16,112},{24,120},{32,0},{40,8},{48,16},{56,24},{64... | collective-permute-start | bytes 196616 | tf_op jit(solution)/shard_map/ppermute | solution.py:669
  90.5 1.8 %collective-permute-done.3.a1 = f32[128,128]{1,0:T(8,128)S(1)} collective-permute-done((f32[128,128]{1,0:T(8,128)S(1)}, f32[128,128]{1,0:T(8,128)S(1)}, u32[]{:S(2)}, u32[]{:S(2)}) %collective-permute-start.3) | collective-permute-done | bytes 65568 | tf_op jit(solution)/shard_map/ppermute | solution.py:669
  92.3 0.7 collective-permute-done.4.a2
  93.0 0.5 collective-permute-done.5.a3
  93.5 1.2 %place.1 = f32[2,64,128]{2,1,0:T(8,128)} custom-call(s32[146]{0:T(256)S(1)} %plan.1.refs_0_, f32[128,128]{1,0:T(8,128)S(1)} %get-tuple-element.36.a0, f32[128,128]{1,0:T(8,128)S(1)} %collective-permute-done.3.a1, f32[128,128]{1,0:T(8,128)S(1)} %collective-permute-done.4.a2, f32[128,128]{1,0:T(8,128)S(1)} %collective-permute-done.5.a3), custom_call_target="tpu_custom_call" | custom-call | tf_op jit(solution)/shard_map/place/pallas_call | solution.py:649
  (2 shorter events, 0.0 us)
Async XLA Ops:
  0.6 15.5 %copy-start = (s32[8,16]{1,0:T(8,128)S(1)}, s32[8,16]{1,0:T(8,128)}, u32[]{:S(2)}) copy-start(s32[8,16]{1,0:T(8,128)} %clinic.1) | copy-start | bytes 1540
  0.6 15.5 %copy-start.1 = (s32[8,32]{1,0:T(8,128)S(1)}, s32[8,32]{1,0:T(8,128)}, u32[]{:S(2)}) copy-start(s32[8,32]{1,0:T(8,128)} %tropic.1) | copy-start | bytes 3076
  5.0 21.9 %all-to-all-start = ((f32[128,4,128]{2,1,0:T(4,128)}), f32[128,4,128]{2,1,0:T(4,128)S(1)}, u32[]{:S(2)}, u32[]{:S(2)}) async-start(f32[128,4,128]{2,1,0:T(4,128)} %bitcast.21), calls=%async_computation | async-start | bytes 524288 | tf_op jit(solution)/shard_map/all_to_all | solution.py:662
  28.3 15.5 %all-to-all-start.1 = ((f32[128,4,128]{2,1,0:T(4,128)}), f32[128,4,128]{2,1,0:T(4,128)S(1)}, u32[]{:S(2)}, u32[]{:S(2)}) async-start(f32[128,4,128]{2,1,0:T(4,128)} %select.1), calls=%async_computation.1 | async-start | bytes 524288 | tf_op jit(solution)/shard_map/all_to_all | solution.py:662
  48.4 15.9 %all-to-all-start.2 = ((f32[128,4,128]{2,1,0:T(4,128)}), f32[128,4,128]{2,1,0:T(4,128)S(1)}, u32[]{:S(2)}, u32[]{:S(2)}) async-start(f32[128,4,128]{2,1,0:T(4,128)} %get-tuple-element.25), calls=%async_computation.2 | async-start | bytes 524288 | tf_op jit(solution)/shard_map/all_to_all | solution.py:662
  66.7 18.9 %collective-permute-start.2 = (f32[192,128]{1,0:T(8,128)S(1)}, f32[192,128]{1,0:T(8,128)S(1)}, u32[]{:S(2)}, u32[]{:S(2)}) collective-permute-start(f32[192,128]{1,0:T(8,128)S(1)} %get-tuple-element.35.a0), channel_id=1, source_target_pairs={{0,24},{8,0},{16,8},{24,16},{32,56},{40,32},{48,40},{56,48},{64,88... | collective-permute-start | bytes 294920 | tf_op jit(solution)/shard_map/ppermute | solution.py:665
  67.6 18.0 %collective-permute-start.1 = (f32[192,128]{1,0:T(8,128)S(1)}, f32[192,128]{1,0:T(8,128)S(1)}, u32[]{:S(2)}, u32[]{:S(2)}) collective-permute-start(f32[192,128]{1,0:T(8,128)S(1)} %get-tuple-element.35.a0), channel_id=1, source_target_pairs={{0,16},{8,24},{16,0},{24,8},{32,48},{40,56},{48,32},{56,40},{64,80... | collective-permute-start | bytes 294920 | tf_op jit(solution)/shard_map/ppermute | solution.py:665
  69.1 16.5 %collective-permute-start = (f32[192,128]{1,0:T(8,128)S(1)}, f32[192,128]{1,0:T(8,128)S(1)}, u32[]{:S(2)}, u32[]{:S(2)}) collective-permute-start(f32[192,128]{1,0:T(8,128)S(1)} %get-tuple-element.35.a0), channel_id=1, source_target_pairs={{0,8},{8,16},{16,24},{24,0},{32,40},{40,48},{48,56},{56,32},{64,72... | collective-permute-start | bytes 294920 | tf_op jit(solution)/shard_map/ppermute | solution.py:665
  69.3 16.2 %all-to-all-start.3 = ((f32[128,1,128]{2,1,0:T(1,128)}), f32[128,1,128]{2,1,0:T(1,128)S(1)}, u32[]{:S(2)}, u32[]{:S(2)}) async-start(f32[128,1,128]{2,1,0:T(1,128)} %get-tuple-element.29), calls=%async_computation.3 | async-start | bytes 131072 | tf_op jit(solution)/shard_map/all_to_all | solution.py:662
  86.4 5.9 %collective-permute-start.3 = (f32[128,128]{1,0:T(8,128)S(1)}, f32[128,128]{1,0:T(8,128)S(1)}, u32[]{:S(2)}, u32[]{:S(2)}) collective-permute-start(f32[128,128]{1,0:T(8,128)S(1)} %get-tuple-element.37), channel_id=1, source_target_pairs={{0,32},{8,40},{16,48},{24,56},{32,64},{40,72},{48,80},{56,88},{64,... | collective-permute-start | bytes 196616 | tf_op jit(solution)/shard_map/ppermute | solution.py:669
  87.3 5.8 %collective-permute-start.4 = (f32[128,128]{1,0:T(8,128)S(1)}, f32[128,128]{1,0:T(8,128)S(1)}, u32[]{:S(2)}, u32[]{:S(2)}) collective-permute-start(f32[128,128]{1,0:T(8,128)S(1)} %get-tuple-element.38), channel_id=1, source_target_pairs={{0,64},{8,72},{16,80},{24,88},{32,96},{40,104},{48,112},{56,120},{... | collective-permute-start | bytes 196616 | tf_op jit(solution)/shard_map/ppermute | solution.py:669
  88.8 4.7 %collective-permute-start.5 = (f32[128,128]{1,0:T(8,128)S(1)}, f32[128,128]{1,0:T(8,128)S(1)}, u32[]{:S(2)}, u32[]{:S(2)}) collective-permute-start(f32[128,128]{1,0:T(8,128)S(1)} %get-tuple-element.39), channel_id=1, source_target_pairs={{0,96},{8,104},{16,112},{24,120},{32,0},{40,8},{48,16},{56,24},{64... | collective-permute-start | bytes 196616 | tf_op jit(solution)/shard_map/ppermute | solution.py:669

commit v4 on v3

--- a/solution.py
+++ b/solution.py
@@ -4,12 +4,14 @@
 from jax import lax
 from jax.experimental import pallas as pl
 from jax.experimental.pallas import tpu as pltpu
-from jax.sharding import PartitionSpec as P
+from jax.sharding import Mesh, PartitionSpec as P
 
 F32 = jnp.float32
 LEV, BN, BE = 36, 64, 128
 NBX = 28
 N_GX, N_GY, SIDE = 16, 8, 4
+SIZES = {"z": 4, "y": 4, "x": 4, "c": 2}
+EVERY = ('c', 'z', 'x', 'y')
 CELLS = LEV * BN
 HALF = BE // 2
 
@@ -56,11 +58,29 @@
     return jax.ShapeDtypeStruct(shape, F32)
 
 
+def place_of(axis, slot, row):
+    return {"z": slot // SIDE, "y": slot % SIDE, "x": row // 2, "c": row % 2}[axis]
+
+
+def device_of(slot, row):
+    index = 0
+    for axis in EVERY:
+        index = index * SIZES[axis] + place_of(axis, slot, row)
+    return index
+
+
+def slot_of(device):
+    stride, at = 1, {}
+    for axis in reversed(EVERY):
+        at[axis] = lax.rem(device // stride, SIZES[axis])
+        stride *= SIZES[axis]
+    return at["z"] * SIDE + at["y"]
+
+
 def make_plan(side, n_gy, slots, clinic, tropic, out, pos):
-    gx = lax.axis_index("gx")
-    gy = lax.axis_index("gy")
-    z = gx // side
-    y = lax.rem(gx, side)
+    z, y = lax.axis_index("z"), lax.axis_index("y")
+    gx = z * side + y
+    gy = lax.axis_index("x") * 2 + lax.axis_index("c")
 
     def clear(i, carry):
         pos[i] = jnp.int32(-1)
@@ -69,26 +89,28 @@
     lax.fori_loop(0, (n_gy + 2) * WRAP, clear, 0, unroll=16)
     for row in range(n_gy):
         for slot in range(slots):
-            pos[(row + 1) * WRAP + 1 + clinic[row, slot]] = jnp.int32(slot * n_gy + row)
+            pos[(row + 1) * WRAP + 1 + clinic[row, slot]] = jnp.int32(device_of(slot, row))
     for row in range(1, n_gy + 1):
         pos[row * WRAP] = pos[row * WRAP + NBX]
         pos[row * WRAP + NBX + 1] = pos[row * WRAP + 1]
     centre = (gy + 1) * WRAP + 1 + clinic[gy, gx]
     for d, (dr, dc) in enumerate(DIRS):
         out[NBR + d] = pos[centre + (dr * WRAP + dc)]
-    me = gx * n_gy + gy
+    me = jnp.int32(0)
+    for axis in EVERY:
+        me = me * SIZES[axis] + lax.axis_index(axis)
     kind_s, kind_n, kind_w = me < SOUTH // PART, me < EAST // PART, me < WEST // PART
     move = jnp.where(kind_s, jnp.int32(-WRAP), jnp.where(kind_n, jnp.int32(WRAP), jnp.where(
         kind_w, jnp.int32(-1), jnp.int32(1))))
     for row in range(n_gy):
         for there in range(slots):
             source = pos[(row + 1) * WRAP + 1 + clinic[row, there] + move]
-            out[RELAY + there * n_gy + row] = jnp.maximum(source, 0)
+            out[RELAY + device_of(there, row)] = jnp.maximum(source, 0)
 
     def owner(there, b):
         column_b = tropic[gy, 2 * there + b]
         device = pos[(gy + 1) * WRAP + 1 + jnp.maximum(column_b, 0)]
-        return jnp.where(column_b < 0, jnp.int32(-1), device // n_gy)
+        return jnp.where(column_b < 0, jnp.int32(-1), slot_of(device))
 
     for k in range(side):
         there = lax.rem(z + k, side) * side + y
@@ -138,14 +160,21 @@
             for k in range(LEV):
                 tile = vel[pl.ds(k * BN, BN), :]
                 first = jnp.where(lane == 2 * LEV + k, pltpu.roll(tile, 2 * LEV + 1 + k, 1), first)
+        if j == 1:
+            copies[5].wait()
+            own[pl.ds(NORTH_V, LEV), :] = vel[pl.ds(CELLS + BN - 1, LEV, stride=BN), :]
+            rows_out = pltpu.make_async_copy(own.at[pl.ds(0, 328)], item.at[pl.ds(0, 328)], sems.at[7])
+            rows_out.start()
         turn[...] = jnp.concatenate([first, second], axis=0).T
         own[pl.ds(EAST + j * LEV, LEV), :] = turn[pl.ds(0, LEV, stride=2), :]
         own[pl.ds(WEST + j * LEV, LEV), :] = turn[pl.ds(1, LEV, stride=2), :]
         if j == 0:
             own[pl.ds(EAST + 2 * LEV, LEV), :] = turn[pl.ds(2 * LEV, LEV), :]
-    copies[5].wait()
-    own[pl.ds(NORTH_V, LEV), :] = vel[pl.ds(CELLS + BN - 1, LEV, stride=BN), :]
-    pltpu.sync_copy(own, item)
+    rest = pl.ds(328, ITEM - 328)
+    rest_out = pltpu.make_async_copy(own.at[rest], item.at[rest], sems.at[8])
+    rest_out.start()
+    rows_out.wait()
+    rest_out.wait()
 
 
 def pack(tracers, velocity, depth):
@@ -160,20 +189,26 @@
             pltpu.VMEM((BE, BE), F32),
             pltpu.VMEM((ITEM, BE), F32),
             pltpu.VMEM((BN, BE), F32),
-            pltpu.SemaphoreType.DMA((7,)),
+            pltpu.SemaphoreType.DMA((9,)),
         ],
         compiler_params=params(12),
         name="pack",
     )(tracers, velocity, depth)
 
 
-def select_kernel(plan, got, out, chosen_parts):
+def select_kernel(plan, got, out, chosen_parts, sems):
     def one(d, carry):
         chosen_parts[d] = got[plan[RELAY + d]]
         return carry
 
-    lax.fori_loop(0, 128, one, 0, unroll=8)
-    pltpu.sync_copy(chosen_parts, out)
+    copies = []
+    for half in range(2):
+        lax.fori_loop(64 * half, 64 * half + 64, one, 0, unroll=16)
+        span = pl.ds(64 * half, 64)
+        copies.append(pltpu.make_async_copy(chosen_parts.at[span], out.at[span], sems.at[half]))
+        copies[-1].start()
+    for copy in copies:
+        copy.wait()
 
 
 def select(plan, got):
@@ -182,7 +217,7 @@
         out_shape=pltpu.HBM((128, PART, BE), F32),
         in_specs=[SM, VM],
         out_specs=HBM,
-        scratch_shapes=[pltpu.VMEM((128, PART, BE), F32)],
+        scratch_shapes=[pltpu.VMEM((128, PART, BE), F32), pltpu.SemaphoreType.DMA((2,))],
         compiler_params=params(2),
         name="select",
     )(plan, got)
@@ -324,7 +359,7 @@
 
 
 EDGE_N, EDGE_S, EDGE = BN, BN + 40, BN + 80
-EDGE_D = 4 * EDGE
+BASE_D, BASE_S, BASE_N, BASE = BN, 2 * BN, 2 * BN + 8, 2 * BN + 16
 
 
 def flux(speed, low, high):
@@ -363,7 +398,7 @@
     outs = []
     if group == 0:
         (plan, _aliased, inv_in, mixing, own_in, halo, depth_in,
-         s, edge_out, force_out, items, inv, mix, edge, turn, parts_out, own, depth, force,
+         s, edge_out, base, items, inv, mix, edge, turn, parts_out, own, depth,
          sems, side_sems) = refs
         sides = [pltpu.make_async_copy(a, b, side_sems.at[i]) for i, (a, b) in enumerate(
             ((own_in, own), (depth_in, depth)))]
@@ -387,8 +422,9 @@
         copy.wait()
     if group == 0:
         edges(plan, own, halo, edge, turn)
-        edge[pl.ds(EDGE_D, 8), :] = halo[pl.ds(NORTH_D - 4, 8), :]
-        edge[pl.ds(EDGE_D + 8, 8), :] = halo[pl.ds(SOUTH_D, 8), :]
+        base[pl.ds(BASE_D, BN), :] = depth[...]
+        base[pl.ds(BASE_S, 8), :] = halo[pl.ds(NORTH_D - 4, 8), :]
+        base[pl.ds(BASE_N, 8), :] = halo[pl.ds(SOUTH_D, 8), :]
         outs.append(pltpu.make_async_copy(edge, edge_out, side_sems.at[3]))
         outs[-1].start()
     lane = lax.broadcasted_iota(jnp.int32, (BN, BE), 1)
@@ -439,9 +475,7 @@
                 outs[-1].start()
     if group == 0:
         field = total
-        force[...] = field
-        outs.append(pltpu.make_async_copy(force, force_out, side_sems.at[4]))
-        outs[-1].start()
+        base[pl.ds(0, BN), :] = field
         turned = jnp.concatenate([field, depth[...]], axis=0).T
         east_item, west_item = turned[BE - 3:, :], turned[:3, :]
         sends = (east_item, west_item, field[BN - 3:, :], field[:3, :],
@@ -460,15 +494,15 @@
 
 
 def solve(group, args, chunk=12, out_chunk=6):
-    edge_rows = EDGE_D + 16
+    edge_rows = 4 * EDGE
     block = lambda rows: pltpu.VMEM((rows, BE), F32)
     if group == 0:
         in_specs = [SM, VM, HBM, HBM, HBM, VM, HBM]
-        outs = [cells(0, 2), pltpu.HBM((edge_rows, BE), F32), pltpu.HBM((BN, BE), F32),
+        outs = [cells(0, 2), pltpu.HBM((edge_rows, BE), F32), block(BASE),
                 pltpu.HBM((128, PART, BE), F32)]
-        out_specs = [VM] + [HBM] * 3
+        out_specs = [VM, HBM, VM, HBM]
         scratch = [cells(), cells(), block(edge_rows), block(BE), pltpu.VMEM((128, PART, BE), F32),
-                   block(ITEM), block(BN), block(BN)]
+                   block(ITEM), block(BN)]
     else:
         in_specs = [VM] + [HBM] * 4
         outs, out_specs = [cells(0, 2), pltpu.HBM((4 * CELLS, BE), F32)], [VM, HBM]
@@ -499,14 +533,7 @@
 TALL, WIDE = BN + 8, 2 * BE
 
 
-def krylov_kernel(plan, field, depth, edge, got, vectors, sums, b_s, d_s, edge_d, sems):
-    copies = [
-        pltpu.make_async_copy(field, b_s.at[pl.ds(0, BN), pl.ds(0, BE)], sems.at[0]),
-        pltpu.make_async_copy(depth, d_s.at[pl.ds(0, BN), pl.ds(0, BE)], sems.at[1]),
-        pltpu.make_async_copy(edge.at[pl.ds(EDGE_D, 16)], edge_d, sems.at[2]),
-    ]
-    for copy in copies:
-        copy.start()
+def krylov_kernel(plan, base, got, vectors, sums, b_s, d_s):
     nothing = jnp.zeros((3, BE), F32)
 
     def item(d):
@@ -515,6 +542,8 @@
 
     for ref in (b_s, d_s):
         ref[pl.ds(BN, 8), :] = jnp.zeros((8, WIDE), F32)
+    b_s[pl.ds(0, BN), pl.ds(0, BE)] = base[pl.ds(0, BN), :]
+    d_s[pl.ds(0, BN), pl.ds(0, BE)] = base[pl.ds(BASE_D, BN), :]
     b_s[pl.ds(BN, 3), pl.ds(0, BE)] = item(2)
     b_s[pl.ds(TALL - 3, 3), pl.ds(0, BE)] = item(3)
     middle = jnp.zeros((BE - 6, BE), F32)
@@ -532,12 +561,10 @@
     b_s[pl.ds(BN, 8), pl.ds(BE, BE)] = corners[:8]
     d_s[pl.ds(BN, 8), pl.ds(BE, BE)] = corners[BN:BN + 8]
 
-    for copy in copies:
-        copy.wait()
     d_s[pl.ds(BN, 3), pl.ds(0, BE)] = jnp.where(
-        plan[NBR + 2] >= 0, edge_d[pl.ds(8, 3), :], 0.0)
+        plan[NBR + 2] >= 0, base[pl.ds(BASE_N, 3), :], 0.0)
     d_s[pl.ds(TALL - 3, 3), pl.ds(0, BE)] = jnp.where(
-        plan[NBR + 3] >= 0, edge_d[pl.ds(4, 3), :], 0.0)
+        plan[NBR + 3] >= 0, base[pl.ds(BASE_S + 4, 3), :], 0.0)
     d = d_s[...]
     east = lambda a: pltpu.roll(a, WIDE - 1, 1)
     west = lambda a: pltpu.roll(a, 1, 1)
@@ -569,20 +596,19 @@
         sums[i] = total
 
 
-def krylov(plan, field, depth, edge, got):
+def krylov(plan, base, got):
     return pl.pallas_call(
         krylov_kernel,
         out_shape=(
             jax.ShapeDtypeStruct((3 * BN, BE), F32),
             jax.ShapeDtypeStruct((128, 1, BE), F32),
         ),
-        in_specs=[SM] + [HBM] * 3 + [VM],
+        in_specs=[SM, VM, VM],
         out_specs=(VM, VM),
-        scratch_shapes=[pltpu.VMEM((TALL, WIDE), F32)] * 2 + [
-            pltpu.VMEM((16, BE), F32), pltpu.SemaphoreType.DMA((3,))],
+        scratch_shapes=[pltpu.VMEM((TALL, WIDE), F32)] * 2,
         compiler_params=params(4),
         name="krylov",
-    )(plan, field, depth, edge, got)
+    )(plan, base, got)
 
 
 def combine_kernel(plan, sums, a0, a1, a2, a3, o0, o1, o2, o3):
@@ -659,15 +685,13 @@
 def body(tracers, velocity, mixing_rate, column_depth, ocean_mask, clinic_list, tropic_list):
     side = SIDE
     depth = column_depth.reshape(BN, BE)
-    every = lambda value: lax.all_to_all(value, ("gx", "gy"), 0, 0)
+    every = lambda value: lax.all_to_all(value, EVERY, 0, 0)
 
     def along_y(value, k):
-        return lax.ppermute(value, "gx", [
-            (z * side + y, z * side + (y + k) % side) for z in range(side) for y in range(side)])
+        return lax.ppermute(value, "y", [(y, (y + k) % side) for y in range(side)])
 
     def along_z(value, k):
-        return lax.ppermute(value, "gx", [
-            (z * side + y, (z + k) % side * side + y) for z in range(side) for y in range(side)])
+        return lax.ppermute(value, "z", [(z, (z + k) % side) for z in range(side)])
 
     in_hbm = lambda value: pltpu.with_memory_space_constraint(value, pltpu.HBM)
     tracers = in_hbm(tracers.reshape(4 * CELLS, BE))
@@ -689,12 +713,12 @@
     first_two, inv = in_vmem(first_two), in_hbm(inv)
     scattered = every(own.reshape(128, PART, BE))
     halo = every(select(plan, scattered)).reshape(ITEM, BE)
-    mixed, edge, field, items = solve(0, (plan, first_two, inv, mixing, in_hbm(own), halo, depth))
+    mixed, edge, base, items = solve(0, (plan, first_two, inv, mixing, in_hbm(own), halo, depth))
     got = every(items)
-    edge, field = in_hbm(edge), in_hbm(field)
+    edge = in_hbm(edge)
     last_two, new = stencil(1, (tracers, velocity, in_vmem(mixed)))
     got, last_two = lax.optimization_barrier((got, last_two))
-    vectors, sums = krylov(plan, field, depth, edge, got)
+    vectors, sums = krylov(plan, in_vmem(base), got)
     totals = every(sums)
     _, new = solve(1, (in_vmem(last_two), inv, mixing, edge, in_hbm(new)))
     totals, new = lax.optimization_barrier((totals, new))
@@ -706,18 +730,12 @@
 
 
 def solution(mesh):
+    mesh = Mesh(mesh.devices.reshape(*(SIZES[axis] for axis in "zyxc")), tuple("zyxc"))
+    gx, gy = ("z", "y"), ("x", "c")
     return jax.shard_map(
         body,
         mesh=mesh,
-        in_specs=(
-            P("gy", "gx", None, None, None, None),
-            P("gy", "gx", None, None, None, None),
-            P("gy", "gx", None, None, None),
-            P("gy", "gx", None, None),
-            P(),
-            P(),
-            P(),
-        ),
-        out_specs=(P("gy", "gx", None, None, None, None), P("gy", "gx", None, None)),
+        in_specs=(P(gy, gx), P(gy, gx), P(gy, gx), P(gy, gx), P(), P(), P()),
+        out_specs=(P(gy, gx), P(gy, gx)),
         check_vma=False,
     )

time: 95.1 us -> 93.7 us (0.985)
  waiting for transfers between devices: 25.7 us -> 23.9 us
  starting transfers between devices: 34.8 us -> 36 us
    all_to_all x4, waiting for transfers between devices: 22.7 us -> 21.1 us  [body(): every = lambda value: lax.all_to_all(value, EVERY, 0, 0)]
    ppermute x6, starting transfers between devices: 6.73 us -> 8.31 us  [the longest x3 4.27 us: along_z(): return lax.ppermute(value, 'z', [(z, (z + k) % side) for z in range(side)])]
  transfers between devices with their start and end apart: 10 -> 10, of which waited for: 7 -> 6; matrix products, arithmetic and copies ran while one was open for 0% -> 0% of each run, Pallas kernels for 20% -> 20%
where the time goes in v4:
time: 93.7 us; the launch traced here: 93.3 us
  starting transfers between devices  36 us (38%)
  Pallas kernels  32.7 us (35%)
  waiting for transfers between devices  23.9 us (26%)
    all_to_all x4, starting transfers between devices, body(): every = lambda value: lax.all_to_all(value, EVERY, 0, 0)  27.7 us
    all_to_all x4, waiting for transfers between devices, body(): every = lambda value: lax.all_to_all(value, EVERY, 0, 0)  21.1 us
    pallas_call x2, Pallas kernels, stencil(): pl.pallas_call(functools.partial(stencil_kernel, group, chunk), out_shape...  12.2 us
    pallas_call x2, Pallas kernels, solve(): pl.pallas_call(functools.partial(solve_kernel, group, chunk, out_chunk),...  8.85 us
    ppermute x3, starting transfers between devices, along_z(): return lax.ppermute(value, 'z', [(z, (z + k) % side) for z in range(side)])  4.27 us
    pallas_call x1, Pallas kernels, pack(): pl.pallas_call(pack_kernel, out_shape=pltpu.HBM((ITEM, BE), F32), in_spec...  4.27 us
    ppermute x3, starting transfers between devices, along_y(): return lax.ppermute(value, 'y', [(y, (y + k) % side) for y in range(side)])  4.03 us
    ppermute x3, waiting for transfers between devices, along_z(): return lax.ppermute(value, 'z', [(z, (z + k) % side) for z in range(side)])  2.83 us
  transfers between devices with their start and end apart: 10, of which 6 were waited for; matrix products, arithmetic and copies ran while one was open for 0% of the time, Pallas kernels for 20%

profile of v4, /device:TPU:0, one launch (start us, length us, event | category | flops | bytes accessed | tf_op | source)
XLA Modules:
  0.0 93.3 jit_solution(8533410435651132122)
XLA Ops:
  0.6 4.3 %pack.1.refs_4_ = f32[512,128]{1,0:T(8,128)} custom-call(f32[9216,128]{1,0:T(8,128)} %bitcast.11, f32[4608,128]{1,0:T(8,128)} %bitcast.14, f32[64,128]{1,0:T(8,128)} %bitcast.22), custom_call_target="tpu_custom_call" | custom-call | tf_op jit(solution)/shard_map/pack/pallas_call | solution.py:181
  4.9 11.1 %all-to-all-start = ((f32[128,4,128]{2,1,0:T(4,128)}), f32[128,4,128]{2,1,0:T(4,128)S(1)}, u32[]{:S(2)}, u32[]{:S(2)}) async-start(f32[128,4,128]{2,1,0:T(4,128)} %bitcast.21), calls=%async_computation | async-start | bytes 524288 | tf_op jit(solution)/shard_map/all_to_all | solution.py:688
  16.1 0.0 copy-done
  16.1 0.0 copy-done.1
  16.1 2.2 %plan.1.refs_0_ = s32[146]{0:T(256)S(1)} custom-call(s32[8,16]{1,0:T(8,128)S(1)} %copy-done, s32[8,32]{1,0:T(8,128)S(1)} %copy-done.1), custom_call_target="tpu_custom_call" | custom-call | tf_op jit(solution)/shard_map/plan/pallas_call | solution.py:703
  18.3 8.1 %all-to-all-done.got = f32[128,4,128]{2,1,0:T(4,128)S(1)} async-done(((f32[128,4,128]{2,1,0:T(4,128)}), f32[128,4,128]{2,1,0:T(4,128)S(1)}, u32[]{:S(2)}, u32[]{:S(2)}) %all-to-all-start) | async-done | bytes 262176 | tf_op jit(solution)/shard_map/all_to_all | solution.py:688
  26.3 1.4 %select.1 = f32[128,4,128]{2,1,0:T(4,128)} custom-call(s32[146]{0:T(256)S(1)} %plan.1.refs_0_, f32[128,4,128]{2,1,0:T(4,128)S(1)} %all-to-all-done.got), custom_call_target="tpu_custom_call" | custom-call | tf_op jit(solution)/shard_map/select/pallas_call | solution.py:215
  27.8 4.7 %all-to-all-start.1 = ((f32[128,4,128]{2,1,0:T(4,128)}), f32[128,4,128]{2,1,0:T(4,128)S(1)}, u32[]{:S(2)}, u32[]{:S(2)}) async-start(f32[128,4,128]{2,1,0:T(4,128)} %select.1), calls=%async_computation.1 | async-start | bytes 524288 | tf_op jit(solution)/shard_map/all_to_all | solution.py:688
  32.5 6.1 %stencil0.1 = (f32[4608,128]{1,0:T(8,128)S(1)}, f32[2304,128]{1,0:T(8,128)}) custom-call(f32[9216,128]{1,0:T(8,128)} %bitcast.12, f32[4608,128]{1,0:T(8,128)} %bitcast.15, f32[2240,128]{1,0:T(8,128)} %bitcast.17), custom_call_target="tpu_custom_call" | custom-call | tf_op jit(solution)/shard_map/stencil0/pallas_call | solution.py:345
  38.6 4.2 %all-to-all-done.1 = f32[128,4,128]{2,1,0:T(4,128)S(1)} async-done(((f32[128,4,128]{2,1,0:T(4,128)}), f32[128,4,128]{2,1,0:T(4,128)S(1)}, u32[]{:S(2)}, u32[]{:S(2)}) %all-to-all-start.1) | async-done | bytes 262176 | tf_op jit(solution)/shard_map/all_to_all | solution.py:688
  42.7 4.5 %solve0.1 = (f32[4608,128]{1,0:T(8,128)S(1)}, f32[576,128]{1,0:T(8,128)}, f32[144,128]{1,0:T(8,128)S(1)}, f32[128,4,128]{2,1,0:T(4,128)}) custom-call(s32[146]{0:T(256)S(1)} %plan.1.refs_0_, f32[4608,128]{1,0:T(8,128)S(1)} %get-tuple-element.21.refs_1_, f32[2304,128]{1,0:T(8,128)} %get-tuple-element.22.refs_2_.refs_1_, ...), custom_call_target="tpu_custom_call", output_to_operand_aliasing={{0}: (1, {})} | custom-call | tf_op jit(solution)/shard_map/solve0/pallas_call | solution.py:514
  47.3 5.6 %all-to-all-start.2 = ((f32[128,4,128]{2,1,0:T(4,128)}), f32[128,4,128]{2,1,0:T(4,128)S(1)}, u32[]{:S(2)}, u32[]{:S(2)}) async-start(f32[128,4,128]{2,1,0:T(4,128)} %get-tuple-element.24), calls=%async_computation.2 | async-start | bytes 524288 | tf_op jit(solution)/shard_map/all_to_all | solution.py:688
  52.9 6.1 %stencil1.1 = (f32[4608,128]{1,0:T(8,128)S(1)}, f32[9216,128]{1,0:T(8,128)}) custom-call(f32[9216,128]{1,0:T(8,128)} %bitcast.13, f32[4608,128]{1,0:T(8,128)} %bitcast.16, f32[4608,128]{1,0:T(8,128)S(1)} %get-tuple-element.25.refs_2_), custom_call_target="tpu_custom_call", output_to_operand_aliasing={{0}: (2, {})} | custom-call | tf_op jit(solution)/shard_map/stencil1/pallas_call | solution.py:345
  59.0 4.1 %all-to-all-done.2.got = f32[128,4,128]{2,1,0:T(4,128)S(1)} async-done(((f32[128,4,128]{2,1,0:T(4,128)}), f32[128,4,128]{2,1,0:T(4,128)S(1)}, u32[]{:S(2)}, u32[]{:S(2)}) %all-to-all-start.2) | async-done | bytes 262176 | tf_op jit(solution)/shard_map/all_to_all | solution.py:688
  63.1 1.8 %krylov.1 = (f32[192,128]{1,0:T(8,128)S(1)}, f32[128,1,128]{2,1,0:T(1,128)}) custom-call(s32[146]{0:T(256)S(1)} %plan.1.refs_0_, f32[144,128]{1,0:T(8,128)S(1)} %get-tuple-element.23.base, f32[128,4,128]{2,1,0:T(4,128)S(1)} %all-to-all-done.2.got), custom_call_target="tpu_custom_call" | custom-call | tf_op jit(solution)/shard_map/krylov/pallas_call | solution.py:600
  64.9 0.7 collective-permute-start
  65.6 2.3 %collective-permute-start.1 = (f32[192,128]{1,0:T(8,128)S(1)}, f32[192,128]{1,0:T(8,128)S(1)}, u32[]{:S(2)}, u32[]{:S(2)}) collective-permute-start(f32[192,128]{1,0:T(8,128)S(1)} %get-tuple-element.35.a0), channel_id=1, source_target_pairs={{0,16},{8,24},{16,0},{24,8},{1,17},{9,25},{17,1},{25,9},{2,18},{10... | collective-permute-start | bytes 294920 | tf_op jit(solution)/shard_map/ppermute | solution.py:691
  67.9 1.1 %collective-permute-start.2 = (f32[192,128]{1,0:T(8,128)S(1)}, f32[192,128]{1,0:T(8,128)S(1)}, u32[]{:S(2)}, u32[]{:S(2)}) collective-permute-start(f32[192,128]{1,0:T(8,128)S(1)} %get-tuple-element.35.a0), channel_id=1, source_target_pairs={{0,24},{8,0},{16,8},{24,16},{1,25},{9,1},{17,9},{25,17},{2,26},{10... | collective-permute-start | bytes 294920 | tf_op jit(solution)/shard_map/ppermute | solution.py:691
  68.9 6.2 %all-to-all-start.3 = ((f32[128,1,128]{2,1,0:T(1,128)}), f32[128,1,128]{2,1,0:T(1,128)S(1)}, u32[]{:S(2)}, u32[]{:S(2)}) async-start(f32[128,1,128]{2,1,0:T(1,128)} %get-tuple-element.28), calls=%async_computation.3 | async-start | bytes 131072 | tf_op jit(solution)/shard_map/all_to_all | solution.py:688
  75.2 4.3 %solve1.1 = (f32[4608,128]{1,0:T(8,128)S(1)}, f32[9216,128]{1,0:T(8,128)}) custom-call(f32[4608,128]{1,0:T(8,128)S(1)} %get-tuple-element.29.refs_0_, f32[2304,128]{1,0:T(8,128)} %get-tuple-element.22.refs_2_.refs_1_, f32[2240,128]{1,0:T(8,128)} %bitcast.19, f32[576,128]{1,0:T(8,128)} %get-tuple-element.30.refs_3_, ...), custom_call_target="tpu_custom_call", output_to_operand_aliasing={{0}: (0, {}), {1}: (4, {})} | custom-call | tf_op jit(solution)/shard_map/solve1/pallas_call | solution.py:514
  79.5 4.7 %all-to-all-done.3 = f32[128,1,128]{2,1,0:T(1,128)S(1)} async-done(((f32[128,1,128]{2,1,0:T(1,128)}), f32[128,1,128]{2,1,0:T(1,128)S(1)}, u32[]{:S(2)}, u32[]{:S(2)}) %all-to-all-start.3) | async-done | bytes 65568 | tf_op jit(solution)/shard_map/all_to_all | solution.py:688
  84.2 0.0 collective-permute-done.a1
  84.2 0.0 collective-permute-done.1.a2
  84.2 0.0 collective-permute-done.2.a3
  84.2 0.8 combine.1
  85.0 0.8 collective-permute-start.3
  85.8 1.7 %collective-permute-start.4 = (f32[128,128]{1,0:T(8,128)S(1)}, f32[128,128]{1,0:T(8,128)S(1)}, u32[]{:S(2)}, u32[]{:S(2)}) collective-permute-start(f32[128,128]{1,0:T(8,128)S(1)} %get-tuple-element.38), channel_id=1, source_target_pairs={{0,64},{32,96},{64,0},{96,32},{1,65},{33,97},{65,1},{97,33},{2,66}... | collective-permute-start | bytes 196616 | tf_op jit(solution)/shard_map/ppermute | solution.py:694
  87.5 1.8 %collective-permute-start.5 = (f32[128,128]{1,0:T(8,128)S(1)}, f32[128,128]{1,0:T(8,128)S(1)}, u32[]{:S(2)}, u32[]{:S(2)}) collective-permute-start(f32[128,128]{1,0:T(8,128)S(1)} %get-tuple-element.39), channel_id=1, source_target_pairs={{0,96},{32,0},{64,32},{96,64},{1,97},{33,1},{65,33},{97,65},{2,98}... | collective-permute-start | bytes 196616 | tf_op jit(solution)/shard_map/ppermute | solution.py:694
  89.3 2.4 %collective-permute-done.3.a1 = f32[128,128]{1,0:T(8,128)S(1)} collective-permute-done((f32[128,128]{1,0:T(8,128)S(1)}, f32[128,128]{1,0:T(8,128)S(1)}, u32[]{:S(2)}, u32[]{:S(2)}) %collective-permute-start.3) | collective-permute-done | bytes 65568 | tf_op jit(solution)/shard_map/ppermute | solution.py:694
  91.7 0.0 collective-permute-done.4.a2
  91.7 0.4 collective-permute-done.5.a3
  92.1 1.2 %place.1 = f32[2,64,128]{2,1,0:T(8,128)} custom-call(s32[146]{0:T(256)S(1)} %plan.1.refs_0_, f32[128,128]{1,0:T(8,128)S(1)} %get-tuple-element.36.a0, f32[128,128]{1,0:T(8,128)S(1)} %collective-permute-done.3.a1, f32[128,128]{1,0:T(8,128)S(1)} %collective-permute-done.4.a2, f32[128,128]{1,0:T(8,128)S(1)} %collective-permute-done.5.a3), custom_call_target="tpu_custom_call" | custom-call | tf_op jit(solution)/shard_map/place/pallas_call | solution.py:675
  (2 shorter events, 0.0 us)
Async XLA Ops:
  0.6 15.5 %copy-start = (s32[8,16]{1,0:T(8,128)S(1)}, s32[8,16]{1,0:T(8,128)}, u32[]{:S(2)}) copy-start(s32[8,16]{1,0:T(8,128)} %clinic.1) | copy-start | bytes 1540
  0.6 15.5 %copy-start.1 = (s32[8,32]{1,0:T(8,128)S(1)}, s32[8,32]{1,0:T(8,128)}, u32[]{:S(2)}) copy-start(s32[8,32]{1,0:T(8,128)} %tropic.1) | copy-start | bytes 3076
  4.9 21.4 %all-to-all-start = ((f32[128,4,128]{2,1,0:T(4,128)}), f32[128,4,128]{2,1,0:T(4,128)S(1)}, u32[]{:S(2)}, u32[]{:S(2)}) async-start(f32[128,4,128]{2,1,0:T(4,128)} %bitcast.21), calls=%async_computation | async-start | bytes 524288 | tf_op jit(solution)/shard_map/all_to_all | solution.py:688
  27.8 15.0 %all-to-all-start.1 = ((f32[128,4,128]{2,1,0:T(4,128)}), f32[128,4,128]{2,1,0:T(4,128)S(1)}, u32[]{:S(2)}, u32[]{:S(2)}) async-start(f32[128,4,128]{2,1,0:T(4,128)} %select.1), calls=%async_computation.1 | async-start | bytes 524288 | tf_op jit(solution)/shard_map/all_to_all | solution.py:688
  47.3 15.8 %all-to-all-start.2 = ((f32[128,4,128]{2,1,0:T(4,128)}), f32[128,4,128]{2,1,0:T(4,128)S(1)}, u32[]{:S(2)}, u32[]{:S(2)}) async-start(f32[128,4,128]{2,1,0:T(4,128)} %get-tuple-element.24), calls=%async_computation.2 | async-start | bytes 524288 | tf_op jit(solution)/shard_map/all_to_all | solution.py:688
  64.9 19.3 %collective-permute-start = (f32[192,128]{1,0:T(8,128)S(1)}, f32[192,128]{1,0:T(8,128)S(1)}, u32[]{:S(2)}, u32[]{:S(2)}) collective-permute-start(f32[192,128]{1,0:T(8,128)S(1)} %get-tuple-element.35.a0), channel_id=1, source_target_pairs={{0,8},{8,16},{16,24},{24,0},{1,9},{9,17},{17,25},{25,1},{2,10},{10... | collective-permute-start | bytes 294920 | tf_op jit(solution)/shard_map/ppermute | solution.py:691
  65.6 18.6 %collective-permute-start.1 = (f32[192,128]{1,0:T(8,128)S(1)}, f32[192,128]{1,0:T(8,128)S(1)}, u32[]{:S(2)}, u32[]{:S(2)}) collective-permute-start(f32[192,128]{1,0:T(8,128)S(1)} %get-tuple-element.35.a0), channel_id=1, source_target_pairs={{0,16},{8,24},{16,0},{24,8},{1,17},{9,25},{17,1},{25,9},{2,18},{10... | collective-permute-start | bytes 294920 | tf_op jit(solution)/shard_map/ppermute | solution.py:691
  67.9 16.4 %collective-permute-start.2 = (f32[192,128]{1,0:T(8,128)S(1)}, f32[192,128]{1,0:T(8,128)S(1)}, u32[]{:S(2)}, u32[]{:S(2)}) collective-permute-start(f32[192,128]{1,0:T(8,128)S(1)} %get-tuple-element.35.a0), channel_id=1, source_target_pairs={{0,24},{8,0},{16,8},{24,16},{1,25},{9,1},{17,9},{25,17},{2,26},{10... | collective-permute-start | bytes 294920 | tf_op jit(solution)/shard_map/ppermute | solution.py:691
  68.9 15.3 %all-to-all-start.3 = ((f32[128,1,128]{2,1,0:T(1,128)}), f32[128,1,128]{2,1,0:T(1,128)S(1)}, u32[]{:S(2)}, u32[]{:S(2)}) async-start(f32[128,1,128]{2,1,0:T(1,128)} %get-tuple-element.28), calls=%async_computation.3 | async-start | bytes 131072 | tf_op jit(solution)/shard_map/all_to_all | solution.py:688
  85.0 6.7 %collective-permute-start.3 = (f32[128,128]{1,0:T(8,128)S(1)}, f32[128,128]{1,0:T(8,128)S(1)}, u32[]{:S(2)}, u32[]{:S(2)}) collective-permute-start(f32[128,128]{1,0:T(8,128)S(1)} %get-tuple-element.37), channel_id=1, source_target_pairs={{0,32},{32,64},{64,96},{96,0},{1,33},{33,65},{65,97},{97,1},{2,34}... | collective-permute-start | bytes 196616 | tf_op jit(solution)/shard_map/ppermute | solution.py:694
  85.8 5.9 %collective-permute-start.4 = (f32[128,128]{1,0:T(8,128)S(1)}, f32[128,128]{1,0:T(8,128)S(1)}, u32[]{:S(2)}, u32[]{:S(2)}) collective-permute-start(f32[128,128]{1,0:T(8,128)S(1)} %get-tuple-element.38), channel_id=1, source_target_pairs={{0,64},{32,96},{64,0},{96,32},{1,65},{33,97},{65,1},{97,33},{2,66}... | collective-permute-start | bytes 196616 | tf_op jit(solution)/shard_map/ppermute | solution.py:694
  87.5 4.6 %collective-permute-start.5 = (f32[128,128]{1,0:T(8,128)S(1)}, f32[128,128]{1,0:T(8,128)S(1)}, u32[]{:S(2)}, u32[]{:S(2)}) collective-permute-start(f32[128,128]{1,0:T(8,128)S(1)} %get-tuple-element.39), channel_id=1, source_target_pairs={{0,96},{32,0},{64,32},{96,64},{1,97},{33,1},{65,33},{97,65},{2,98}... | collective-permute-start | bytes 196616 | tf_op jit(solution)/shard_map/ppermute | solution.py:694

commit v5 on v4

--- a/solution.py
+++ b/solution.py
@@ -713,14 +713,14 @@
     first_two, inv = in_vmem(first_two), in_hbm(inv)
     scattered = every(own.reshape(128, PART, BE))
     halo = every(select(plan, scattered)).reshape(ITEM, BE)
-    mixed, edge, base, items = solve(0, (plan, first_two, inv, mixing, in_hbm(own), halo, depth))
+    mixed, edge, base, items = solve(0, (plan, first_two, inv, mixing, in_hbm(own), halo, depth), chunk=36)
     got = every(items)
     edge = in_hbm(edge)
     last_two, new = stencil(1, (tracers, velocity, in_vmem(mixed)))
     got, last_two = lax.optimization_barrier((got, last_two))
     vectors, sums = krylov(plan, in_vmem(base), got)
     totals = every(sums)
-    _, new = solve(1, (in_vmem(last_two), inv, mixing, edge, in_hbm(new)))
+    _, new = solve(1, (in_vmem(last_two), inv, mixing, edge, in_hbm(new)), chunk=18)
     totals, new = lax.optimization_barrier((totals, new))
     line = [vectors] + [along_y(vectors, k) for k in range(1, side)]
     sends = combine(plan, totals.reshape(128, BE), line)

time: 93.7 us -> 93.6 us (level)
  no operation moved by 1% of the time
where the time goes in v5:
time: 93.6 us; the launch traced here: 93.3 us
  starting transfers between devices  36 us (38%)
  Pallas kernels  32.4 us (35%)
  waiting for transfers between devices  24.1 us (26%)
    all_to_all x4, starting transfers between devices, body(): every = lambda value: lax.all_to_all(value, EVERY, 0, 0)  27.7 us
    all_to_all x4, waiting for transfers between devices, body(): every = lambda value: lax.all_to_all(value, EVERY, 0, 0)  21.2 us
    pallas_call x2, Pallas kernels, stencil(): pl.pallas_call(functools.partial(stencil_kernel, group, chunk), out_shape...  12.2 us
    pallas_call x2, Pallas kernels, solve(): pl.pallas_call(functools.partial(solve_kernel, group, chunk, out_chunk),...  8.58 us
    ppermute x3, starting transfers between devices, along_z(): return lax.ppermute(value, 'z', [(z, (z + k) % side) for z in range(side)])  4.27 us
    pallas_call x1, Pallas kernels, pack(): pl.pallas_call(pack_kernel, out_shape=pltpu.HBM((ITEM, BE), F32), in_spec...  4.27 us
    ppermute x3, starting transfers between devices, along_y(): return lax.ppermute(value, 'y', [(y, (y + k) % side) for y in range(side)])  4.03 us
    ppermute x3, waiting for transfers between devices, along_z(): return lax.ppermute(value, 'z', [(z, (z + k) % side) for z in range(side)])  2.83 us
  transfers between devices with their start and end apart: 10, of which 6 were waited for; matrix products, arithmetic and copies ran while one was open for 0% of the time, Pallas kernels for 20%

profile of v5, /device:TPU:0, one launch (start us, length us, event | category | flops | bytes accessed | tf_op | source)
XLA Modules:
  0.0 93.3 jit_solution(4262965217355175826)
XLA Ops:
  0.6 4.3 %pack.1.refs_4_ = f32[512,128]{1,0:T(8,128)} custom-call(f32[9216,128]{1,0:T(8,128)} %bitcast.11, f32[4608,128]{1,0:T(8,128)} %bitcast.14, f32[64,128]{1,0:T(8,128)} %bitcast.22), custom_call_target="tpu_custom_call" | custom-call | tf_op jit(solution)/shard_map/pack/pallas_call | solution.py:181
  4.9 11.1 %all-to-all-start = ((f32[128,4,128]{2,1,0:T(4,128)}), f32[128,4,128]{2,1,0:T(4,128)S(1)}, u32[]{:S(2)}, u32[]{:S(2)}) async-start(f32[128,4,128]{2,1,0:T(4,128)} %bitcast.21), calls=%async_computation | async-start | bytes 524288 | tf_op jit(solution)/shard_map/all_to_all | solution.py:688
  16.1 0.0 copy-done
  16.1 0.0 copy-done.1
  16.1 2.2 %plan.1.refs_0_ = s32[146]{0:T(256)S(1)} custom-call(s32[8,16]{1,0:T(8,128)S(1)} %copy-done, s32[8,32]{1,0:T(8,128)S(1)} %copy-done.1), custom_call_target="tpu_custom_call" | custom-call | tf_op jit(solution)/shard_map/plan/pallas_call | solution.py:703
  18.3 8.1 %all-to-all-done.got = f32[128,4,128]{2,1,0:T(4,128)S(1)} async-done(((f32[128,4,128]{2,1,0:T(4,128)}), f32[128,4,128]{2,1,0:T(4,128)S(1)}, u32[]{:S(2)}, u32[]{:S(2)}) %all-to-all-start) | async-done | bytes 262176 | tf_op jit(solution)/shard_map/all_to_all | solution.py:688
  26.3 1.4 %select.1 = f32[128,4,128]{2,1,0:T(4,128)} custom-call(s32[146]{0:T(256)S(1)} %plan.1.refs_0_, f32[128,4,128]{2,1,0:T(4,128)S(1)} %all-to-all-done.got), custom_call_target="tpu_custom_call" | custom-call | tf_op jit(solution)/shard_map/select/pallas_call | solution.py:215
  27.8 4.7 %all-to-all-start.1 = ((f32[128,4,128]{2,1,0:T(4,128)}), f32[128,4,128]{2,1,0:T(4,128)S(1)}, u32[]{:S(2)}, u32[]{:S(2)}) async-start(f32[128,4,128]{2,1,0:T(4,128)} %select.1), calls=%async_computation.1 | async-start | bytes 524288 | tf_op jit(solution)/shard_map/all_to_all | solution.py:688
  32.5 6.1 %stencil0.1 = (f32[4608,128]{1,0:T(8,128)S(1)}, f32[2304,128]{1,0:T(8,128)}) custom-call(f32[9216,128]{1,0:T(8,128)} %bitcast.12, f32[4608,128]{1,0:T(8,128)} %bitcast.15, f32[2240,128]{1,0:T(8,128)} %bitcast.17), custom_call_target="tpu_custom_call" | custom-call | tf_op jit(solution)/shard_map/stencil0/pallas_call | solution.py:345
  38.6 4.2 %all-to-all-done.1 = f32[128,4,128]{2,1,0:T(4,128)S(1)} async-done(((f32[128,4,128]{2,1,0:T(4,128)}), f32[128,4,128]{2,1,0:T(4,128)S(1)}, u32[]{:S(2)}, u32[]{:S(2)}) %all-to-all-start.1) | async-done | bytes 262176 | tf_op jit(solution)/shard_map/all_to_all | solution.py:688
  42.7 4.4 %solve0.1 = (f32[4608,128]{1,0:T(8,128)S(1)}, f32[576,128]{1,0:T(8,128)}, f32[144,128]{1,0:T(8,128)S(1)}, f32[128,4,128]{2,1,0:T(4,128)}) custom-call(s32[146]{0:T(256)S(1)} %plan.1.refs_0_, f32[4608,128]{1,0:T(8,128)S(1)} %get-tuple-element.21.refs_1_, f32[2304,128]{1,0:T(8,128)} %get-tuple-element.22.refs_2_.refs_1_, ...), custom_call_target="tpu_custom_call", output_to_operand_aliasing={{0}: (1, {})} | custom-call | tf_op jit(solution)/shard_map/solve0/pallas_call | solution.py:514
  47.2 5.6 %all-to-all-start.2 = ((f32[128,4,128]{2,1,0:T(4,128)}), f32[128,4,128]{2,1,0:T(4,128)S(1)}, u32[]{:S(2)}, u32[]{:S(2)}) async-start(f32[128,4,128]{2,1,0:T(4,128)} %get-tuple-element.24), calls=%async_computation.2 | async-start | bytes 524288 | tf_op jit(solution)/shard_map/all_to_all | solution.py:688
  52.8 6.1 %stencil1.1 = (f32[4608,128]{1,0:T(8,128)S(1)}, f32[9216,128]{1,0:T(8,128)}) custom-call(f32[9216,128]{1,0:T(8,128)} %bitcast.13, f32[4608,128]{1,0:T(8,128)} %bitcast.16, f32[4608,128]{1,0:T(8,128)S(1)} %get-tuple-element.25.refs_2_), custom_call_target="tpu_custom_call", output_to_operand_aliasing={{0}: (2, {})} | custom-call | tf_op jit(solution)/shard_map/stencil1/pallas_call | solution.py:345
  58.9 4.1 %all-to-all-done.2.got = f32[128,4,128]{2,1,0:T(4,128)S(1)} async-done(((f32[128,4,128]{2,1,0:T(4,128)}), f32[128,4,128]{2,1,0:T(4,128)S(1)}, u32[]{:S(2)}, u32[]{:S(2)}) %all-to-all-start.2) | async-done | bytes 262176 | tf_op jit(solution)/shard_map/all_to_all | solution.py:688
  63.0 1.8 %krylov.1 = (f32[192,128]{1,0:T(8,128)S(1)}, f32[128,1,128]{2,1,0:T(1,128)}) custom-call(s32[146]{0:T(256)S(1)} %plan.1.refs_0_, f32[144,128]{1,0:T(8,128)S(1)} %get-tuple-element.23.base, f32[128,4,128]{2,1,0:T(4,128)S(1)} %all-to-all-done.2.got), custom_call_target="tpu_custom_call" | custom-call | tf_op jit(solution)/shard_map/krylov/pallas_call | solution.py:600
  64.8 0.7 collective-permute-start
  65.5 2.3 %collective-permute-start.1 = (f32[192,128]{1,0:T(8,128)S(1)}, f32[192,128]{1,0:T(8,128)S(1)}, u32[]{:S(2)}, u32[]{:S(2)}) collective-permute-start(f32[192,128]{1,0:T(8,128)S(1)} %get-tuple-element.35.a0), channel_id=1, source_target_pairs={{0,16},{8,24},{16,0},{24,8},{1,17},{9,25},{17,1},{25,9},{2,18},{10... | collective-permute-start | bytes 294920 | tf_op jit(solution)/shard_map/ppermute | solution.py:691
  67.8 1.1 %collective-permute-start.2 = (f32[192,128]{1,0:T(8,128)S(1)}, f32[192,128]{1,0:T(8,128)S(1)}, u32[]{:S(2)}, u32[]{:S(2)}) collective-permute-start(f32[192,128]{1,0:T(8,128)S(1)} %get-tuple-element.35.a0), channel_id=1, source_target_pairs={{0,24},{8,0},{16,8},{24,16},{1,25},{9,1},{17,9},{25,17},{2,26},{10... | collective-permute-start | bytes 294920 | tf_op jit(solution)/shard_map/ppermute | solution.py:691
  68.9 6.2 %all-to-all-start.3 = ((f32[128,1,128]{2,1,0:T(1,128)}), f32[128,1,128]{2,1,0:T(1,128)S(1)}, u32[]{:S(2)}, u32[]{:S(2)}) async-start(f32[128,1,128]{2,1,0:T(1,128)} %get-tuple-element.28), calls=%async_computation.3 | async-start | bytes 131072 | tf_op jit(solution)/shard_map/all_to_all | solution.py:688
  75.1 4.1 %solve1.1 = (f32[4608,128]{1,0:T(8,128)S(1)}, f32[9216,128]{1,0:T(8,128)}) custom-call(f32[4608,128]{1,0:T(8,128)S(1)} %get-tuple-element.29.refs_0_, f32[2304,128]{1,0:T(8,128)} %get-tuple-element.22.refs_2_.refs_1_, f32[2240,128]{1,0:T(8,128)} %bitcast.19, f32[576,128]{1,0:T(8,128)} %get-tuple-element.30.refs_3_, ...), custom_call_target="tpu_custom_call", output_to_operand_aliasing={{0}: (0, {}), {1}: (4, {})} | custom-call | tf_op jit(solution)/shard_map/solve1/pallas_call | solution.py:514
  79.2 4.9 %all-to-all-done.3 = f32[128,1,128]{2,1,0:T(1,128)S(1)} async-done(((f32[128,1,128]{2,1,0:T(1,128)}), f32[128,1,128]{2,1,0:T(1,128)S(1)}, u32[]{:S(2)}, u32[]{:S(2)}) %all-to-all-start.3) | async-done | bytes 65568 | tf_op jit(solution)/shard_map/all_to_all | solution.py:688
  84.1 0.0 collective-permute-done.a1
  84.1 0.0 collective-permute-done.1.a2
  84.1 0.0 collective-permute-done.2.a3
  84.2 0.8 combine.1
  85.0 0.8 collective-permute-start.3
  85.7 1.7 %collective-permute-start.4 = (f32[128,128]{1,0:T(8,128)S(1)}, f32[128,128]{1,0:T(8,128)S(1)}, u32[]{:S(2)}, u32[]{:S(2)}) collective-permute-start(f32[128,128]{1,0:T(8,128)S(1)} %get-tuple-element.38), channel_id=1, source_target_pairs={{0,64},{32,96},{64,0},{96,32},{1,65},{33,97},{65,1},{97,33},{2,66}... | collective-permute-start | bytes 196616 | tf_op jit(solution)/shard_map/ppermute | solution.py:694
  87.4 1.8 %collective-permute-start.5 = (f32[128,128]{1,0:T(8,128)S(1)}, f32[128,128]{1,0:T(8,128)S(1)}, u32[]{:S(2)}, u32[]{:S(2)}) collective-permute-start(f32[128,128]{1,0:T(8,128)S(1)} %get-tuple-element.39), channel_id=1, source_target_pairs={{0,96},{32,0},{64,32},{96,64},{1,97},{33,1},{65,33},{97,65},{2,98}... | collective-permute-start | bytes 196616 | tf_op jit(solution)/shard_map/ppermute | solution.py:694
  89.2 2.4 %collective-permute-done.3.a1 = f32[128,128]{1,0:T(8,128)S(1)} collective-permute-done((f32[128,128]{1,0:T(8,128)S(1)}, f32[128,128]{1,0:T(8,128)S(1)}, u32[]{:S(2)}, u32[]{:S(2)}) %collective-permute-start.3) | collective-permute-done | bytes 65568 | tf_op jit(solution)/shard_map/ppermute | solution.py:694
  91.6 0.0 collective-permute-done.4.a2
  91.6 0.4 collective-permute-done.5.a3
  92.1 1.2 %place.1 = f32[2,64,128]{2,1,0:T(8,128)} custom-call(s32[146]{0:T(256)S(1)} %plan.1.refs_0_, f32[128,128]{1,0:T(8,128)S(1)} %get-tuple-element.36.a0, f32[128,128]{1,0:T(8,128)S(1)} %collective-permute-done.3.a1, f32[128,128]{1,0:T(8,128)S(1)} %collective-permute-done.4.a2, f32[128,128]{1,0:T(8,128)S(1)} %collective-permute-done.5.a3), custom_call_target="tpu_custom_call" | custom-call | tf_op jit(solution)/shard_map/place/pallas_call | solution.py:675
  (2 shorter events, 0.0 us)
Async XLA Ops:
  0.6 15.5 %copy-start = (s32[8,16]{1,0:T(8,128)S(1)}, s32[8,16]{1,0:T(8,128)}, u32[]{:S(2)}) copy-start(s32[8,16]{1,0:T(8,128)} %clinic.1) | copy-start | bytes 1540
  0.6 15.5 %copy-start.1 = (s32[8,32]{1,0:T(8,128)S(1)}, s32[8,32]{1,0:T(8,128)}, u32[]{:S(2)}) copy-start(s32[8,32]{1,0:T(8,128)} %tropic.1) | copy-start | bytes 3076
  4.9 21.4 %all-to-all-start = ((f32[128,4,128]{2,1,0:T(4,128)}), f32[128,4,128]{2,1,0:T(4,128)S(1)}, u32[]{:S(2)}, u32[]{:S(2)}) async-start(f32[128,4,128]{2,1,0:T(4,128)} %bitcast.21), calls=%async_computation | async-start | bytes 524288 | tf_op jit(solution)/shard_map/all_to_all | solution.py:688
  27.8 15.0 %all-to-all-start.1 = ((f32[128,4,128]{2,1,0:T(4,128)}), f32[128,4,128]{2,1,0:T(4,128)S(1)}, u32[]{:S(2)}, u32[]{:S(2)}) async-start(f32[128,4,128]{2,1,0:T(4,128)} %select.1), calls=%async_computation.1 | async-start | bytes 524288 | tf_op jit(solution)/shard_map/all_to_all | solution.py:688
  47.2 15.8 %all-to-all-start.2 = ((f32[128,4,128]{2,1,0:T(4,128)}), f32[128,4,128]{2,1,0:T(4,128)S(1)}, u32[]{:S(2)}, u32[]{:S(2)}) async-start(f32[128,4,128]{2,1,0:T(4,128)} %get-tuple-element.24), calls=%async_computation.2 | async-start | bytes 524288 | tf_op jit(solution)/shard_map/all_to_all | solution.py:688
  64.8 19.3 %collective-permute-start = (f32[192,128]{1,0:T(8,128)S(1)}, f32[192,128]{1,0:T(8,128)S(1)}, u32[]{:S(2)}, u32[]{:S(2)}) collective-permute-start(f32[192,128]{1,0:T(8,128)S(1)} %get-tuple-element.35.a0), channel_id=1, source_target_pairs={{0,8},{8,16},{16,24},{24,0},{1,9},{9,17},{17,25},{25,1},{2,10},{10... | collective-permute-start | bytes 294920 | tf_op jit(solution)/shard_map/ppermute | solution.py:691
  65.5 18.6 %collective-permute-start.1 = (f32[192,128]{1,0:T(8,128)S(1)}, f32[192,128]{1,0:T(8,128)S(1)}, u32[]{:S(2)}, u32[]{:S(2)}) collective-permute-start(f32[192,128]{1,0:T(8,128)S(1)} %get-tuple-element.35.a0), channel_id=1, source_target_pairs={{0,16},{8,24},{16,0},{24,8},{1,17},{9,25},{17,1},{25,9},{2,18},{10... | collective-permute-start | bytes 294920 | tf_op jit(solution)/shard_map/ppermute | solution.py:691
  67.8 16.4 %collective-permute-start.2 = (f32[192,128]{1,0:T(8,128)S(1)}, f32[192,128]{1,0:T(8,128)S(1)}, u32[]{:S(2)}, u32[]{:S(2)}) collective-permute-start(f32[192,128]{1,0:T(8,128)S(1)} %get-tuple-element.35.a0), channel_id=1, source_target_pairs={{0,24},{8,0},{16,8},{24,16},{1,25},{9,1},{17,9},{25,17},{2,26},{10... | collective-permute-start | bytes 294920 | tf_op jit(solution)/shard_map/ppermute | solution.py:691
  68.9 15.3 %all-to-all-start.3 = ((f32[128,1,128]{2,1,0:T(1,128)}), f32[128,1,128]{2,1,0:T(1,128)S(1)}, u32[]{:S(2)}, u32[]{:S(2)}) async-start(f32[128,1,128]{2,1,0:T(1,128)} %get-tuple-element.28), calls=%async_computation.3 | async-start | bytes 131072 | tf_op jit(solution)/shard_map/all_to_all | solution.py:688
  85.0 6.7 %collective-permute-start.3 = (f32[128,128]{1,0:T(8,128)S(1)}, f32[128,128]{1,0:T(8,128)S(1)}, u32[]{:S(2)}, u32[]{:S(2)}) collective-permute-start(f32[128,128]{1,0:T(8,128)S(1)} %get-tuple-element.37), channel_id=1, source_target_pairs={{0,32},{32,64},{64,96},{96,0},{1,33},{33,65},{65,97},{97,1},{2,34}... | collective-permute-start | bytes 196616 | tf_op jit(solution)/shard_map/ppermute | solution.py:694
  85.7 5.9 %collective-permute-start.4 = (f32[128,128]{1,0:T(8,128)S(1)}, f32[128,128]{1,0:T(8,128)S(1)}, u32[]{:S(2)}, u32[]{:S(2)}) collective-permute-start(f32[128,128]{1,0:T(8,128)S(1)} %get-tuple-element.38), channel_id=1, source_target_pairs={{0,64},{32,96},{64,0},{96,32},{1,65},{33,97},{65,1},{97,33},{2,66}... | collective-permute-start | bytes 196616 | tf_op jit(solution)/shard_map/ppermute | solution.py:694
  87.4 4.6 %collective-permute-start.5 = (f32[128,128]{1,0:T(8,128)S(1)}, f32[128,128]{1,0:T(8,128)S(1)}, u32[]{:S(2)}, u32[]{:S(2)}) collective-permute-start(f32[128,128]{1,0:T(8,128)S(1)} %get-tuple-element.39), channel_id=1, source_target_pairs={{0,96},{32,0},{64,32},{96,64},{1,97},{33,1},{65,33},{97,65},{2,98}... | collective-permute-start | bytes 196616 | tf_op jit(solution)/shard_map/ppermute | solution.py:694

commit v6 on v5

--- a/solution.py
+++ b/solution.py
@@ -719,7 +719,7 @@
     last_two, new = stencil(1, (tracers, velocity, in_vmem(mixed)))
     got, last_two = lax.optimization_barrier((got, last_two))
     vectors, sums = krylov(plan, in_vmem(base), got)
-    totals = every(sums)
+    totals = lax.all_to_all(sums, ("c", "x", "y", "z"), 0, 0)
     _, new = solve(1, (in_vmem(last_two), inv, mixing, edge, in_hbm(new)), chunk=18)
     totals, new = lax.optimization_barrier((totals, new))
     line = [vectors] + [along_y(vectors, k) for k in range(1, side)]

time: 93.6 us -> 93.5 us (level)
    all_to_all x4 -> x3, starting transfers between devices: 27.7 us -> 21.5 us  [body(): every = lambda value: lax.all_to_all(value, EVERY, 0, 0)]
    all_to_all x0 -> x1, starting transfers between devices: none -> 6.23 us  [body(): totals = lax.all_to_all(sums, ('c', 'x', 'y', 'z'), 0, 0)]
    all_to_all x4 -> x3, waiting for transfers between devices: 21.2 us -> 16.4 us  [body(): every = lambda value: lax.all_to_all(value, EVERY, 0, 0)]
    all_to_all x0 -> x1, waiting for transfers between devices: none -> 4.77 us  [body(): totals = lax.all_to_all(sums, ('c', 'x', 'y', 'z'), 0, 0)]
where the time goes in v6:
time: 93.5 us; the launch traced here: 93.1 us
  starting transfers between devices  36 us (39%)
  Pallas kernels  32.4 us (35%)
  waiting for transfers between devices  24 us (26%)
    all_to_all x3, starting transfers between devices, body(): every = lambda value: lax.all_to_all(value, EVERY, 0, 0)  21.5 us
    all_to_all x3, waiting for transfers between devices, body(): every = lambda value: lax.all_to_all(value, EVERY, 0, 0)  16.4 us
    pallas_call x2, Pallas kernels, stencil(): pl.pallas_call(functools.partial(stencil_kernel, group, chunk), out_shape...  12.2 us
    pallas_call x2, Pallas kernels, solve(): pl.pallas_call(functools.partial(solve_kernel, group, chunk, out_chunk),...  8.58 us
    all_to_all x1, starting transfers between devices, body(): totals = lax.all_to_all(sums, ('c', 'x', 'y', 'z'), 0, 0)  6.23 us
    all_to_all x1, waiting for transfers between devices, body(): totals = lax.all_to_all(sums, ('c', 'x', 'y', 'z'), 0, 0)  4.77 us
    pallas_call x1, Pallas kernels, pack(): pl.pallas_call(pack_kernel, out_shape=pltpu.HBM((ITEM, BE), F32), in_spec...  4.27 us
    ppermute x3, starting transfers between devices, along_z(): return lax.ppermute(value, 'z', [(z, (z + k) % side) for z in range(side)])  4.22 us
  transfers between devices with their start and end apart: 10, of which 6 were waited for; matrix products, arithmetic and copies ran while one was open for 0% of the time, Pallas kernels for 20%

profile of v6, /device:TPU:0, one launch (start us, length us, event | category | flops | bytes accessed | tf_op | source)
XLA Modules:
  0.0 93.1 jit_solution(12424296279469017281)
XLA Ops:
  0.6 4.3 %pack.1.refs_4_ = f32[512,128]{1,0:T(8,128)} custom-call(f32[9216,128]{1,0:T(8,128)} %bitcast.11, f32[4608,128]{1,0:T(8,128)} %bitcast.14, f32[64,128]{1,0:T(8,128)} %bitcast.22), custom_call_target="tpu_custom_call" | custom-call | tf_op jit(solution)/shard_map/pack/pallas_call | solution.py:181
  4.9 11.1 %all-to-all-start = ((f32[128,4,128]{2,1,0:T(4,128)}), f32[128,4,128]{2,1,0:T(4,128)S(1)}, u32[]{:S(2)}, u32[]{:S(2)}) async-start(f32[128,4,128]{2,1,0:T(4,128)} %bitcast.21), calls=%async_computation | async-start | bytes 524288 | tf_op jit(solution)/shard_map/all_to_all | solution.py:688
  16.1 0.0 copy-done
  16.1 0.0 copy-done.1
  16.1 2.2 %plan.1.refs_0_ = s32[146]{0:T(256)S(1)} custom-call(s32[8,16]{1,0:T(8,128)S(1)} %copy-done, s32[8,32]{1,0:T(8,128)S(1)} %copy-done.1), custom_call_target="tpu_custom_call" | custom-call | tf_op jit(solution)/shard_map/plan/pallas_call | solution.py:703
  18.3 8.1 %all-to-all-done.got = f32[128,4,128]{2,1,0:T(4,128)S(1)} async-done(((f32[128,4,128]{2,1,0:T(4,128)}), f32[128,4,128]{2,1,0:T(4,128)S(1)}, u32[]{:S(2)}, u32[]{:S(2)}) %all-to-all-start) | async-done | bytes 262176 | tf_op jit(solution)/shard_map/all_to_all | solution.py:688
  26.3 1.4 %select.1 = f32[128,4,128]{2,1,0:T(4,128)} custom-call(s32[146]{0:T(256)S(1)} %plan.1.refs_0_, f32[128,4,128]{2,1,0:T(4,128)S(1)} %all-to-all-done.got), custom_call_target="tpu_custom_call" | custom-call | tf_op jit(solution)/shard_map/select/pallas_call | solution.py:215
  27.8 4.7 %all-to-all-start.1 = ((f32[128,4,128]{2,1,0:T(4,128)}), f32[128,4,128]{2,1,0:T(4,128)S(1)}, u32[]{:S(2)}, u32[]{:S(2)}) async-start(f32[128,4,128]{2,1,0:T(4,128)} %select.1), calls=%async_computation.1 | async-start | bytes 524288 | tf_op jit(solution)/shard_map/all_to_all | solution.py:688
  32.5 6.1 %stencil0.1 = (f32[4608,128]{1,0:T(8,128)S(1)}, f32[2304,128]{1,0:T(8,128)}) custom-call(f32[9216,128]{1,0:T(8,128)} %bitcast.12, f32[4608,128]{1,0:T(8,128)} %bitcast.15, f32[2240,128]{1,0:T(8,128)} %bitcast.17), custom_call_target="tpu_custom_call" | custom-call | tf_op jit(solution)/shard_map/stencil0/pallas_call | solution.py:345
  38.6 4.2 %all-to-all-done.1 = f32[128,4,128]{2,1,0:T(4,128)S(1)} async-done(((f32[128,4,128]{2,1,0:T(4,128)}), f32[128,4,128]{2,1,0:T(4,128)S(1)}, u32[]{:S(2)}, u32[]{:S(2)}) %all-to-all-start.1) | async-done | bytes 262176 | tf_op jit(solution)/shard_map/all_to_all | solution.py:688
  42.7 4.4 %solve0.1 = (f32[4608,128]{1,0:T(8,128)S(1)}, f32[576,128]{1,0:T(8,128)}, f32[144,128]{1,0:T(8,128)S(1)}, f32[128,4,128]{2,1,0:T(4,128)}) custom-call(s32[146]{0:T(256)S(1)} %plan.1.refs_0_, f32[4608,128]{1,0:T(8,128)S(1)} %get-tuple-element.21.refs_1_, f32[2304,128]{1,0:T(8,128)} %get-tuple-element.22.refs_2_.refs_1_, ...), custom_call_target="tpu_custom_call", output_to_operand_aliasing={{0}: (1, {})} | custom-call | tf_op jit(solution)/shard_map/solve0/pallas_call | solution.py:514
  47.2 5.6 %all-to-all-start.2 = ((f32[128,4,128]{2,1,0:T(4,128)}), f32[128,4,128]{2,1,0:T(4,128)S(1)}, u32[]{:S(2)}, u32[]{:S(2)}) async-start(f32[128,4,128]{2,1,0:T(4,128)} %get-tuple-element.24), calls=%async_computation.2 | async-start | bytes 524288 | tf_op jit(solution)/shard_map/all_to_all | solution.py:688
  52.8 6.1 %stencil1.1 = (f32[4608,128]{1,0:T(8,128)S(1)}, f32[9216,128]{1,0:T(8,128)}) custom-call(f32[9216,128]{1,0:T(8,128)} %bitcast.13, f32[4608,128]{1,0:T(8,128)} %bitcast.16, f32[4608,128]{1,0:T(8,128)S(1)} %get-tuple-element.25.refs_2_), custom_call_target="tpu_custom_call", output_to_operand_aliasing={{0}: (2, {})} | custom-call | tf_op jit(solution)/shard_map/stencil1/pallas_call | solution.py:345
  58.9 4.1 %all-to-all-done.2.got = f32[128,4,128]{2,1,0:T(4,128)S(1)} async-done(((f32[128,4,128]{2,1,0:T(4,128)}), f32[128,4,128]{2,1,0:T(4,128)S(1)}, u32[]{:S(2)}, u32[]{:S(2)}) %all-to-all-start.2) | async-done | bytes 262176 | tf_op jit(solution)/shard_map/all_to_all | solution.py:688
  63.0 1.8 %krylov.1 = (f32[192,128]{1,0:T(8,128)S(1)}, f32[128,1,128]{2,1,0:T(1,128)}) custom-call(s32[146]{0:T(256)S(1)} %plan.1.refs_0_, f32[144,128]{1,0:T(8,128)S(1)} %get-tuple-element.23.base, f32[128,4,128]{2,1,0:T(4,128)S(1)} %all-to-all-done.2.got), custom_call_target="tpu_custom_call" | custom-call | tf_op jit(solution)/shard_map/krylov/pallas_call | solution.py:600
  64.8 0.7 collective-permute-start
  65.5 2.3 %collective-permute-start.1 = (f32[192,128]{1,0:T(8,128)S(1)}, f32[192,128]{1,0:T(8,128)S(1)}, u32[]{:S(2)}, u32[]{:S(2)}) collective-permute-start(f32[192,128]{1,0:T(8,128)S(1)} %get-tuple-element.35.a0), channel_id=1, source_target_pairs={{0,16},{8,24},{16,0},{24,8},{1,17},{9,25},{17,1},{25,9},{2,18},{10... | collective-permute-start | bytes 294920 | tf_op jit(solution)/shard_map/ppermute | solution.py:691
  67.8 1.1 %collective-permute-start.2 = (f32[192,128]{1,0:T(8,128)S(1)}, f32[192,128]{1,0:T(8,128)S(1)}, u32[]{:S(2)}, u32[]{:S(2)}) collective-permute-start(f32[192,128]{1,0:T(8,128)S(1)} %get-tuple-element.35.a0), channel_id=1, source_target_pairs={{0,24},{8,0},{16,8},{24,16},{1,25},{9,1},{17,9},{25,17},{2,26},{10... | collective-permute-start | bytes 294920 | tf_op jit(solution)/shard_map/ppermute | solution.py:691
  68.9 6.2 %all-to-all-start.3 = ((f32[128,1,128]{2,1,0:T(1,128)}), f32[128,1,128]{2,1,0:T(1,128)S(1)}, u32[]{:S(2)}, u32[]{:S(2)}) async-start(f32[128,1,128]{2,1,0:T(1,128)} %get-tuple-element.28), calls=%async_computation.3 | async-start | bytes 131072 | tf_op jit(solution)/shard_map/all_to_all | solution.py:722
  75.1 4.1 %solve1.1 = (f32[4608,128]{1,0:T(8,128)S(1)}, f32[9216,128]{1,0:T(8,128)}) custom-call(f32[4608,128]{1,0:T(8,128)S(1)} %get-tuple-element.29.refs_0_, f32[2304,128]{1,0:T(8,128)} %get-tuple-element.22.refs_2_.refs_1_, f32[2240,128]{1,0:T(8,128)} %bitcast.19, f32[576,128]{1,0:T(8,128)} %get-tuple-element.30.refs_3_, ...), custom_call_target="tpu_custom_call", output_to_operand_aliasing={{0}: (0, {}), {1}: (4, {})} | custom-call | tf_op jit(solution)/shard_map/solve1/pallas_call | solution.py:514
  79.2 4.8 %all-to-all-done.3 = f32[128,1,128]{2,1,0:T(1,128)S(1)} async-done(((f32[128,1,128]{2,1,0:T(1,128)}), f32[128,1,128]{2,1,0:T(1,128)S(1)}, u32[]{:S(2)}, u32[]{:S(2)}) %all-to-all-start.3) | async-done | bytes 65568 | tf_op jit(solution)/shard_map/all_to_all | solution.py:722
  84.0 0.0 collective-permute-done.a1
  84.0 0.0 collective-permute-done.1.a2
  84.0 0.0 collective-permute-done.2.a3
  84.0 0.8 combine.1
  84.8 0.9 collective-permute-start.3
  85.7 1.8 %collective-permute-start.4 = (f32[128,128]{1,0:T(8,128)S(1)}, f32[128,128]{1,0:T(8,128)S(1)}, u32[]{:S(2)}, u32[]{:S(2)}) collective-permute-start(f32[128,128]{1,0:T(8,128)S(1)} %get-tuple-element.38), channel_id=1, source_target_pairs={{0,64},{32,96},{64,0},{96,32},{1,65},{33,97},{65,1},{97,33},{2,66}... | collective-permute-start | bytes 196616 | tf_op jit(solution)/shard_map/ppermute | solution.py:694
  87.6 1.5 %collective-permute-start.5 = (f32[128,128]{1,0:T(8,128)S(1)}, f32[128,128]{1,0:T(8,128)S(1)}, u32[]{:S(2)}, u32[]{:S(2)}) collective-permute-start(f32[128,128]{1,0:T(8,128)S(1)} %get-tuple-element.39), channel_id=1, source_target_pairs={{0,96},{32,0},{64,32},{96,64},{1,97},{33,1},{65,33},{97,65},{2,98}... | collective-permute-start | bytes 196616 | tf_op jit(solution)/shard_map/ppermute | solution.py:694
  89.1 2.6 %collective-permute-done.3.a1 = f32[128,128]{1,0:T(8,128)S(1)} collective-permute-done((f32[128,128]{1,0:T(8,128)S(1)}, f32[128,128]{1,0:T(8,128)S(1)}, u32[]{:S(2)}, u32[]{:S(2)}) %collective-permute-start.3) | collective-permute-done | bytes 65568 | tf_op jit(solution)/shard_map/ppermute | solution.py:694
  91.6 0.0 collective-permute-done.4.a2
  91.6 0.3 collective-permute-done.5.a3
  91.9 1.2 %place.1 = f32[2,64,128]{2,1,0:T(8,128)} custom-call(s32[146]{0:T(256)S(1)} %plan.1.refs_0_, f32[128,128]{1,0:T(8,128)S(1)} %get-tuple-element.36.a0, f32[128,128]{1,0:T(8,128)S(1)} %collective-permute-done.3.a1, f32[128,128]{1,0:T(8,128)S(1)} %collective-permute-done.4.a2, f32[128,128]{1,0:T(8,128)S(1)} %collective-permute-done.5.a3), custom_call_target="tpu_custom_call" | custom-call | tf_op jit(solution)/shard_map/place/pallas_call | solution.py:675
  (2 shorter events, 0.0 us)
Async XLA Ops:
  0.6 15.5 %copy-start = (s32[8,16]{1,0:T(8,128)S(1)}, s32[8,16]{1,0:T(8,128)}, u32[]{:S(2)}) copy-start(s32[8,16]{1,0:T(8,128)} %clinic.1) | copy-start | bytes 1540
  0.6 15.5 %copy-start.1 = (s32[8,32]{1,0:T(8,128)S(1)}, s32[8,32]{1,0:T(8,128)}, u32[]{:S(2)}) copy-start(s32[8,32]{1,0:T(8,128)} %tropic.1) | copy-start | bytes 3076
  4.9 21.4 %all-to-all-start = ((f32[128,4,128]{2,1,0:T(4,128)}), f32[128,4,128]{2,1,0:T(4,128)S(1)}, u32[]{:S(2)}, u32[]{:S(2)}) async-start(f32[128,4,128]{2,1,0:T(4,128)} %bitcast.21), calls=%async_computation | async-start | bytes 524288 | tf_op jit(solution)/shard_map/all_to_all | solution.py:688
  27.8 15.0 %all-to-all-start.1 = ((f32[128,4,128]{2,1,0:T(4,128)}), f32[128,4,128]{2,1,0:T(4,128)S(1)}, u32[]{:S(2)}, u32[]{:S(2)}) async-start(f32[128,4,128]{2,1,0:T(4,128)} %select.1), calls=%async_computation.1 | async-start | bytes 524288 | tf_op jit(solution)/shard_map/all_to_all | solution.py:688
  47.2 15.8 %all-to-all-start.2 = ((f32[128,4,128]{2,1,0:T(4,128)}), f32[128,4,128]{2,1,0:T(4,128)S(1)}, u32[]{:S(2)}, u32[]{:S(2)}) async-start(f32[128,4,128]{2,1,0:T(4,128)} %get-tuple-element.24), calls=%async_computation.2 | async-start | bytes 524288 | tf_op jit(solution)/shard_map/all_to_all | solution.py:688
  64.8 19.2 %collective-permute-start = (f32[192,128]{1,0:T(8,128)S(1)}, f32[192,128]{1,0:T(8,128)S(1)}, u32[]{:S(2)}, u32[]{:S(2)}) collective-permute-start(f32[192,128]{1,0:T(8,128)S(1)} %get-tuple-element.35.a0), channel_id=1, source_target_pairs={{0,8},{8,16},{16,24},{24,0},{1,9},{9,17},{17,25},{25,1},{2,10},{10... | collective-permute-start | bytes 294920 | tf_op jit(solution)/shard_map/ppermute | solution.py:691
  65.5 18.5 %collective-permute-start.1 = (f32[192,128]{1,0:T(8,128)S(1)}, f32[192,128]{1,0:T(8,128)S(1)}, u32[]{:S(2)}, u32[]{:S(2)}) collective-permute-start(f32[192,128]{1,0:T(8,128)S(1)} %get-tuple-element.35.a0), channel_id=1, source_target_pairs={{0,16},{8,24},{16,0},{24,8},{1,17},{9,25},{17,1},{25,9},{2,18},{10... | collective-permute-start | bytes 294920 | tf_op jit(solution)/shard_map/ppermute | solution.py:691
  67.8 16.2 %collective-permute-start.2 = (f32[192,128]{1,0:T(8,128)S(1)}, f32[192,128]{1,0:T(8,128)S(1)}, u32[]{:S(2)}, u32[]{:S(2)}) collective-permute-start(f32[192,128]{1,0:T(8,128)S(1)} %get-tuple-element.35.a0), channel_id=1, source_target_pairs={{0,24},{8,0},{16,8},{24,16},{1,25},{9,1},{17,9},{25,17},{2,26},{10... | collective-permute-start | bytes 294920 | tf_op jit(solution)/shard_map/ppermute | solution.py:691
  68.9 15.2 %all-to-all-start.3 = ((f32[128,1,128]{2,1,0:T(1,128)}), f32[128,1,128]{2,1,0:T(1,128)S(1)}, u32[]{:S(2)}, u32[]{:S(2)}) async-start(f32[128,1,128]{2,1,0:T(1,128)} %get-tuple-element.28), calls=%async_computation.3 | async-start | bytes 131072 | tf_op jit(solution)/shard_map/all_to_all | solution.py:722
  84.8 6.8 %collective-permute-start.3 = (f32[128,128]{1,0:T(8,128)S(1)}, f32[128,128]{1,0:T(8,128)S(1)}, u32[]{:S(2)}, u32[]{:S(2)}) collective-permute-start(f32[128,128]{1,0:T(8,128)S(1)} %get-tuple-element.37), channel_id=1, source_target_pairs={{0,32},{32,64},{64,96},{96,0},{1,33},{33,65},{65,97},{97,1},{2,34}... | collective-permute-start | bytes 196616 | tf_op jit(solution)/shard_map/ppermute | solution.py:694
  85.7 5.9 %collective-permute-start.4 = (f32[128,128]{1,0:T(8,128)S(1)}, f32[128,128]{1,0:T(8,128)S(1)}, u32[]{:S(2)}, u32[]{:S(2)}) collective-permute-start(f32[128,128]{1,0:T(8,128)S(1)} %get-tuple-element.38), channel_id=1, source_target_pairs={{0,64},{32,96},{64,0},{96,32},{1,65},{33,97},{65,1},{97,33},{2,66}... | collective-permute-start | bytes 196616 | tf_op jit(solution)/shard_map/ppermute | solution.py:694
  87.6 4.4 %collective-permute-start.5 = (f32[128,128]{1,0:T(8,128)S(1)}, f32[128,128]{1,0:T(8,128)S(1)}, u32[]{:S(2)}, u32[]{:S(2)}) collective-permute-start(f32[128,128]{1,0:T(8,128)S(1)} %get-tuple-element.39), channel_id=1, source_target_pairs={{0,96},{32,0},{64,32},{96,64},{1,97},{33,1},{65,33},{97,65},{2,98}... | collective-permute-start | bytes 196616 | tf_op jit(solution)/shard_map/ppermute | solution.py:694

commit v7 on v6

--- a/solution.py
+++ b/solution.py
@@ -132,9 +132,14 @@
     for f in order:
         source, at = (tracers, f) if f < 4 else (velocity, f - 4)
         target = q if f < 4 else vel
-        span = pl.ds(at * CELLS, CELLS)
+        size = CELLS // 2 if f == 0 else CELLS
+        span = pl.ds(at * CELLS, size)
         copies[f] = pltpu.make_async_copy(source.at[span], target.at[span], sems.at[f])
         copies[f].start()
+        if f == 0:
+            span = pl.ds(size, size)
+            second_half = pltpu.make_async_copy(source.at[span], target.at[span], sems.at[9])
+            second_half.start()
     fetch_depth.wait()
     lane = lax.broadcasted_iota(jnp.int32, (BN, BE), 1)
     level = lane // 2
@@ -147,6 +152,8 @@
         copies[f].wait()
         sides = jnp.zeros((BN, BE), F32)
         for k in range(LEV):
+            if f == 0 and k == LEV // 2:
+                second_half.wait()
             tile = q[pl.ds(f * CELLS + k * BN, BN), :]
             sides = jnp.where(level == k, pltpu.roll(tile, 2 * k + 1, 1), sides)
         own[pl.ds(NORTH_Q[f], LEV), :] = q[pl.ds(f * CELLS + BN - 1, LEV, stride=BN), :]
@@ -189,7 +196,7 @@
             pltpu.VMEM((BE, BE), F32),
             pltpu.VMEM((ITEM, BE), F32),
             pltpu.VMEM((BN, BE), F32),
-            pltpu.SemaphoreType.DMA((9,)),
+            pltpu.SemaphoreType.DMA((10,)),
         ],
         compiler_params=params(12),
         name="pack",

time: 93.5 us -> 93.4 us (level)
  no operation moved by 1% of the time
where the time goes in v7:
time: 93.4 us; the launch traced here: 93.1 us
  starting transfers between devices  36 us (39%)
  Pallas kernels  32.4 us (35%)
  waiting for transfers between devices  24 us (26%)
    all_to_all x3, starting transfers between devices, body(): every = lambda value: lax.all_to_all(value, EVERY, 0, 0)  21.5 us
    all_to_all x3, waiting for transfers between devices, body(): every = lambda value: lax.all_to_all(value, EVERY, 0, 0)  16.4 us
    pallas_call x2, Pallas kernels, stencil(): pl.pallas_call(functools.partial(stencil_kernel, group, chunk), out_shape...  12.2 us
    pallas_call x2, Pallas kernels, solve(): pl.pallas_call(functools.partial(solve_kernel, group, chunk, out_chunk),...  8.58 us
    all_to_all x1, starting transfers between devices, body(): totals = lax.all_to_all(sums, ('c', 'x', 'y', 'z'), 0, 0)  6.23 us
    all_to_all x1, waiting for transfers between devices, body(): totals = lax.all_to_all(sums, ('c', 'x', 'y', 'z'), 0, 0)  4.77 us
    pallas_call x1, Pallas kernels, pack(): pl.pallas_call(pack_kernel, out_shape=pltpu.HBM((ITEM, BE), F32), in_spec...  4.24 us
    ppermute x3, starting transfers between devices, along_z(): return lax.ppermute(value, 'z', [(z, (z + k) % side) for z in range(side)])  4.22 us
  transfers between devices with their start and end apart: 10, of which 6 were waited for; matrix products, arithmetic and copies ran while one was open for 0% of the time, Pallas kernels for 20%

profile of v7, /device:TPU:0, one launch (start us, length us, event | category | flops | bytes accessed | tf_op | source)
XLA Modules:
  0.0 93.1 jit_solution(1656321035382791491)
XLA Ops:
  0.6 0.0 copy-start
  0.6 0.0 copy-start.1
  0.6 4.2 %pack.1.refs_4_ = f32[512,128]{1,0:T(8,128)} custom-call(f32[9216,128]{1,0:T(8,128)} %bitcast.11, f32[4608,128]{1,0:T(8,128)} %bitcast.14, f32[64,128]{1,0:T(8,128)} %bitcast.22), custom_call_target="tpu_custom_call" | custom-call | tf_op jit(solution)/shard_map/pack/pallas_call | solution.py:188
  4.9 11.1 %all-to-all-start = ((f32[128,4,128]{2,1,0:T(4,128)}), f32[128,4,128]{2,1,0:T(4,128)S(1)}, u32[]{:S(2)}, u32[]{:S(2)}) async-start(f32[128,4,128]{2,1,0:T(4,128)} %bitcast.21), calls=%async_computation | async-start | bytes 524288 | tf_op jit(solution)/shard_map/all_to_all | solution.py:695
  16.1 2.2 %plan.1.refs_0_ = s32[146]{0:T(256)S(1)} custom-call(s32[8,16]{1,0:T(8,128)S(1)} %copy-done, s32[8,32]{1,0:T(8,128)S(1)} %copy-done.1), custom_call_target="tpu_custom_call" | custom-call | tf_op jit(solution)/shard_map/plan/pallas_call | solution.py:710
  18.2 8.1 %all-to-all-done.got = f32[128,4,128]{2,1,0:T(4,128)S(1)} async-done(((f32[128,4,128]{2,1,0:T(4,128)}), f32[128,4,128]{2,1,0:T(4,128)S(1)}, u32[]{:S(2)}, u32[]{:S(2)}) %all-to-all-start) | async-done | bytes 262176 | tf_op jit(solution)/shard_map/all_to_all | solution.py:695
  26.3 1.4 %select.1 = f32[128,4,128]{2,1,0:T(4,128)} custom-call(s32[146]{0:T(256)S(1)} %plan.1.refs_0_, f32[128,4,128]{2,1,0:T(4,128)S(1)} %all-to-all-done.got), custom_call_target="tpu_custom_call" | custom-call | tf_op jit(solution)/shard_map/select/pallas_call | solution.py:222
  27.7 4.7 %all-to-all-start.1 = ((f32[128,4,128]{2,1,0:T(4,128)}), f32[128,4,128]{2,1,0:T(4,128)S(1)}, u32[]{:S(2)}, u32[]{:S(2)}) async-start(f32[128,4,128]{2,1,0:T(4,128)} %select.1), calls=%async_computation.1 | async-start | bytes 524288 | tf_op jit(solution)/shard_map/all_to_all | solution.py:695
  32.5 6.1 %stencil0.1 = (f32[4608,128]{1,0:T(8,128)S(1)}, f32[2304,128]{1,0:T(8,128)}) custom-call(f32[9216,128]{1,0:T(8,128)} %bitcast.12, f32[4608,128]{1,0:T(8,128)} %bitcast.15, f32[2240,128]{1,0:T(8,128)} %bitcast.17), custom_call_target="tpu_custom_call" | custom-call | tf_op jit(solution)/shard_map/stencil0/pallas_call | solution.py:352
  38.5 4.2 %all-to-all-done.1 = f32[128,4,128]{2,1,0:T(4,128)S(1)} async-done(((f32[128,4,128]{2,1,0:T(4,128)}), f32[128,4,128]{2,1,0:T(4,128)S(1)}, u32[]{:S(2)}, u32[]{:S(2)}) %all-to-all-start.1) | async-done | bytes 262176 | tf_op jit(solution)/shard_map/all_to_all | solution.py:695
  42.7 4.4 %solve0.1 = (f32[4608,128]{1,0:T(8,128)S(1)}, f32[576,128]{1,0:T(8,128)}, f32[144,128]{1,0:T(8,128)S(1)}, f32[128,4,128]{2,1,0:T(4,128)}) custom-call(s32[146]{0:T(256)S(1)} %plan.1.refs_0_, f32[4608,128]{1,0:T(8,128)S(1)} %get-tuple-element.21.refs_1_, f32[2304,128]{1,0:T(8,128)} %get-tuple-element.22.refs_2_.refs_1_, ...), custom_call_target="tpu_custom_call", output_to_operand_aliasing={{0}: (1, {})} | custom-call | tf_op jit(solution)/shard_map/solve0/pallas_call | solution.py:521
  47.2 5.6 %all-to-all-start.2 = ((f32[128,4,128]{2,1,0:T(4,128)}), f32[128,4,128]{2,1,0:T(4,128)S(1)}, u32[]{:S(2)}, u32[]{:S(2)}) async-start(f32[128,4,128]{2,1,0:T(4,128)} %get-tuple-element.24), calls=%async_computation.2 | async-start | bytes 524288 | tf_op jit(solution)/shard_map/all_to_all | solution.py:695
  52.8 6.1 %stencil1.1 = (f32[4608,128]{1,0:T(8,128)S(1)}, f32[9216,128]{1,0:T(8,128)}) custom-call(f32[9216,128]{1,0:T(8,128)} %bitcast.13, f32[4608,128]{1,0:T(8,128)} %bitcast.16, f32[4608,128]{1,0:T(8,128)S(1)} %get-tuple-element.25.refs_2_), custom_call_target="tpu_custom_call", output_to_operand_aliasing={{0}: (2, {})} | custom-call | tf_op jit(solution)/shard_map/stencil1/pallas_call | solution.py:352
  58.9 4.1 %all-to-all-done.2.got = f32[128,4,128]{2,1,0:T(4,128)S(1)} async-done(((f32[128,4,128]{2,1,0:T(4,128)}), f32[128,4,128]{2,1,0:T(4,128)S(1)}, u32[]{:S(2)}, u32[]{:S(2)}) %all-to-all-start.2) | async-done | bytes 262176 | tf_op jit(solution)/shard_map/all_to_all | solution.py:695
  63.0 1.8 %krylov.1 = (f32[192,128]{1,0:T(8,128)S(1)}, f32[128,1,128]{2,1,0:T(1,128)}) custom-call(s32[146]{0:T(256)S(1)} %plan.1.refs_0_, f32[144,128]{1,0:T(8,128)S(1)} %get-tuple-element.23.base, f32[128,4,128]{2,1,0:T(4,128)S(1)} %all-to-all-done.2.got), custom_call_target="tpu_custom_call" | custom-call | tf_op jit(solution)/shard_map/krylov/pallas_call | solution.py:607
  64.8 0.7 collective-permute-start
  65.5 2.3 %collective-permute-start.1 = (f32[192,128]{1,0:T(8,128)S(1)}, f32[192,128]{1,0:T(8,128)S(1)}, u32[]{:S(2)}, u32[]{:S(2)}) collective-permute-start(f32[192,128]{1,0:T(8,128)S(1)} %get-tuple-element.35.a0), channel_id=1, source_target_pairs={{0,16},{8,24},{16,0},{24,8},{1,17},{9,25},{17,1},{25,9},{2,18},{10... | collective-permute-start | bytes 294920 | tf_op jit(solution)/shard_map/ppermute | solution.py:698
  67.8 1.1 %collective-permute-start.2 = (f32[192,128]{1,0:T(8,128)S(1)}, f32[192,128]{1,0:T(8,128)S(1)}, u32[]{:S(2)}, u32[]{:S(2)}) collective-permute-start(f32[192,128]{1,0:T(8,128)S(1)} %get-tuple-element.35.a0), channel_id=1, source_target_pairs={{0,24},{8,0},{16,8},{24,16},{1,25},{9,1},{17,9},{25,17},{2,26},{10... | collective-permute-start | bytes 294920 | tf_op jit(solution)/shard_map/ppermute | solution.py:698
  68.8 6.2 %all-to-all-start.3 = ((f32[128,1,128]{2,1,0:T(1,128)}), f32[128,1,128]{2,1,0:T(1,128)S(1)}, u32[]{:S(2)}, u32[]{:S(2)}) async-start(f32[128,1,128]{2,1,0:T(1,128)} %get-tuple-element.28), calls=%async_computation.3 | async-start | bytes 131072 | tf_op jit(solution)/shard_map/all_to_all | solution.py:729
  75.1 4.1 %solve1.1 = (f32[4608,128]{1,0:T(8,128)S(1)}, f32[9216,128]{1,0:T(8,128)}) custom-call(f32[4608,128]{1,0:T(8,128)S(1)} %get-tuple-element.29.refs_0_, f32[2304,128]{1,0:T(8,128)} %get-tuple-element.22.refs_2_.refs_1_, f32[2240,128]{1,0:T(8,128)} %bitcast.19, f32[576,128]{1,0:T(8,128)} %get-tuple-element.30.refs_3_, ...), custom_call_target="tpu_custom_call", output_to_operand_aliasing={{0}: (0, {}), {1}: (4, {})} | custom-call | tf_op jit(solution)/shard_map/solve1/pallas_call | solution.py:521
  79.2 4.8 %all-to-all-done.3 = f32[128,1,128]{2,1,0:T(1,128)S(1)} async-done(((f32[128,1,128]{2,1,0:T(1,128)}), f32[128,1,128]{2,1,0:T(1,128)S(1)}, u32[]{:S(2)}, u32[]{:S(2)}) %all-to-all-start.3) | async-done | bytes 65568 | tf_op jit(solution)/shard_map/all_to_all | solution.py:729
  84.0 0.0 collective-permute-done.a1
  84.0 0.0 collective-permute-done.1.a2
  84.0 0.0 collective-permute-done.2.a3
  84.0 0.8 combine.1
  84.8 0.9 collective-permute-start.3
  85.7 1.8 %collective-permute-start.4 = (f32[128,128]{1,0:T(8,128)S(1)}, f32[128,128]{1,0:T(8,128)S(1)}, u32[]{:S(2)}, u32[]{:S(2)}) collective-permute-start(f32[128,128]{1,0:T(8,128)S(1)} %get-tuple-element.38), channel_id=1, source_target_pairs={{0,64},{32,96},{64,0},{96,32},{1,65},{33,97},{65,1},{97,33},{2,66}... | collective-permute-start | bytes 196616 | tf_op jit(solution)/shard_map/ppermute | solution.py:701
  87.6 1.5 %collective-permute-start.5 = (f32[128,128]{1,0:T(8,128)S(1)}, f32[128,128]{1,0:T(8,128)S(1)}, u32[]{:S(2)}, u32[]{:S(2)}) collective-permute-start(f32[128,128]{1,0:T(8,128)S(1)} %get-tuple-element.39), channel_id=1, source_target_pairs={{0,96},{32,0},{64,32},{96,64},{1,97},{33,1},{65,33},{97,65},{2,98}... | collective-permute-start | bytes 196616 | tf_op jit(solution)/shard_map/ppermute | solution.py:701
  89.0 2.6 %collective-permute-done.3.a1 = f32[128,128]{1,0:T(8,128)S(1)} collective-permute-done((f32[128,128]{1,0:T(8,128)S(1)}, f32[128,128]{1,0:T(8,128)S(1)}, u32[]{:S(2)}, u32[]{:S(2)}) %collective-permute-start.3) | collective-permute-done | bytes 65568 | tf_op jit(solution)/shard_map/ppermute | solution.py:701
  91.6 0.0 collective-permute-done.4.a2
  91.6 0.3 collective-permute-done.5.a3
  91.9 1.2 %place.1 = f32[2,64,128]{2,1,0:T(8,128)} custom-call(s32[146]{0:T(256)S(1)} %plan.1.refs_0_, f32[128,128]{1,0:T(8,128)S(1)} %get-tuple-element.36.a0, f32[128,128]{1,0:T(8,128)S(1)} %collective-permute-done.3.a1, f32[128,128]{1,0:T(8,128)S(1)} %collective-permute-done.4.a2, f32[128,128]{1,0:T(8,128)S(1)} %collective-permute-done.5.a3), custom_call_target="tpu_custom_call" | custom-call | tf_op jit(solution)/shard_map/place/pallas_call | solution.py:682
  (2 shorter events, 0.0 us)
Async XLA Ops:
  0.6 15.4 %copy-start = (s32[8,16]{1,0:T(8,128)S(1)}, s32[8,16]{1,0:T(8,128)}, u32[]{:S(2)}) copy-start(s32[8,16]{1,0:T(8,128)} %clinic.1) | copy-start | bytes 1540
  0.6 15.4 %copy-start.1 = (s32[8,32]{1,0:T(8,128)S(1)}, s32[8,32]{1,0:T(8,128)}, u32[]{:S(2)}) copy-start(s32[8,32]{1,0:T(8,128)} %tropic.1) | copy-start | bytes 3076
  4.9 21.4 %all-to-all-start = ((f32[128,4,128]{2,1,0:T(4,128)}), f32[128,4,128]{2,1,0:T(4,128)S(1)}, u32[]{:S(2)}, u32[]{:S(2)}) async-start(f32[128,4,128]{2,1,0:T(4,128)} %bitcast.21), calls=%async_computation | async-start | bytes 524288 | tf_op jit(solution)/shard_map/all_to_all | solution.py:695
  27.7 15.0 %all-to-all-start.1 = ((f32[128,4,128]{2,1,0:T(4,128)}), f32[128,4,128]{2,1,0:T(4,128)S(1)}, u32[]{:S(2)}, u32[]{:S(2)}) async-start(f32[128,4,128]{2,1,0:T(4,128)} %select.1), calls=%async_computation.1 | async-start | bytes 524288 | tf_op jit(solution)/shard_map/all_to_all | solution.py:695
  47.2 15.8 %all-to-all-start.2 = ((f32[128,4,128]{2,1,0:T(4,128)}), f32[128,4,128]{2,1,0:T(4,128)S(1)}, u32[]{:S(2)}, u32[]{:S(2)}) async-start(f32[128,4,128]{2,1,0:T(4,128)} %get-tuple-element.24), calls=%async_computation.2 | async-start | bytes 524288 | tf_op jit(solution)/shard_map/all_to_all | solution.py:695
  64.8 19.2 %collective-permute-start = (f32[192,128]{1,0:T(8,128)S(1)}, f32[192,128]{1,0:T(8,128)S(1)}, u32[]{:S(2)}, u32[]{:S(2)}) collective-permute-start(f32[192,128]{1,0:T(8,128)S(1)} %get-tuple-element.35.a0), channel_id=1, source_target_pairs={{0,8},{8,16},{16,24},{24,0},{1,9},{9,17},{17,25},{25,1},{2,10},{10... | collective-permute-start | bytes 294920 | tf_op jit(solution)/shard_map/ppermute | solution.py:698
  65.5 18.5 %collective-permute-start.1 = (f32[192,128]{1,0:T(8,128)S(1)}, f32[192,128]{1,0:T(8,128)S(1)}, u32[]{:S(2)}, u32[]{:S(2)}) collective-permute-start(f32[192,128]{1,0:T(8,128)S(1)} %get-tuple-element.35.a0), channel_id=1, source_target_pairs={{0,16},{8,24},{16,0},{24,8},{1,17},{9,25},{17,1},{25,9},{2,18},{10... | collective-permute-start | bytes 294920 | tf_op jit(solution)/shard_map/ppermute | solution.py:698
  67.8 16.2 %collective-permute-start.2 = (f32[192,128]{1,0:T(8,128)S(1)}, f32[192,128]{1,0:T(8,128)S(1)}, u32[]{:S(2)}, u32[]{:S(2)}) collective-permute-start(f32[192,128]{1,0:T(8,128)S(1)} %get-tuple-element.35.a0), channel_id=1, source_target_pairs={{0,24},{8,0},{16,8},{24,16},{1,25},{9,1},{17,9},{25,17},{2,26},{10... | collective-permute-start | bytes 294920 | tf_op jit(solution)/shard_map/ppermute | solution.py:698
  68.8 15.2 %all-to-all-start.3 = ((f32[128,1,128]{2,1,0:T(1,128)}), f32[128,1,128]{2,1,0:T(1,128)S(1)}, u32[]{:S(2)}, u32[]{:S(2)}) async-start(f32[128,1,128]{2,1,0:T(1,128)} %get-tuple-element.28), calls=%async_computation.3 | async-start | bytes 131072 | tf_op jit(solution)/shard_map/all_to_all | solution.py:729
  84.8 6.8 %collective-permute-start.3 = (f32[128,128]{1,0:T(8,128)S(1)}, f32[128,128]{1,0:T(8,128)S(1)}, u32[]{:S(2)}, u32[]{:S(2)}) collective-permute-start(f32[128,128]{1,0:T(8,128)S(1)} %get-tuple-element.37), channel_id=1, source_target_pairs={{0,32},{32,64},{64,96},{96,0},{1,33},{33,65},{65,97},{97,1},{2,34}... | collective-permute-start | bytes 196616 | tf_op jit(solution)/shard_map/ppermute | solution.py:701
  85.7 5.9 %collective-permute-start.4 = (f32[128,128]{1,0:T(8,128)S(1)}, f32[128,128]{1,0:T(8,128)S(1)}, u32[]{:S(2)}, u32[]{:S(2)}) collective-permute-start(f32[128,128]{1,0:T(8,128)S(1)} %get-tuple-element.38), channel_id=1, source_target_pairs={{0,64},{32,96},{64,0},{96,32},{1,65},{33,97},{65,1},{97,33},{2,66}... | collective-permute-start | bytes 196616 | tf_op jit(solution)/shard_map/ppermute | solution.py:701
  87.6 4.4 %collective-permute-start.5 = (f32[128,128]{1,0:T(8,128)S(1)}, f32[128,128]{1,0:T(8,128)S(1)}, u32[]{:S(2)}, u32[]{:S(2)}) collective-permute-start(f32[128,128]{1,0:T(8,128)S(1)} %get-tuple-element.39), channel_id=1, source_target_pairs={{0,96},{32,0},{64,32},{96,64},{1,97},{33,1},{65,33},{97,65},{2,98}... | collective-permute-start | bytes 196616 | tf_op jit(solution)/shard_map/ppermute | solution.py:701
